TPU v7x, 128 devices: a whole 4x4x4 slice. The times are simulated.
128 devices in a mesh: ctx: 8 (over y_lo, x), head: 16 (over z, y_hi, core).
Axes of the slice: x: 4, y: 4 (y_hi: 2, y_lo: 2; y = y_hi * 2 + y_lo), z: 4, core: 2. Of those that a mesh axis runs over, the one named last changes fastest.
Arguments:
- passage_q: bfloat16 [8192, 16384], P(('ctx', 'head')), may hold values from -12 to 12
- passage_k: bfloat16 [8192, 1024], P(('ctx', 'head')), may hold values from -12 to 12
- passage_v: bfloat16 [8192, 1024], P(('ctx', 'head')), may hold values from -6 to 6
- new_q: bfloat16 [2048, 16384], P(('ctx', 'head')), may hold values from -12 to 12
- new_k: bfloat16 [2048, 1024], P(('ctx', 'head')), may hold values from -12 to 12
- new_v: bfloat16 [2048, 1024], P(('ctx', 'head')), may hold values from -6 to 6
- segments: int32 [8192], replicated, may hold values from 0 to 31, never falling along the last dimension, each value on 1 to 512 neighbouring positions
Outputs:
- passage_out: bfloat16 [8192, 16384], P(('ctx', 'head'))
- new_out: bfloat16 [2048, 16384], P(('ctx', 'head'))
Inputs may be any that keep to these rules, and one draw needn't show every extreme that they name: `segments`: passages are runs of equal numbers, rising by one from run to run, each of 1 to 512 tokens; some passage has exactly 512.
All inputs are finite; a program needn't handle non-finite values.
Results may differ from a plain program's by a relative error of at most 0.008.
Values may be sent and summed in bfloat16 or wider, within the bound.
No kernel may reach another device: no remote copies, remote signals or barrier semaphores. Data moves between devices by JAX's collectives and lax.ppermute only.
A program may use at most 128 MiB of HBM per device.

v0:
```python
import jax
import jax.numpy as jnp
from jax import lax
from jax.sharding import PartitionSpec as P

QH = 128
KVH = 8
HD = 128
MOST = 512


big_neg = -1e30


def shifted(block, axis, distance):
    devices = range(lax.axis_size(axis))
    route = [(i - distance, i) for i in devices if i - distance in devices]
    return lax.ppermute(block, axis, route)


def attend(q_block, k_block, v_block, visible):
    scores = jnp.einsum(
        "qhd,kd->qhk", q_block, k_block, preferred_element_type=jnp.float32
    ) * HD ** (-0.5)
    if visible is None:
        row_max = jnp.max(scores, axis=-1)
        weights = jnp.exp(scores - row_max[..., None])
    else:
        masked = jnp.where(visible[:, None, :], scores, big_neg)
        row_max = jnp.max(masked, axis=-1)
        weights = jnp.where(visible[:, None, :], jnp.exp(masked - row_max[..., None]), 0.0)
    row_sum = jnp.sum(weights, axis=-1)
    weighted = jnp.einsum(
        "qhk,kd->qhd", weights.astype(jnp.bfloat16), v_block, preferred_element_type=jnp.float32
    )
    return (weighted, row_max, row_sum)


def combine_parts(first_part, second_part):
    top_max = jnp.maximum(first_part[1], second_part[1])
    first_w = jnp.exp(first_part[1] - top_max)
    second_w = jnp.exp(second_part[1] - top_max)
    weighted = first_part[0] * first_w[..., None] + second_part[0] * second_w[..., None]
    return (weighted, top_max, first_part[2] * first_w + second_part[2] * second_w)


def local_passages(passage_q, passage_k, passage_v, segments, head_count):
    flat_index = lax.axis_index("ctx") * head_count + lax.axis_index("head")
    row_count = passage_k.shape[0]
    group_size = QH // KVH
    hops = max(1, (MOST - 1 + row_count - 1) // row_count)
    window = hops * row_count
    empty = jnp.zeros((window, KVH * HD), jnp.bfloat16)

    def hop(step, carry):
        moving_k, moving_v, buffer_k, buffer_v = carry
        moving_k, moving_v = shifted((moving_k, moving_v), ("ctx", "head"), 1)
        place = ((hops - 1 - step) * row_count).astype(jnp.int32)
        buffer_k = lax.dynamic_update_slice_in_dim(buffer_k, moving_k, place, 0)
        buffer_v = lax.dynamic_update_slice_in_dim(buffer_v, moving_v, place, 0)
        return (moving_k, moving_v, buffer_k, buffer_v)

    carried = lax.fori_loop(0, hops, hop, (passage_k, passage_v, empty, empty))
    keys_ext = jnp.concatenate([carried[2], passage_k], axis=0).reshape(window + row_count, KVH, HD)
    vals_ext = jnp.concatenate([carried[3], passage_v], axis=0).reshape(window + row_count, KVH, HD)
    seg_padded = jnp.concatenate([jnp.full((window,), -1, jnp.int32), segments])
    seg_key = lax.dynamic_slice_in_dim(seg_padded, flat_index * row_count, window + row_count, 0)
    seg_query = seg_key[window:]
    causal = jnp.arange(window + row_count)[None, :] - window <= jnp.arange(row_count)[:, None]
    visible = causal & (seg_query[:, None] == seg_key[None, :])
    q_heads = jnp.transpose(passage_q.reshape(row_count, KVH, group_size, HD), (1, 0, 2, 3))
    k_heads = jnp.transpose(keys_ext, (1, 0, 2))
    v_heads = jnp.transpose(vals_ext, (1, 0, 2))

    def per_head(inputs):
        q_head, k_head, v_head = inputs
        weighted, row_max, row_sum = attend(q_head, k_head, v_head, visible)
        return (weighted / row_sum[..., None]).astype(jnp.bfloat16)

    outputs = lax.map(per_head, (q_heads, k_heads, v_heads))
    return jnp.transpose(outputs, (1, 0, 2, 3)).reshape(row_count, QH * HD)


def on_device(passage_q, passage_k, passage_v, new_q, new_k, new_v, segments):
    head_count = lax.axis_size("head")
    ctx_count = lax.axis_size("ctx")
    ctx_index = lax.axis_index("ctx")
    heads_local = QH // head_count
    copy_count = head_count // KVH

    def spread(kv_rows):
        row_count = kv_rows.shape[0]
        return jnp.repeat(kv_rows.reshape(row_count, KVH, HD), copy_count, axis=1).reshape(
            row_count, head_count * HD
        )

    fresh_q, fresh_k, fresh_v, pass_k, pass_v = (
        lax.all_to_all(new_q, "head", split_axis=1, concat_axis=0, tiled=True),
        lax.all_to_all(spread(new_k), "head", split_axis=1, concat_axis=0, tiled=True),
        lax.all_to_all(spread(new_v), "head", split_axis=1, concat_axis=0, tiled=True),
        lax.all_to_all(spread(passage_k), "head", split_axis=1, concat_axis=0, tiled=True),
        lax.all_to_all(spread(passage_v), "head", split_axis=1, concat_axis=0, tiled=True),
    )
    pass_out = local_passages(passage_q, passage_k, passage_v, segments, head_count)
    new_local = fresh_q.shape[0]
    all_queries = lax.all_gather(fresh_q, "ctx", axis=0, tiled=True)
    total_new = all_queries.shape[0]
    query_rows = min(512, total_new)
    query_groups = all_queries.reshape(total_new // query_rows, query_rows, heads_local, HD)
    key_pos = ctx_index * new_local + jnp.arange(new_local, dtype=jnp.int32)

    def partial_block(inputs):
        q_block, block_id = inputs
        passage_part = attend(q_block, pass_k, pass_v, None)
        query_pos = block_id * query_rows + jnp.arange(query_rows, dtype=jnp.int32)
        visible = key_pos[None, :] <= query_pos[:, None]
        return combine_parts(passage_part, attend(q_block, fresh_k, fresh_v, visible))

    weighted, row_max, row_sum = lax.map(
        partial_block, (query_groups, jnp.arange(total_new // query_rows, dtype=jnp.int32))
    )
    weighted = weighted.reshape(1, total_new, heads_local * HD)
    row_max = row_max.reshape(1, total_new, heads_local)
    row_sum = row_sum.reshape(1, total_new, heads_local)
    parts_w, parts_max, parts_sum = (
        lax.all_to_all(weighted, "ctx", split_axis=1, concat_axis=0, tiled=True),
        lax.all_to_all(row_max, "ctx", split_axis=1, concat_axis=0, tiled=True),
        lax.all_to_all(row_sum, "ctx", split_axis=1, concat_axis=0, tiled=True),
    )
    top_max = jnp.max(parts_max, axis=0)
    factors = jnp.exp(parts_max - top_max[None])
    numer_sum = jnp.sum(
        parts_w.reshape(ctx_count, new_local, heads_local, HD) * factors[..., None], axis=0
    )
    denom_sum = jnp.sum(parts_sum * factors, axis=0)
    fresh_out = (
        (numer_sum / denom_sum[..., None]).astype(jnp.bfloat16).reshape(new_local, heads_local * HD)
    )
    fresh_rows_out = lax.all_to_all(fresh_out, "head", split_axis=0, concat_axis=1, tiled=True)
    return (pass_out, fresh_rows_out)


def solution(mesh):
    in_specs = (
        P(("ctx", "head"), None),
        P(("ctx", "head"), None),
        P(("ctx", "head"), None),
        P(("ctx", "head"), None),
        P(("ctx", "head"), None),
        P(("ctx", "head"), None),
        P(),
    )
    out_specs = (P(("ctx", "head"), None), P(("ctx", "head"), None))
    return jax.shard_map(
        on_device, mesh=mesh, in_specs=in_specs, out_specs=out_specs, check_vma=False
    )
```

profile of v0, /device:TPU:31, one launch (start us, length us, event | category | flops | bytes accessed | tf_op | source)
XLA Modules:
  0.0 535.6 jit_solution(4962880424613716463)
XLA Ops:
  8.4 18.2 %all_to_all.147 = bf16[16,16,1024]{2,0,1:T(8,128)(2,1)} all-to-all(bf16[16,16,1024]{2,0,1:T(8,128)(2,1)S(1)} %bitcast.235), channel_id=1, replica_groups=mesh['ctx'=8,'head'=16] {'head'}, dimensions={1} | all-to-all | bytes 1048576 | tf_op jit(solution)/shard_map/all_to_all | solution.py:98
  27.3 6.1 %all-to-all-start.3 = ((bf16[16,16,128]{2,0,1:T(8,128)(2,1)}), bf16[16,16,128]{2,0,1:T(8,128)(2,1)S(1)}, u32[]{:S(2)}, u32[]{:S(2)}) async-start(bf16[16,16,128]{2,0,1:T(8,128)(2,1)} %bitcast.12), calls=%async_computation.3 | async-start | bytes 131072 | tf_op jit(solution)/shard_map/all_to_all | solution.py:99
  33.4 40.5 %all-to-all-done.3 = bf16[16,16,128]{2,0,1:T(8,128)(2,1)S(1)} async-done(((bf16[16,16,128]{2,0,1:T(8,128)(2,1)}), bf16[16,16,128]{2,0,1:T(8,128)(2,1)S(1)}, u32[]{:S(2)}, u32[]{:S(2)}) %all-to-all-start.3) | async-done | bytes 65568 | tf_op jit(solution)/shard_map/all_to_all | solution.py:99
  74.5 9.7 %all-to-all-start.4 = ((bf16[16,16,128]{2,0,1:T(8,128)(2,1)}), bf16[16,16,128]{2,0,1:T(8,128)(2,1)S(1)}, u32[]{:S(2)}, u32[]{:S(2)}) async-start(bf16[16,16,128]{2,0,1:T(8,128)(2,1)} %bitcast.15), calls=%async_computation.4 | async-start | bytes 131072 | tf_op jit(solution)/shard_map/all_to_all | solution.py:100
  84.3 4.9 all-to-all-done.4
  89.9 6.3 %all-to-all-start.1 = ((bf16[64,16,128]{2,0,1:T(8,128)(2,1)}), bf16[64,16,128]{2,0,1:T(8,128)(2,1)S(1)}, u32[]{:S(2)}, u32[]{:S(2)}) async-start(bf16[64,16,128]{2,0,1:T(8,128)(2,1)} %bitcast.6), calls=%async_computation.1 | async-start | bytes 524288 | tf_op jit(solution)/shard_map/all_to_all | solution.py:101
  96.2 6.8 %all-to-all-done.1 = bf16[64,16,128]{2,0,1:T(8,128)(2,1)S(1)} async-done(((bf16[64,16,128]{2,0,1:T(8,128)(2,1)}), bf16[64,16,128]{2,0,1:T(8,128)(2,1)S(1)}, u32[]{:S(2)}, u32[]{:S(2)}) %all-to-all-start.1) | async-done | bytes 262176 | tf_op jit(solution)/shard_map/all_to_all | solution.py:101
  103.7 6.3 %all-to-all-start.2 = ((bf16[64,16,128]{2,0,1:T(8,128)(2,1)}), bf16[64,16,128]{2,0,1:T(8,128)(2,1)S(1)}, u32[]{:S(2)}, u32[]{:S(2)}) async-start(bf16[64,16,128]{2,0,1:T(8,128)(2,1)} %bitcast.9), calls=%async_computation.2 | async-start | bytes 524288 | tf_op jit(solution)/shard_map/all_to_all | solution.py:102
  110.0 5.2 copy.99
  116.8 77.5 %while.47 = (s32[]{:T(128)}, f32[4,512,8,128]{3,2,1,0:T(8,128)}, f32[4,512,8]{1,2,0:T(8,128)S(1)}, f32[4,512,8]{1,2,0:T(8,128)S(1)}, bf16[4,512,8,128]{3,2,1,0:T...) while((s32[]{:T(128)}, f32[4,512,8,128]{3,2,1,0:T(8,128)}, ...), condition=%wide.region_11.12_spmd.clone, body=%wide.region_6.11_spmd.clone.sunk | while | flops 2733265664 | bytes 79108272 | solution.py:119
  125.5 3.5 fusion.145
  129.1 4.5 add_bitcast_fusion.2
  144.9 3.5 fusion.145
  148.5 4.5 add_bitcast_fusion.2
  164.2 3.5 fusion.145
  167.8 4.5 add_bitcast_fusion.2
  183.6 3.5 fusion.145
  187.2 4.5 add_bitcast_fusion.2
  195.3 9.5 %reduce.1 = f32[2048,8]{1,0:T(8,128)S(1)} reduce(f32[2048,1,8]{2,1,0:T(1,128)S(1)} %bitcast.225, f32[]{:T(128)} %broadcast.94), dimensions={1}, to_apply=%bitcast.154.reduce_sub_computation | reduce | bytes 131076
  206.0 4.8 all-to-all-start.7
  211.4 9.3 %reduce.3 = f32[2048,8]{1,0:T(8,128)S(1)} reduce(f32[2048,1,8]{2,1,0:T(1,128)S(1)} %bitcast.226, f32[]{:T(128)} %broadcast.94), dimensions={1}, to_apply=%bitcast.152.reduce_sub_computation | reduce | bytes 131076
  221.2 7.9 %all_to_all.148 = f32[8,1,2048]{2,1,0:T(1,128)S(1)} all-to-all(f32[8,1,2048]{2,1,0:T(1,128)S(1)} %reshape.231), channel_id=1, replica_groups=mesh['ctx'=8,'head'=16] {'ctx'}, dimensions={0} | all-to-all | bytes 131072 | tf_op jit(solution)/shard_map/all_to_all | solution.py:127
  229.1 7.2 %all-to-all-start.5 = ((f32[1,2048,1024]{2,0,1:T(1,128)}), f32[1,2048,1024]{2,0,1:T(1,128)}, u32[]{:S(2)}, u32[]{:S(2)}) async-start(f32[1,2048,1024]{2,0,1:T(1,128)} %bitcast.220), calls=%async_computation.5 | async-start | bytes 16777216 | tf_op jit(solution)/shard_map/all_to_all | solution.py:126
  237.3 188.0 %while.45 = (s32[]{:T(128)}, bf16[64,1024]{1,0:T(8,128)(2,1)S(1)}, bf16[64,1024]{1,0:T(8,128)(2,1)S(1)}, bf16[512,1024]{1,0:T(8,128)(2,1)S(1)}, bf16[512,1024]{1...) while((s32[]{:T(128)}, bf16[64,1024]{1,0:T(8,128)(2,1)S(1)}, ...), condition=%wide.region_1.0_spmd, body=%wide.region_0.0_spmd.sunk | while | flops 7 | bytes 2097399 | solution.py:63
  237.3 5.8 %collective-permute-start.1 = (bf16[64,1024]{1,0:T(8,128)(2,1)S(1)}, bf16[64,1024]{1,0:T(8,128)(2,1)S(1)}, u32[]{:S(2)}, u32[]{:S(2)}) collective-permute-start(bf16[64,1024]{1,0:T(8,128)(2,1)S(1)} %get-tuple-element.553), channel_id=1, source_target_pairs={{0,1},{1,2},{2,3},{3,4},{4,5},{5,6},{6,7},{7,8},{8,9},{9,10},{10,1... | collective-permute-start | bytes 393224 | tf_op jit(solution)/shard_map/while/body/eval_jaxpr/ppermute | solution.py:18
  245.1 38.3 %collective-permute-done.1 = bf16[64,1024]{1,0:T(8,128)(2,1)S(1)} collective-permute-done((bf16[64,1024]{1,0:T(8,128)(2,1)S(1)}, bf16[64,1024]{1,0:T(8,128)(2,1)S(1)}, u32[]{:S(2)}, u32[]{:S(2)}) %collective-permute-start.1) | collective-permute-done | bytes 131104 | tf_op jit(solution)/shard_map/while/body/eval_jaxpr/ppermute | solution.py:18
  284.9 6.8 %collective-permute-start.1 = (bf16[64,1024]{1,0:T(8,128)(2,1)S(1)}, bf16[64,1024]{1,0:T(8,128)(2,1)S(1)}, u32[]{:S(2)}, u32[]{:S(2)}) collective-permute-start(bf16[64,1024]{1,0:T(8,128)(2,1)S(1)} %get-tuple-element.553), channel_id=1, source_target_pairs={{0,1},{1,2},{2,3},{3,4},{4,5},{5,6},{6,7},{7,8},{8,9},{9,10},{10,1... | collective-permute-start | bytes 393224 | tf_op jit(solution)/shard_map/while/body/eval_jaxpr/ppermute | solution.py:18
  293.6 41.1 %collective-permute-done.1 = bf16[64,1024]{1,0:T(8,128)(2,1)S(1)} collective-permute-done((bf16[64,1024]{1,0:T(8,128)(2,1)S(1)}, bf16[64,1024]{1,0:T(8,128)(2,1)S(1)}, u32[]{:S(2)}, u32[]{:S(2)}) %collective-permute-start.1) | collective-permute-done | bytes 131104 | tf_op jit(solution)/shard_map/while/body/eval_jaxpr/ppermute | solution.py:18
  334.7 2.8 collective-permute-done
  337.6 6.9 %collective-permute-start.1 = (bf16[64,1024]{1,0:T(8,128)(2,1)S(1)}, bf16[64,1024]{1,0:T(8,128)(2,1)S(1)}, u32[]{:S(2)}, u32[]{:S(2)}) collective-permute-start(bf16[64,1024]{1,0:T(8,128)(2,1)S(1)} %get-tuple-element.553), channel_id=1, source_target_pairs={{0,1},{1,2},{2,3},{3,4},{4,5},{5,6},{6,7},{7,8},{8,9},{9,10},{10,1... | collective-permute-start | bytes 393224 | tf_op jit(solution)/shard_map/while/body/eval_jaxpr/ppermute | solution.py:18
  348.5 6.8 %collective-permute-start.1 = (bf16[64,1024]{1,0:T(8,128)(2,1)S(1)}, bf16[64,1024]{1,0:T(8,128)(2,1)S(1)}, u32[]{:S(2)}, u32[]{:S(2)}) collective-permute-start(bf16[64,1024]{1,0:T(8,128)(2,1)S(1)} %get-tuple-element.553), channel_id=1, source_target_pairs={{0,1},{1,2},{2,3},{3,4},{4,5},{5,6},{6,7},{7,8},{8,9},{9,10},{10,1... | collective-permute-start | bytes 393224 | tf_op jit(solution)/shard_map/while/body/eval_jaxpr/ppermute | solution.py:18
  357.2 14.9 %collective-permute-done.1 = bf16[64,1024]{1,0:T(8,128)(2,1)S(1)} collective-permute-done((bf16[64,1024]{1,0:T(8,128)(2,1)S(1)}, bf16[64,1024]{1,0:T(8,128)(2,1)S(1)}, u32[]{:S(2)}, u32[]{:S(2)}) %collective-permute-start.1) | collective-permute-done | bytes 131104 | tf_op jit(solution)/shard_map/while/body/eval_jaxpr/ppermute | solution.py:18
  378.0 6.9 %collective-permute-done.1 = bf16[64,1024]{1,0:T(8,128)(2,1)S(1)} collective-permute-done((bf16[64,1024]{1,0:T(8,128)(2,1)S(1)}, bf16[64,1024]{1,0:T(8,128)(2,1)S(1)}, u32[]{:S(2)}, u32[]{:S(2)}) %collective-permute-start.1) | collective-permute-done | bytes 131104 | tf_op jit(solution)/shard_map/while/body/eval_jaxpr/ppermute | solution.py:18
  390.8 6.9 %collective-permute-done.1 = bf16[64,1024]{1,0:T(8,128)(2,1)S(1)} collective-permute-done((bf16[64,1024]{1,0:T(8,128)(2,1)S(1)}, bf16[64,1024]{1,0:T(8,128)(2,1)S(1)}, u32[]{:S(2)}, u32[]{:S(2)}) %collective-permute-start.1) | collective-permute-done | bytes 131104 | tf_op jit(solution)/shard_map/while/body/eval_jaxpr/ppermute | solution.py:18
  403.6 6.9 %collective-permute-done.1 = bf16[64,1024]{1,0:T(8,128)(2,1)S(1)} collective-permute-done((bf16[64,1024]{1,0:T(8,128)(2,1)S(1)}, bf16[64,1024]{1,0:T(8,128)(2,1)S(1)}, u32[]{:S(2)}, u32[]{:S(2)}) %collective-permute-start.1) | collective-permute-done | bytes 131104 | tf_op jit(solution)/shard_map/while/body/eval_jaxpr/ppermute | solution.py:18
  416.4 6.9 %collective-permute-done.1 = bf16[64,1024]{1,0:T(8,128)(2,1)S(1)} collective-permute-done((bf16[64,1024]{1,0:T(8,128)(2,1)S(1)}, bf16[64,1024]{1,0:T(8,128)(2,1)S(1)}, u32[]{:S(2)}, u32[]{:S(2)}) %collective-permute-start.1) | collective-permute-done | bytes 131104 | tf_op jit(solution)/shard_map/while/body/eval_jaxpr/ppermute | solution.py:18
  437.7 4.6 mul.96
  442.3 13.6 %multiply_reduce_fusion.1 = f32[256,1024]{1,0:T(8,128)S(1)} fusion(f32[1,8,256,1024]{3,0,2,1:T(1,128)} %bitcast.19, f32[1,8,256,1024]{3,0,2,1:T(1,128)} %bitcast.214), kind=kLoop, calls=%fused_computation.89 | loop fusion | flops 3932160 | bytes 17825792 | tf_op jit(solution)/shard_map/reduce_sum | solution.py:132
  456.9 25.2 %all-to-all-start.8 = ((bf16[16,16,1024]{2,1,0:T(8,128)(2,1)}), bf16[16,16,1024]{2,1,0:T(8,128)(2,1)S(1)}, u32[]{:S(2)}, u32[]{:S(2)}) async-start(bf16[16,16,1024]{2,1,0:T(8,128)(2,1)} %divide_convert_fusion), calls=%async_computation.8 | async-start | bytes 1048576 | tf_op jit(solution)/shard_map/all_to_all | solution.py:139
  482.1 42.4 %while.46 = (s32[]{:T(128)}, bf16[8,64,16,128]{3,2,1,0:T(8,128)(2,1)S(1)}, bf16[8,64,16,128]{3,2,0,1:T(8,128)(2,1)}, bf16[8,576,128]{2,1,0:T(8,128)(2,1)}, bf16[...) while((s32[]{:T(128)}, ...), condition=%wide.region_5.6_spmd.clone, body=%wide.region_2.5_spmd.clone.sunk | while | flops 459257984 | bytes 1474405 | solution.py:80
  484.6 2.9 fusion.136
  489.9 2.9 fusion.136
  495.2 2.9 fusion.136
  500.4 2.9 fusion.136
  505.7 2.9 fusion.136
  511.1 2.9 fusion.136
  516.3 2.9 fusion.136
  521.6 2.9 fusion.136
  (189 shorter events, 125.3 us)
Async XLA Ops:
  7.2 19.5 %copy-start = (bf16[16,1024]{1,0:T(8,128)(2,1)S(1)}, bf16[16,1024]{1,0:T(8,128)(2,1)}, u32[]{:S(2)}) copy-start(bf16[16,1024]{1,0:T(8,128)(2,1)} %param.17) | copy-start | bytes 98308
  7.2 26.2 %copy-start.8 = (bf16[16,1024]{1,0:T(8,128)(2,1)S(1)}, bf16[16,1024]{1,0:T(8,128)(2,1)}, u32[]{:S(2)}) copy-start(bf16[16,1024]{1,0:T(8,128)(2,1)} %param.18) | copy-start | bytes 98308
  7.2 77.1 %copy-start.4 = (bf16[64,1024]{1,0:T(8,128)(2,1)S(1)}, bf16[64,1024]{1,0:T(8,128)(2,1)}, u32[]{:S(2)}) copy-start(bf16[64,1024]{1,0:T(8,128)(2,1)} %param.14) | copy-start | bytes 393220
  7.2 89.0 %copy-start.6 = (bf16[64,1024]{1,0:T(8,128)(2,1)S(1)}, bf16[64,1024]{1,0:T(8,128)(2,1)}, u32[]{:S(2)}) copy-start(bf16[64,1024]{1,0:T(8,128)(2,1)} %param.15) | copy-start | bytes 393220
  7.2 102.8 %all-gather.2.cloned.1.call-start = ((), (), s32[]{:S(2)}) async-start(), calls=%async_computation.9 | async-start | bytes 4718592 | tf_op jit(solution)/shard_map/all_gather | solution.py:106
  27.3 46.6 %all-to-all-start.3 = ((bf16[16,16,128]{2,0,1:T(8,128)(2,1)}), bf16[16,16,128]{2,0,1:T(8,128)(2,1)S(1)}, u32[]{:S(2)}, u32[]{:S(2)}) async-start(bf16[16,16,128]{2,0,1:T(8,128)(2,1)} %bitcast.12), calls=%async_computation.3 | async-start | bytes 131072 | tf_op jit(solution)/shard_map/all_to_all | solution.py:99
  74.5 14.6 %all-to-all-start.4 = ((bf16[16,16,128]{2,0,1:T(8,128)(2,1)}), bf16[16,16,128]{2,0,1:T(8,128)(2,1)S(1)}, u32[]{:S(2)}, u32[]{:S(2)}) async-start(bf16[16,16,128]{2,0,1:T(8,128)(2,1)} %bitcast.15), calls=%async_computation.4 | async-start | bytes 131072 | tf_op jit(solution)/shard_map/all_to_all | solution.py:100
  89.9 13.0 %all-to-all-start.1 = ((bf16[64,16,128]{2,0,1:T(8,128)(2,1)}), bf16[64,16,128]{2,0,1:T(8,128)(2,1)S(1)}, u32[]{:S(2)}, u32[]{:S(2)}) async-start(bf16[64,16,128]{2,0,1:T(8,128)(2,1)} %bitcast.6), calls=%async_computation.1 | async-start | bytes 524288 | tf_op jit(solution)/shard_map/all_to_all | solution.py:101
  103.7 13.1 %all-to-all-start.2 = ((bf16[64,16,128]{2,0,1:T(8,128)(2,1)}), bf16[64,16,128]{2,0,1:T(8,128)(2,1)S(1)}, u32[]{:S(2)}, u32[]{:S(2)}) async-start(bf16[64,16,128]{2,0,1:T(8,128)(2,1)} %bitcast.9), calls=%async_computation.2 | async-start | bytes 524288 | tf_op jit(solution)/shard_map/all_to_all | solution.py:102
  206.0 15.2 %all-to-all-start.7 = ((f32[8,1,2048]{2,1,0:T(1,128)}), f32[8,1,2048]{2,1,0:T(1,128)S(1)}, u32[]{:S(2)}, u32[]{:S(2)}) async-start(f32[8,1,2048]{2,1,0:T(1,128)} %reshape.233), calls=%async_computation.7 | async-start | bytes 131072 | tf_op jit(solution)/shard_map/all_to_all | solution.py:128
  229.1 7.2 %copy-start.9 = (s32[8192]{0:T(1024)S(1)}, s32[8192]{0:T(1024)}, u32[]{:S(2)}) copy-start(s32[8192]{0:T(1024)} %param.19) | copy-start | bytes 98308
  229.1 208.6 %all-to-all-start.5 = ((f32[1,2048,1024]{2,0,1:T(1,128)}), f32[1,2048,1024]{2,0,1:T(1,128)}, u32[]{:S(2)}, u32[]{:S(2)}) async-start(f32[1,2048,1024]{2,0,1:T(1,128)} %bitcast.220), calls=%async_computation.5 | async-start | bytes 16777216 | tf_op jit(solution)/shard_map/all_to_all | solution.py:126
  236.3 0.9 copy-start.5
  236.3 1.0 copy-start.7
  237.3 46.1 %collective-permute-start.1 = (bf16[64,1024]{1,0:T(8,128)(2,1)S(1)}, bf16[64,1024]{1,0:T(8,128)(2,1)S(1)}, u32[]{:S(2)}, u32[]{:S(2)}) collective-permute-start(bf16[64,1024]{1,0:T(8,128)(2,1)S(1)} %get-tuple-element.553), channel_id=1, source_target_pairs={{0,1},{1,2},{2,3},{3,4},{4,5},{5,6},{6,7},{7,8},{8,9},{9,10},{10,1... | collective-permute-start | bytes 393224 | tf_op jit(solution)/shard_map/while/body/eval_jaxpr/ppermute | solution.py:18
  243.1 41.7 %collective-permute-start = (bf16[64,1024]{1,0:T(8,128)(2,1)S(1)}, bf16[64,1024]{1,0:T(8,128)(2,1)S(1)}, u32[]{:S(2)}, u32[]{:S(2)}) collective-permute-start(bf16[64,1024]{1,0:T(8,128)(2,1)S(1)} %get-tuple-element.552), channel_id=1, source_target_pairs={{0,1},{1,2},{2,3},{3,4},{4,5},{5,6},{6,7},{7,8},{8,9},{9,10},{10,1... | collective-permute-start | bytes 393224 | tf_op jit(solution)/shard_map/while/body/eval_jaxpr/ppermute | solution.py:18
  284.9 49.9 %collective-permute-start.1 = (bf16[64,1024]{1,0:T(8,128)(2,1)S(1)}, bf16[64,1024]{1,0:T(8,128)(2,1)S(1)}, u32[]{:S(2)}, u32[]{:S(2)}) collective-permute-start(bf16[64,1024]{1,0:T(8,128)(2,1)S(1)} %get-tuple-element.553), channel_id=1, source_target_pairs={{0,1},{1,2},{2,3},{3,4},{4,5},{5,6},{6,7},{7,8},{8,9},{9,10},{10,1... | collective-permute-start | bytes 393224 | tf_op jit(solution)/shard_map/while/body/eval_jaxpr/ppermute | solution.py:18
  291.7 45.9 %collective-permute-start = (bf16[64,1024]{1,0:T(8,128)(2,1)S(1)}, bf16[64,1024]{1,0:T(8,128)(2,1)S(1)}, u32[]{:S(2)}, u32[]{:S(2)}) collective-permute-start(bf16[64,1024]{1,0:T(8,128)(2,1)S(1)} %get-tuple-element.552), channel_id=1, source_target_pairs={{0,1},{1,2},{2,3},{3,4},{4,5},{5,6},{6,7},{7,8},{8,9},{9,10},{10,1... | collective-permute-start | bytes 393224 | tf_op jit(solution)/shard_map/while/body/eval_jaxpr/ppermute | solution.py:18
  337.6 8.9 %collective-permute-start.1 = (bf16[64,1024]{1,0:T(8,128)(2,1)S(1)}, bf16[64,1024]{1,0:T(8,128)(2,1)S(1)}, u32[]{:S(2)}, u32[]{:S(2)}) collective-permute-start(bf16[64,1024]{1,0:T(8,128)(2,1)S(1)} %get-tuple-element.553), channel_id=1, source_target_pairs={{0,1},{1,2},{2,3},{3,4},{4,5},{5,6},{6,7},{7,8},{8,9},{9,10},{10,1... | collective-permute-start | bytes 393224 | tf_op jit(solution)/shard_map/while/body/eval_jaxpr/ppermute | solution.py:18
  344.6 3.9 collective-permute-start
  348.5 23.6 %collective-permute-start.1 = (bf16[64,1024]{1,0:T(8,128)(2,1)S(1)}, bf16[64,1024]{1,0:T(8,128)(2,1)S(1)}, u32[]{:S(2)}, u32[]{:S(2)}) collective-permute-start(bf16[64,1024]{1,0:T(8,128)(2,1)S(1)} %get-tuple-element.553), channel_id=1, source_target_pairs={{0,1},{1,2},{2,3},{3,4},{4,5},{5,6},{6,7},{7,8},{8,9},{9,10},{10,1... | collective-permute-start | bytes 393224 | tf_op jit(solution)/shard_map/while/body/eval_jaxpr/ppermute | solution.py:18
  355.3 18.8 %collective-permute-start = (bf16[64,1024]{1,0:T(8,128)(2,1)S(1)}, bf16[64,1024]{1,0:T(8,128)(2,1)S(1)}, u32[]{:S(2)}, u32[]{:S(2)}) collective-permute-start(bf16[64,1024]{1,0:T(8,128)(2,1)S(1)} %get-tuple-element.552), channel_id=1, source_target_pairs={{0,1},{1,2},{2,3},{3,4},{4,5},{5,6},{6,7},{7,8},{8,9},{9,10},{10,1... | collective-permute-start | bytes 393224 | tf_op jit(solution)/shard_map/while/body/eval_jaxpr/ppermute | solution.py:18
  374.1 10.8 %collective-permute-start.1 = (bf16[64,1024]{1,0:T(8,128)(2,1)S(1)}, bf16[64,1024]{1,0:T(8,128)(2,1)S(1)}, u32[]{:S(2)}, u32[]{:S(2)}) collective-permute-start(bf16[64,1024]{1,0:T(8,128)(2,1)S(1)} %get-tuple-element.553), channel_id=1, source_target_pairs={{0,1},{1,2},{2,3},{3,4},{4,5},{5,6},{6,7},{7,8},{8,9},{9,10},{10,1... | collective-permute-start | bytes 393224 | tf_op jit(solution)/shard_map/while/body/eval_jaxpr/ppermute | solution.py:18
  376.1 10.8 %collective-permute-start = (bf16[64,1024]{1,0:T(8,128)(2,1)S(1)}, bf16[64,1024]{1,0:T(8,128)(2,1)S(1)}, u32[]{:S(2)}, u32[]{:S(2)}) collective-permute-start(bf16[64,1024]{1,0:T(8,128)(2,1)S(1)} %get-tuple-element.552), channel_id=1, source_target_pairs={{0,1},{1,2},{2,3},{3,4},{4,5},{5,6},{6,7},{7,8},{8,9},{9,10},{10,1... | collective-permute-start | bytes 393224 | tf_op jit(solution)/shard_map/while/body/eval_jaxpr/ppermute | solution.py:18
  386.9 10.8 %collective-permute-start.1 = (bf16[64,1024]{1,0:T(8,128)(2,1)S(1)}, bf16[64,1024]{1,0:T(8,128)(2,1)S(1)}, u32[]{:S(2)}, u32[]{:S(2)}) collective-permute-start(bf16[64,1024]{1,0:T(8,128)(2,1)S(1)} %get-tuple-element.553), channel_id=1, source_target_pairs={{0,1},{1,2},{2,3},{3,4},{4,5},{5,6},{6,7},{7,8},{8,9},{9,10},{10,1... | collective-permute-start | bytes 393224 | tf_op jit(solution)/shard_map/while/body/eval_jaxpr/ppermute | solution.py:18
  388.9 10.8 %collective-permute-start = (bf16[64,1024]{1,0:T(8,128)(2,1)S(1)}, bf16[64,1024]{1,0:T(8,128)(2,1)S(1)}, u32[]{:S(2)}, u32[]{:S(2)}) collective-permute-start(bf16[64,1024]{1,0:T(8,128)(2,1)S(1)} %get-tuple-element.552), channel_id=1, source_target_pairs={{0,1},{1,2},{2,3},{3,4},{4,5},{5,6},{6,7},{7,8},{8,9},{9,10},{10,1... | collective-permute-start | bytes 393224 | tf_op jit(solution)/shard_map/while/body/eval_jaxpr/ppermute | solution.py:18
  399.7 10.8 %collective-permute-start.1 = (bf16[64,1024]{1,0:T(8,128)(2,1)S(1)}, bf16[64,1024]{1,0:T(8,128)(2,1)S(1)}, u32[]{:S(2)}, u32[]{:S(2)}) collective-permute-start(bf16[64,1024]{1,0:T(8,128)(2,1)S(1)} %get-tuple-element.553), channel_id=1, source_target_pairs={{0,1},{1,2},{2,3},{3,4},{4,5},{5,6},{6,7},{7,8},{8,9},{9,10},{10,1... | collective-permute-start | bytes 393224 | tf_op jit(solution)/shard_map/while/body/eval_jaxpr/ppermute | solution.py:18
  401.7 10.8 %collective-permute-start = (bf16[64,1024]{1,0:T(8,128)(2,1)S(1)}, bf16[64,1024]{1,0:T(8,128)(2,1)S(1)}, u32[]{:S(2)}, u32[]{:S(2)}) collective-permute-start(bf16[64,1024]{1,0:T(8,128)(2,1)S(1)} %get-tuple-element.552), channel_id=1, source_target_pairs={{0,1},{1,2},{2,3},{3,4},{4,5},{5,6},{6,7},{7,8},{8,9},{9,10},{10,1... | collective-permute-start | bytes 393224 | tf_op jit(solution)/shard_map/while/body/eval_jaxpr/ppermute | solution.py:18
  412.5 10.8 %collective-permute-start.1 = (bf16[64,1024]{1,0:T(8,128)(2,1)S(1)}, bf16[64,1024]{1,0:T(8,128)(2,1)S(1)}, u32[]{:S(2)}, u32[]{:S(2)}) collective-permute-start(bf16[64,1024]{1,0:T(8,128)(2,1)S(1)} %get-tuple-element.553), channel_id=1, source_target_pairs={{0,1},{1,2},{2,3},{3,4},{4,5},{5,6},{6,7},{7,8},{8,9},{9,10},{10,1... | collective-permute-start | bytes 393224 | tf_op jit(solution)/shard_map/while/body/eval_jaxpr/ppermute | solution.py:18
  414.5 10.8 %collective-permute-start = (bf16[64,1024]{1,0:T(8,128)(2,1)S(1)}, bf16[64,1024]{1,0:T(8,128)(2,1)S(1)}, u32[]{:S(2)}, u32[]{:S(2)}) collective-permute-start(bf16[64,1024]{1,0:T(8,128)(2,1)S(1)} %get-tuple-element.552), channel_id=1, source_target_pairs={{0,1},{1,2},{2,3},{3,4},{4,5},{5,6},{6,7},{7,8},{8,9},{9,10},{10,1... | collective-permute-start | bytes 393224 | tf_op jit(solution)/shard_map/while/body/eval_jaxpr/ppermute | solution.py:18
  427.4 1.8 copy-start.2
  455.9 26.2 %copy-start.3 = (bf16[8,64,16,128]{3,2,1,0:T(8,128)(2,1)S(1)}, bf16[8,64,16,128]{3,2,1,0:T(8,128)(2,1)}, u32[]{:S(2)}) copy-start(bf16[8,64,16,128]{3,2,1,0:T(8,128)(2,1)} %custom-call) | copy-start | bytes 6291460
  456.9 71.0 %all-to-all-start.8 = ((bf16[16,16,1024]{2,1,0:T(8,128)(2,1)}), bf16[16,16,1024]{2,1,0:T(8,128)(2,1)S(1)}, u32[]{:S(2)}, u32[]{:S(2)}) async-start(bf16[16,16,1024]{2,1,0:T(8,128)(2,1)} %divide_convert_fusion), calls=%async_computation.8 | async-start | bytes 1048576 | tf_op jit(solution)/shard_map/all_to_all | solution.py:139
  525.1 3.6 copy-start.1
Sparse Core Ops, SparseCore 0:
  26.8 48.2 all-gather.1
where the time goes:
time: 537 us; the launch traced here: 536 us
  waiting for transfers between devices  191 us (36%)
  starting transfers between devices  115 us (21%)
  matrix products  79.1 us (15%)
  other arithmetic  55.3 us (10%)
  local copies, waits for them, and re-layouts  50.5 us (9%)
  blocking collectives  26.1 us (5%)
  between operations  14.4 us (3%)
    ppermute x16, waiting for transfers between devices, shifted(): return lax.ppermute(block, axis, route)  138 us
    ppermute x16, starting transfers between devices, shifted(): return lax.ppermute(block, axis, route)  49.3 us
    dot_general x16, matrix products, attend(): jnp.einsum('qhk,kd->qhd', weights.astype(jnp.bfloat16), v_block, preferre...  47.2 us
    all_to_all x1, waiting for transfers between devices, on_device(): lax.all_to_all(spread(new_k), 'head', split_axis=1, concat_axis=0, tiled=...  40.5 us
    all_to_all x1, starting transfers between devices, on_device(): lax.all_to_all(fresh_out, 'head', split_axis=0, concat_axis=1, tiled=True)  25.2 us
    unnamed x32, local copies, waits for them, and re-layouts  19.4 us
    unnamed x3, other arithmetic  19.2 us
    sub x8, matrix products, attend(): masked - row_max[..., None]  18.5 us
  transfers between devices with their start and end apart: 24, of which 19 were waited for; matrix products, arithmetic and copies ran while one was open for 14% of the time, Pallas kernels for 0%

commit v1 on v0

v1 whole, which is shorter than its diff:
```python
import functools

import jax
import jax.numpy as jnp
from jax import lax
from jax.experimental import pallas as pl
from jax.experimental.pallas import tpu as pltpu
from jax.sharding import PartitionSpec as P

QH, KVH, HD = 128, 8, 128
GROUP = QH // KVH
PT, NT = 64, 16
BOTH = ("ctx", "head")
COUNT = 128
PEERS = 32
HEADS = 4
ROWS = PEERS * HEADS * NT
KVR = 80
BF, F32 = jnp.bfloat16, jnp.float32
NEG = -1e30
SCALE = HD**-0.5 * 1.4426950408889634
VM = pl.BlockSpec(memory_space=pltpu.VMEM)

GROUPS = [[(y * 4 + x) * 16 + h for y in range(2) for h in range(16)] for x in range(4)]
SIBLING = [(i, i ^ 1) for i in range(COUNT)]
OTHER_Y = [(i, i ^ 2) for i in range(COUNT)]
BACK1 = [(i, i + 4) for i in range(COUNT - 4)]
BACK2 = [(i, i + 8) for i in range(COUNT - 8)]


def along_x(d):
    return [(i, (i // 64) * 64 + (i // 16 + d) % 4 * 16 + i % 16) for i in range(COUNT)]


def params(**kw):
    return pltpu.CompilerParams(vmem_limit_bytes=56 * 2**20, **kw)


def pack_kv(k_ref, v_ref, nk_ref, nv_ref, out_ref, win_ref):
    for j in range(KVH):
        cols = slice(j * HD, (j + 1) * HD)
        for core in range(2):
            half = slice(32 * core, 32 * core + 32)
            new = nv_ref if core else nk_ref
            for y in range(2):
                d = y * 16 + j * 2 + core
                out_ref[d, 0:32, :] = k_ref[half, cols]
                out_ref[d, 32:64, :] = v_ref[half, cols]
                out_ref[d, 64:80, :] = new[:, cols]
    win_ref[:, : KVH * HD] = k_ref[...]
    win_ref[:, KVH * HD :] = v_ref[...]


def head_of(d, h):
    y, j, core = d // 16, d % 16 // 2, d % 2
    return j * GROUP + (y * 2 + core) * HEADS + h


def pack_q(q_ref, out_ref):
    for d in range(PEERS):
        for h in range(HEADS):
            g = head_of(d, h)
            out_ref[d, h * NT : (h + 1) * NT, :] = q_ref[:, g * HD : (g + 1) * HD]


def unpack_out(blk_ref, out_ref):
    for d in range(PEERS):
        for h in range(HEADS):
            g = head_of(d, h)
            out_ref[:, g * HD : (g + 1) * HD] = blk_ref[d, h * NT : (h + 1) * NT, :]


RB = 256


def question(chunks, s_ref, *refs):
    q_ref = refs[0]
    kv = refs[1 : 1 + 2 * chunks]
    out_ref = refs[1 + 2 * chunks]
    step = pl.program_id(0)
    core, x = s_ref[0], s_ref[1]
    q = q_ref[...]
    row = step * RB + lax.broadcasted_iota(jnp.int32, (RB, 1), 0)

    def token(src, t, at_x):
        return ((src // 16) * 4 + at_x) * 256 + (src % 16) * 16 + t

    q_tok = token(row // 64, row % 16, x)
    col = lax.broadcasted_iota(jnp.int32, (1, 512), 1)

    def update(state, k, v, visible):
        m, l, acc = state
        s = lax.dot_general(q, k, (((1,), (1,)), ((), ())), preferred_element_type=F32)
        if visible is not None:
            s = jnp.where(visible, s, NEG)
        top = jnp.max(s, axis=1, keepdims=True)
        m_new = top if m is None else jnp.maximum(m, top)
        p = jnp.exp2((s - m_new) * SCALE)
        psum = jnp.sum(p, axis=1, keepdims=True)
        pv = jnp.dot(p.astype(BF), v, preferred_element_type=F32)
        if m is None:
            return m_new, psum, pv
        a = jnp.exp2((m - m_new) * SCALE)
        return m_new, l * a + psum, acc * a + pv

    state = (None, None, None)
    for c in range(chunks):
        mine, other = kv[2 * c], kv[2 * c + 1]
        for ref in (mine, other):
            k = ref[:, 0:32, :].reshape(1024, HD)
            v = ref[:, 32:64, :].reshape(1024, HD)
            state = update(state, k, v, None)
        a = mine[:, 64:80, :].reshape(512, HD)
        b = other[:, 64:80, :].reshape(512, HD)
        first = core == 0
        k = jnp.where(first, a, b)
        v = jnp.where(first, b, a)
        k_tok = token(col // 16, col % 16, s_ref[2 + c])
        state = update(state, k, v, k_tok <= q_tok)
    m, l, acc = state
    out_ref[...] = (acc / l).astype(BF)


def passage(s_ref, q_ref, start_ref, *refs):
    wins, o_ref, bias_ref = refs[:12], refs[12], refs[13]
    @pl.when(pl.program_id(0) == 0)
    def _():
        yh, core = s_ref[0], s_ref[1]
        col = lax.broadcasted_iota(jnp.int32, (PT, 768), 1)
        blk, t = col // 64, col % 64
        side, level, flip = blk // 6, blk % 6 // 2, blk % 2
        pos = level * 256 + (yh ^ flip) * 128 + (core ^ side) * 64 + t
        q_pos = 512 + yh * 128 + core * 64 + lax.broadcasted_iota(jnp.int32, (PT, 768), 0)
        ok = (pos <= q_pos) & (pos >= start_ref[...])
        bias_ref[...] = jnp.where(ok, 0.0, NEG)

    k = jnp.concatenate([r[...] for r in wins[:6]], axis=0)
    v = jnp.concatenate([r[...] for r in wins[6:]], axis=0)
    bias = bias_ref[...]
    for part in range(4):
        q = jnp.concatenate(
            [q_ref[:, (part * 4 + h) * HD : (part * 4 + h + 1) * HD] for h in range(4)], axis=0
        )
        s = lax.dot_general(q, k, (((1,), (1,)), ((), ())), preferred_element_type=F32)
        s = (s.reshape(4, PT, 768) + bias[None]).reshape(4 * PT, 768)
        m = jnp.max(s, axis=1, keepdims=True)
        p = jnp.exp2((s - m) * SCALE)
        l = jnp.sum(p, axis=1, keepdims=True)
        o = jnp.dot(p.astype(BF), v, preferred_element_type=F32) / l
        o = o.astype(BF)
        for h in range(4):
            o_ref[:, (part * 4 + h) * HD : (part * 4 + h + 1) * HD] = o[h * PT : (h + 1) * PT]


def permute(block, route):
    return lax.ppermute(block, BOTH, route)


def exchange(blocks):
    return lax.all_to_all(
        blocks, BOTH, split_axis=0, concat_axis=0, tiled=True, axis_index_groups=GROUPS
    )


def on_device(passage_q, passage_k, passage_v, new_q, new_k, new_v, segments):
    ctx, head = lax.axis_index("ctx"), lax.axis_index("head")
    x, core, y_hi = ctx % 4, head % 2, head // 2 % 2
    shape = jax.ShapeDtypeStruct

    kv_blocks, own = pl.pallas_call(
        pack_kv,
        out_shape=(shape((PEERS, KVR, HD), BF), shape((PT, 2 * KVH * HD), BF)),
        in_specs=[VM] * 4,
        out_specs=(VM, VM),
        compiler_params=params(),
        name="pack_kv",
    )(passage_k, passage_v, new_k, new_v)
    q_blocks = pl.pallas_call(
        pack_q,
        out_shape=shape((PEERS, HEADS * NT, HD), BF),
        in_specs=[VM],
        out_specs=VM,
        compiler_params=params(),
        name="pack_q",
    )(new_q)

    kv0 = exchange(kv_blocks)
    q = exchange(q_blocks).reshape(ROWS, HD)
    chunks = [kv0] + [permute(kv0, along_x(d)) for d in (1, 3, 2)]
    pairs = []
    for c in chunks:
        pairs += [c, permute(c, SIBLING)]

    level0 = jnp.concatenate([own, permute(own, OTHER_Y)], axis=0)
    level1 = permute(level0, BACK1)
    level2 = permute(level0, BACK2)
    wins = [level2, level1, level0]
    wins += [permute(w, SIBLING) for w in wins]

    where = jnp.stack([core, x, x, (x + 3) % 4, (x + 1) % 4, (x + 2) % 4]).astype(jnp.int32)
    full = pl.BlockSpec((PEERS, KVR, HD), lambda i, s: (0, 0, 0))
    out_rows = pl.pallas_call(
        functools.partial(question, 4),
        out_shape=shape((ROWS, HD), BF),
        grid_spec=pltpu.PrefetchScalarGridSpec(
            num_scalar_prefetch=1,
            grid=(ROWS // RB,),
            in_specs=[pl.BlockSpec((RB, HD), lambda i, s: (i, 0))] + [full] * 8,
            out_specs=pl.BlockSpec((RB, HD), lambda i, s: (i, 0)),
        ),
        compiler_params=params(),
        cost_estimate=pl.CostEstimate(
            flops=4 * ROWS * 10240 * HD, bytes_accessed=8 * 2**20, transcendentals=ROWS * 10240
        ),
        name="question",
    )(where, q, *pairs)
    new_blocks = exchange(out_rows.reshape(PEERS, HEADS * NT, HD))
    new_out = pl.pallas_call(
        unpack_out,
        out_shape=shape((NT, QH * HD), BF),
        in_specs=[VM],
        out_specs=VM,
        compiler_params=params(),
        name="unpack_out",
    )(new_blocks)

    flat = ctx * 16 + head
    padded = jnp.concatenate([jnp.full((512,), -1, jnp.int32), segments])
    near = lax.dynamic_slice_in_dim(padded, flat // 4 * 256, 768, 0)
    seg_q = lax.dynamic_slice_in_dim(segments, flat * PT, PT, 0)
    start = jnp.sum((near[None, :] < seg_q[:, None]).astype(jnp.int32), axis=1, keepdims=True)
    place = jnp.stack([y_hi, core]).astype(jnp.int32)
    col = lambda i, s: (0, i)
    col_v = lambda i, s: (0, i + KVH)
    pass_out = pl.pallas_call(
        passage,
        out_shape=shape((PT, QH * HD), BF),
        grid_spec=pltpu.PrefetchScalarGridSpec(
            num_scalar_prefetch=1,
            grid=(KVH,),
            in_specs=[
                pl.BlockSpec((PT, GROUP * HD), col),
                pl.BlockSpec((PT, 1), lambda i, s: (0, 0)),
            ]
            + [pl.BlockSpec((2 * PT, HD), col)] * 6
            + [pl.BlockSpec((2 * PT, HD), col_v)] * 6,
            out_specs=pl.BlockSpec((PT, GROUP * HD), col),
            scratch_shapes=[pltpu.VMEM((PT, 768), F32)],
        ),
        compiler_params=params(),
        cost_estimate=pl.CostEstimate(
            flops=4 * PT * QH * 768 * HD, bytes_accessed=7 * 2**20, transcendentals=PT * QH * 768
        ),
        name="passage",
    )(place, passage_q, start, *wins, *wins)
    return pass_out, new_out


def solution(mesh):
    row = P(BOTH, None)
    return jax.shard_map(
        on_device,
        mesh=mesh,
        in_specs=(row,) * 6 + (P(),),
        out_specs=(row, row),
        check_vma=False,
    )
```

time: 537 us -> 175 us (0.33)
  the two profiles are of different devices: /device:TPU:31 before, /device:TPU:1 now
where the time goes in v1:
time: 175 us; the launch traced here: 174 us
  Pallas kernels  70.2 us (40%)
  waiting for transfers between devices  52.4 us (30%)
  starting transfers between devices  46.1 us (26%)
  local copies, waits for them, and re-layouts  4.05 us (2%)
    pallas_call x1, Pallas kernels, on_device(): pl.pallas_call(functools.partial(question, 4), out_shape=shape((ROWS, HD)...  47 us
    all_to_all x3, starting transfers between devices, exchange(): lax.all_to_all(blocks, BOTH, split_axis=0, concat_axis=0, tiled=True, axi...  30.5 us
    all_to_all x3, waiting for transfers between devices, exchange(): lax.all_to_all(blocks, BOTH, split_axis=0, concat_axis=0, tiled=True, axi...  27.9 us
    ppermute x13, waiting for transfers between devices, permute(): return lax.ppermute(block, BOTH, route)  24.6 us
    pallas_call x1, Pallas kernels, on_device(): pl.pallas_call(passage, out_shape=shape((PT, QH * HD), BF), grid_spec=plt...  17.4 us
    ppermute x13, starting transfers between devices, permute(): return lax.ppermute(block, BOTH, route)  15.6 us
  transfers between devices with their start and end apart: 16, of which 4 were waited for; matrix products, arithmetic and copies ran while one was open for 2% of the time, Pallas kernels for 38%

profile of v1, /device:TPU:1, one launch (start us, length us, event | category | flops | bytes accessed | tf_op | source)
XLA Modules:
  0.0 174.4 jit_solution(11926953044418599705)
XLA Ops:
  0.6 2.0 %pack_kv.1 = (bf16[32,80,128]{2,1,0:T(8,128)(2,1)}, bf16[64,2048]{1,0:T(8,128)(2,1)}) custom-call(bf16[64,1024]{1,0:T(8,128)(2,1)} %k_ref.1, bf16[64,1024]{1,0:T(8,128)(2,1)} %v_ref.1, bf16[16,1024]{1,0:T(8,128)(2,1)} %nk_ref.1, bf16[16,1024]{1,0:T(8,128)(2,1)} %nv_ref.1), custom_call_target="tpu_custom_call" | custom-call | tf_op jit(solution)/shard_map/pack_kv/pallas_call | solution.py:170
  2.6 9.7 %all-to-all-start.1 = ((bf16[32,80,128]{2,1,0:T(8,128)(2,1)}), bf16[32,80,128]{2,1,0:T(8,128)(2,1)S(1)}, u32[]{:S(2)}, u32[]{:S(2)}) async-start(bf16[32,80,128]{2,1,0:T(8,128)(2,1)} %get-tuple-element.5), calls=%async_computation.1 | async-start | bytes 1310720 | tf_op jit(solution)/shard_map/all_to_all | solution.py:160
  12.3 3.0 %collective-permute-start = (bf16[64,2048]{1,0:T(8,128)(2,1)}, bf16[64,2048]{1,0:T(8,128)(2,1)S(1)}, u32[]{:S(2)}, u32[]{:S(2)}) collective-permute-start(bf16[64,2048]{1,0:T(8,128)(2,1)} %get-tuple-element.4), channel_id=1, source_target_pairs={{0,2},{1,3},{2,0},{3,1},{4,6},{5,7},{6,4},{7,5},{8,10},{9,11},{10,... | collective-permute-start | bytes 786440 | tf_op jit(solution)/shard_map/ppermute | solution.py:156
  15.3 10.2 %all-to-all-done.1.refs_1_ = bf16[32,80,128]{2,1,0:T(8,128)(2,1)S(1)} async-done(((bf16[32,80,128]{2,1,0:T(8,128)(2,1)}), bf16[32,80,128]{2,1,0:T(8,128)(2,1)S(1)}, u32[]{:S(2)}, u32[]{:S(2)}) %all-to-all-start.1) | async-done | bytes 655392 | tf_op jit(solution)/shard_map/all_to_all | solution.py:160
  25.5 2.5 %collective-permute-start.9 = (bf16[32,80,128]{2,1,0:T(8,128)(2,1)S(1)}, bf16[32,80,128]{2,1,0:T(8,128)(2,1)S(1)}, u32[]{:S(2)}, u32[]{:S(2)}) collective-permute-start(bf16[32,80,128]{2,1,0:T(8,128)(2,1)S(1)} %all-to-all-done.1.refs_1_), channel_id=1, source_target_pairs={{0,48},{1,49},{2,50},{3,51},{4,52},{5,53},{6,54},{7,55},{8,56},{9,... | collective-permute-start | bytes 1966088 | tf_op jit(solution)/shard_map/ppermute | solution.py:156
  28.0 0.5 collective-permute-start.11
  28.5 0.6 collective-permute-start.7
  29.1 1.0 constant_dynamic-update-slice_fusion.1
  30.1 0.0 collective-permute-done
  30.1 0.0 copy-start.3
  30.1 3.3 %collective-permute-start.1 = (bf16[128,2048]{1,0:T(8,128)(2,1)S(1)}, bf16[128,2048]{1,0:T(8,128)(2,1)S(1)}, u32[]{:S(2)}, u32[]{:S(2)}) collective-permute-start(bf16[128,2048]{1,0:T(8,128)(2,1)S(1)} %constant_dynamic-update-slice_fusion.refs_2_.refs_8_), channel_id=1, source_target_pairs={{0,8},{1,9},{2,10},{3,11},{4,12},{5,13},{6,14},{7,15},{8,16},{9,17... | collective-permute-start | bytes 1572872 | tf_op jit(solution)/shard_map/ppermute | solution.py:156
  33.4 1.3 collective-permute-start.6
  34.7 21.3 %collective-permute-done.9.refs_5_ = bf16[32,80,128]{2,1,0:T(8,128)(2,1)S(1)} collective-permute-done((bf16[32,80,128]{2,1,0:T(8,128)(2,1)S(1)}, bf16[32,80,128]{2,1,0:T(8,128)(2,1)S(1)}, u32[]{:S(2)}, u32[]{:S(2)}) %collective-permute-start.9) | collective-permute-done | bytes 655392 | tf_op jit(solution)/shard_map/ppermute | solution.py:156
  56.0 1.0 collective-permute-start.10
  57.0 0.0 collective-permute-done.11.refs_7_
  57.0 0.1 collective-permute-start.12
  57.1 3.2 %collective-permute-done.7.refs_3_ = bf16[32,80,128]{2,1,0:T(8,128)(2,1)} collective-permute-done((bf16[32,80,128]{2,1,0:T(8,128)(2,1)S(1)}, bf16[32,80,128]{2,1,0:T(8,128)(2,1)}, u32[]{:S(2)}, u32[]{:S(2)}) %collective-permute-start.7) | collective-permute-done | bytes 655392 | tf_op jit(solution)/shard_map/ppermute | solution.py:156
  60.3 0.5 collective-permute-start.8
  60.8 0.0 collective-permute-done.1.refs_0_.refs_6_
  60.8 2.1 %collective-permute-start.2 = (bf16[128,2048]{1,0:T(8,128)(2,1)S(1)}, bf16[128,2048]{1,0:T(8,128)(2,1)}, u32[]{:S(2)}, u32[]{:S(2)}) collective-permute-start(bf16[128,2048]{1,0:T(8,128)(2,1)S(1)} %constant_dynamic-update-slice_fusion.refs_2_.refs_8_), channel_id=1, source_target_pairs={{0,4},{1,5},{2,6},{3,7},{4,8},{5,9},{6,10},{7,11},{8,12},{9,13},{1... | collective-permute-start | bytes 1572872 | tf_op jit(solution)/shard_map/ppermute | solution.py:156
  62.9 1.9 %pack_q.1 = bf16[32,64,128]{2,1,0:T(8,128)(2,1)} custom-call(bf16[16,16384]{1,0:T(8,128)(2,1)} %q_ref.3), custom_call_target="tpu_custom_call" | custom-call | tf_op jit(solution)/shard_map/pack_q/pallas_call | solution.py:178
  64.8 15.3 %all-to-all-start = ((bf16[32,64,128]{2,1,0:T(8,128)(2,1)}), bf16[32,64,128]{2,1,0:T(8,128)(2,1)S(1)}, u32[]{:S(2)}, u32[]{:S(2)}) async-start(bf16[32,64,128]{2,1,0:T(8,128)(2,1)} %pack_q.1), calls=%async_computation | async-start | bytes 1048576 | tf_op jit(solution)/shard_map/all_to_all | solution.py:160
  80.3 0.1 dynamic_slice.7
  80.3 0.6 stack.33.s_ref
  80.9 0.1 pad_dynamic-slice_fusion
  81.0 0.0 collective-permute-done.2.refs_1_.refs_7_
  81.0 0.3 collective-permute-start.5
  81.3 0.0 collective-permute-done.6.refs_2_
  81.3 0.3 collective-permute-start.3
  81.5 0.0 collective-permute-done.10.refs_6_
  81.5 0.2 collective-permute-start.4
  81.8 17.7 %all-to-all-done = bf16[32,64,128]{2,1,0:T(8,128)(2,1)S(1)} async-done(((bf16[32,64,128]{2,1,0:T(8,128)(2,1)}), bf16[32,64,128]{2,1,0:T(8,128)(2,1)S(1)}, u32[]{:S(2)}, u32[]{:S(2)}) %all-to-all-start) | async-done | bytes 524320 | tf_op jit(solution)/shard_map/all_to_all | solution.py:160
  99.5 0.0 collective-permute-done.12.refs_8_
  99.5 0.0 collective-permute-done.8.refs_4_
  99.5 0.8 copy-done.2
  100.3 47.0 %question.1 = bf16[2048,128]{1,0:T(8,128)(2,1)} custom-call(s32[6]{0:T(128)} %stack.33.s_ref, bf16[2048,128]{1,0:T(8,128)(2,1)} %bitcast.9, bf16[32,80,128]{2,1,0:T(8,128)(2,1)} %copy-done.1, bf16[32,80,128]{2,1,0:T(8,128)(2,1)} %collective-permute-done.6.refs_2_, bf16[32,80,128]{2,1,0:T(8,128)(2,1)} %collective-permute-done.7.refs_3_, ...), custom_call_target="tpu_custom_call" | custom-call | flops 10737418240 | bytes 8388608 | tf_op jit(solution)/shard_map/question/pallas_call | solution.py:202
  147.3 5.4 %all-to-all-start.2 = ((bf16[32,64,128]{2,1,0:T(8,128)(2,1)}), bf16[32,64,128]{2,1,0:T(8,128)(2,1)S(1)}, u32[]{:S(2)}, u32[]{:S(2)}) async-start(bf16[32,64,128]{2,1,0:T(8,128)(2,1)} %bitcast.10), calls=%async_computation.2 | async-start | bytes 1048576 | tf_op jit(solution)/shard_map/all_to_all | solution.py:160
  152.7 0.2 convert_reduce_fusion
  152.9 0.7 copy.10.start_ref
  153.6 0.7 pad_add_fusion.s_ref
  154.3 0.0 collective-permute-done.5.refs_5_.refs_11_
  154.3 0.0 collective-permute-done.3.refs_3_.refs_9_
  154.3 0.0 collective-permute-done.4.refs_4_.refs_10_
  154.3 17.4 %passage.1 = bf16[64,16384]{1,0:T(8,128)(2,1)} custom-call(s32[2]{0:T(128)} %pad_add_fusion.s_ref, bf16[64,16384]{1,0:T(8,128)(2,1)} %q_ref.2, s32[64,1]{1,0:T(8,128)} %copy.10.start_ref, bf16[128,2048]{1,0:T(8,128)(2,1)} %copy-done.7, bf16[128,2048]{1,0:T(8,128)(2,1)} %collective-permute-done.2.refs_1_.refs_7_, bf16[128,2048]{1,0:T(8,128)(2,1)} %copy-done.3, ...), custom_call_target="tpu_custom_call" | custom-call | flops 3221225472 | bytes 7340032 | tf_op jit(solution)/shard_map/passage/pallas_call | solution.py:235
  171.7 0.0 all-to-all-done.2.blk_ref
  171.7 0.0 copy-start
  171.7 0.8 copy-done
  172.5 1.9 %unpack_out.1 = bf16[16,16384]{1,0:T(8,128)(2,1)} custom-call(bf16[32,64,128]{2,1,0:T(8,128)(2,1)} %copy-done), custom_call_target="tpu_custom_call" | custom-call | tf_op jit(solution)/shard_map/unpack_out/pallas_call | solution.py:218
  (13 shorter events, 0.0 us)
Async XLA Ops:
  2.6 77.7 %copy-start.4 = (s32[8192]{0:T(1024)S(1)}, s32[8192]{0:T(1024)}, u32[]{:S(2)}) copy-start(s32[8192]{0:T(1024)} %param.13) | copy-start | bytes 98308
  2.6 22.9 %all-to-all-start.1 = ((bf16[32,80,128]{2,1,0:T(8,128)(2,1)}), bf16[32,80,128]{2,1,0:T(8,128)(2,1)S(1)}, u32[]{:S(2)}, u32[]{:S(2)}) async-start(bf16[32,80,128]{2,1,0:T(8,128)(2,1)} %get-tuple-element.5), calls=%async_computation.1 | async-start | bytes 1310720 | tf_op jit(solution)/shard_map/all_to_all | solution.py:160
  12.3 17.7 %collective-permute-start = (bf16[64,2048]{1,0:T(8,128)(2,1)}, bf16[64,2048]{1,0:T(8,128)(2,1)S(1)}, u32[]{:S(2)}, u32[]{:S(2)}) collective-permute-start(bf16[64,2048]{1,0:T(8,128)(2,1)} %get-tuple-element.4), channel_id=1, source_target_pairs={{0,2},{1,3},{2,0},{3,1},{4,6},{5,7},{6,4},{7,5},{8,10},{9,11},{10,... | collective-permute-start | bytes 786440 | tf_op jit(solution)/shard_map/ppermute | solution.py:156
  25.5 74.0 %copy-start.1 = (bf16[32,80,128]{2,1,0:T(8,128)(2,1)}, bf16[32,80,128]{2,1,0:T(8,128)(2,1)S(1)}, u32[]{:S(2)}) copy-start(bf16[32,80,128]{2,1,0:T(8,128)(2,1)S(1)} %all-to-all-done.1.refs_1_) | copy-start | bytes 1966084
  25.5 30.5 %collective-permute-start.9 = (bf16[32,80,128]{2,1,0:T(8,128)(2,1)S(1)}, bf16[32,80,128]{2,1,0:T(8,128)(2,1)S(1)}, u32[]{:S(2)}, u32[]{:S(2)}) collective-permute-start(bf16[32,80,128]{2,1,0:T(8,128)(2,1)S(1)} %all-to-all-done.1.refs_1_), channel_id=1, source_target_pairs={{0,48},{1,49},{2,50},{3,51},{4,52},{5,53},{6,54},{7,55},{8,56},{9,... | collective-permute-start | bytes 1966088 | tf_op jit(solution)/shard_map/ppermute | solution.py:156
  28.0 29.0 %collective-permute-start.11 = (bf16[32,80,128]{2,1,0:T(8,128)(2,1)S(1)}, bf16[32,80,128]{2,1,0:T(8,128)(2,1)S(1)}, u32[]{:S(2)}, u32[]{:S(2)}) collective-permute-start(bf16[32,80,128]{2,1,0:T(8,128)(2,1)S(1)} %all-to-all-done.1.refs_1_), channel_id=1, source_target_pairs={{0,32},{1,33},{2,34},{3,35},{4,36},{5,37},{6,38},{7,39},{8,40},{9,... | collective-permute-start | bytes 1966088 | tf_op jit(solution)/shard_map/ppermute | solution.py:156
  28.5 31.8 %collective-permute-start.7 = (bf16[32,80,128]{2,1,0:T(8,128)(2,1)S(1)}, bf16[32,80,128]{2,1,0:T(8,128)(2,1)}, u32[]{:S(2)}, u32[]{:S(2)}) collective-permute-start(bf16[32,80,128]{2,1,0:T(8,128)(2,1)S(1)} %all-to-all-done.1.refs_1_), channel_id=1, source_target_pairs={{0,16},{1,17},{2,18},{3,19},{4,20},{5,21},{6,22},{7,23},{8,24},{9,... | collective-permute-start | bytes 1966088 | tf_op jit(solution)/shard_map/ppermute | solution.py:156
  30.1 117.2 %copy-start.3 = (bf16[128,2048]{1,0:T(8,128)(2,1)}, bf16[128,2048]{1,0:T(8,128)(2,1)S(1)}, u32[]{:S(2)}) copy-start(bf16[128,2048]{1,0:T(8,128)(2,1)S(1)} %constant_dynamic-update-slice_fusion.refs_2_.refs_8_) | copy-start | bytes 1572868
  30.1 30.7 %collective-permute-start.1 = (bf16[128,2048]{1,0:T(8,128)(2,1)S(1)}, bf16[128,2048]{1,0:T(8,128)(2,1)S(1)}, u32[]{:S(2)}, u32[]{:S(2)}) collective-permute-start(bf16[128,2048]{1,0:T(8,128)(2,1)S(1)} %constant_dynamic-update-slice_fusion.refs_2_.refs_8_), channel_id=1, source_target_pairs={{0,8},{1,9},{2,10},{3,11},{4,12},{5,13},{6,14},{7,15},{8,16},{9,17... | collective-permute-start | bytes 1572872 | tf_op jit(solution)/shard_map/ppermute | solution.py:156
  33.4 47.9 %collective-permute-start.6 = (bf16[32,80,128]{2,1,0:T(8,128)(2,1)S(1)}, bf16[32,80,128]{2,1,0:T(8,128)(2,1)}, u32[]{:S(2)}, u32[]{:S(2)}) collective-permute-start(bf16[32,80,128]{2,1,0:T(8,128)(2,1)S(1)} %all-to-all-done.1.refs_1_), channel_id=1, source_target_pairs={{0,1},{1,0},{2,3},{3,2},{4,5},{5,4},{6,7},{7,6},{8,9},{9,8},{10,11... | collective-permute-start | bytes 1966088 | tf_op jit(solution)/shard_map/ppermute | solution.py:156
  56.0 43.5 %copy-start.5 = (bf16[32,80,128]{2,1,0:T(8,128)(2,1)}, bf16[32,80,128]{2,1,0:T(8,128)(2,1)S(1)}, u32[]{:S(2)}) copy-start(bf16[32,80,128]{2,1,0:T(8,128)(2,1)S(1)} %collective-permute-done.9.refs_5_) | copy-start | bytes 1966084
  56.0 25.5 %collective-permute-start.10 = (bf16[32,80,128]{2,1,0:T(8,128)(2,1)S(1)}, bf16[32,80,128]{2,1,0:T(8,128)(2,1)}, u32[]{:S(2)}, u32[]{:S(2)}) collective-permute-start(bf16[32,80,128]{2,1,0:T(8,128)(2,1)S(1)} %collective-permute-done.9.refs_5_), channel_id=1, source_target_pairs={{0,1},{1,0},{2,3},{3,2},{4,5},{5,4},{6,7},{7,6},{8,9},{9,8},{10,11... | collective-permute-start | bytes 1966088 | tf_op jit(solution)/shard_map/ppermute | solution.py:156
  57.0 42.5 %copy-start.6 = (bf16[32,80,128]{2,1,0:T(8,128)(2,1)}, bf16[32,80,128]{2,1,0:T(8,128)(2,1)S(1)}, u32[]{:S(2)}) copy-start(bf16[32,80,128]{2,1,0:T(8,128)(2,1)S(1)} %collective-permute-done.11.refs_7_) | copy-start | bytes 1966084
  57.0 42.5 %collective-permute-start.12 = (bf16[32,80,128]{2,1,0:T(8,128)(2,1)S(1)}, bf16[32,80,128]{2,1,0:T(8,128)(2,1)}, u32[]{:S(2)}, u32[]{:S(2)}) collective-permute-start(bf16[32,80,128]{2,1,0:T(8,128)(2,1)S(1)} %collective-permute-done.11.refs_7_), channel_id=1, source_target_pairs={{0,1},{1,0},{2,3},{3,2},{4,5},{5,4},{6,7},{7,6},{8,9},{9,8},{10,11... | collective-permute-start | bytes 1966088 | tf_op jit(solution)/shard_map/ppermute | solution.py:156
  60.3 39.2 %collective-permute-start.8 = (bf16[32,80,128]{2,1,0:T(8,128)(2,1)}, bf16[32,80,128]{2,1,0:T(8,128)(2,1)}, u32[]{:S(2)}, u32[]{:S(2)}) collective-permute-start(bf16[32,80,128]{2,1,0:T(8,128)(2,1)} %collective-permute-done.7.refs_3_), channel_id=1, source_target_pairs={{0,1},{1,0},{2,3},{3,2},{4,5},{5,4},{6,7},{7,6},{8,9},{9,8},{10,11... | collective-permute-start | bytes 1966088 | tf_op jit(solution)/shard_map/ppermute | solution.py:156
  60.8 4.0 %copy-start.7 = (bf16[128,2048]{1,0:T(8,128)(2,1)}, bf16[128,2048]{1,0:T(8,128)(2,1)S(1)}, u32[]{:S(2)}) copy-start(bf16[128,2048]{1,0:T(8,128)(2,1)S(1)} %collective-permute-done.1.refs_0_.refs_6_) | copy-start | bytes 1572868
  60.8 20.2 %collective-permute-start.2 = (bf16[128,2048]{1,0:T(8,128)(2,1)S(1)}, bf16[128,2048]{1,0:T(8,128)(2,1)}, u32[]{:S(2)}, u32[]{:S(2)}) collective-permute-start(bf16[128,2048]{1,0:T(8,128)(2,1)S(1)} %constant_dynamic-update-slice_fusion.refs_2_.refs_8_), channel_id=1, source_target_pairs={{0,4},{1,5},{2,6},{3,7},{4,8},{5,9},{6,10},{7,11},{8,12},{9,13},{1... | collective-permute-start | bytes 1572872 | tf_op jit(solution)/shard_map/ppermute | solution.py:156
  64.8 34.7 %all-to-all-start = ((bf16[32,64,128]{2,1,0:T(8,128)(2,1)}), bf16[32,64,128]{2,1,0:T(8,128)(2,1)S(1)}, u32[]{:S(2)}, u32[]{:S(2)}) async-start(bf16[32,64,128]{2,1,0:T(8,128)(2,1)} %pack_q.1), calls=%async_computation | async-start | bytes 1048576 | tf_op jit(solution)/shard_map/all_to_all | solution.py:160
  81.0 73.3 %collective-permute-start.5 = (bf16[128,2048]{1,0:T(8,128)(2,1)S(1)}, bf16[128,2048]{1,0:T(8,128)(2,1)}, u32[]{:S(2)}, u32[]{:S(2)}) collective-permute-start(bf16[128,2048]{1,0:T(8,128)(2,1)S(1)} %constant_dynamic-update-slice_fusion.refs_2_.refs_8_), channel_id=1, source_target_pairs={{0,1},{1,0},{2,3},{3,2},{4,5},{5,4},{6,7},{7,6},{8,9},{9,8},{10,11... | collective-permute-start | bytes 1572872 | tf_op jit(solution)/shard_map/ppermute | solution.py:156
  81.3 73.0 %collective-permute-start.3 = (bf16[128,2048]{1,0:T(8,128)(2,1)}, bf16[128,2048]{1,0:T(8,128)(2,1)}, u32[]{:S(2)}, u32[]{:S(2)}) collective-permute-start(bf16[128,2048]{1,0:T(8,128)(2,1)} %copy-done.7), channel_id=1, source_target_pairs={{0,1},{1,0},{2,3},{3,2},{4,5},{5,4},{6,7},{7,6},{8,9},{9,8},{10,11... | collective-permute-start | bytes 1572872 | tf_op jit(solution)/shard_map/ppermute | solution.py:156
  81.5 72.7 %collective-permute-start.4 = (bf16[128,2048]{1,0:T(8,128)(2,1)}, bf16[128,2048]{1,0:T(8,128)(2,1)}, u32[]{:S(2)}, u32[]{:S(2)}) collective-permute-start(bf16[128,2048]{1,0:T(8,128)(2,1)} %collective-permute-done.2.refs_1_.refs_7_), channel_id=1, source_target_pairs={{0,1},{1,0},{2,3},{3,2},{4,5},{5,4},{6,7},{7,6},{8,9},{9,8},{10,11... | collective-permute-start | bytes 1572872 | tf_op jit(solution)/shard_map/ppermute | solution.py:156
  99.5 0.8 copy-start.2
  147.3 24.4 %all-to-all-start.2 = ((bf16[32,64,128]{2,1,0:T(8,128)(2,1)}), bf16[32,64,128]{2,1,0:T(8,128)(2,1)S(1)}, u32[]{:S(2)}, u32[]{:S(2)}) async-start(bf16[32,64,128]{2,1,0:T(8,128)(2,1)} %bitcast.10), calls=%async_computation.2 | async-start | bytes 1048576 | tf_op jit(solution)/shard_map/all_to_all | solution.py:160
  171.7 0.8 copy-start

commit v2 on v1

v2 whole, which is shorter than its diff:
```python
import functools

import jax
import jax.numpy as jnp
from jax import lax
from jax.experimental import pallas as pl
from jax.experimental.pallas import tpu as pltpu
from jax.sharding import PartitionSpec as P

QH, KVH, HD = 128, 8, 128
GROUP = QH // KVH
PT, NT = 64, 16
BOTH = ("ctx", "head")
COUNT = 128
PEERS = 32
HEADS = 4
ROWS = PEERS * HEADS * NT
KVR = 80
BF, F32 = jnp.bfloat16, jnp.float32
NEG = -1e30
SCALE = HD**-0.5 * 1.4426950408889634
VM = pl.BlockSpec(memory_space=pltpu.VMEM)

GROUPS = [[(y * 4 + x) * 16 + h for y in range(2) for h in range(16)] for x in range(4)]
SIBLING = [(i, i ^ 1) for i in range(COUNT)]
OTHER_Y = [(i, i ^ 2) for i in range(COUNT)]
BACK1 = [(i, i + 4) for i in range(COUNT - 4)]
BACK2 = [(i, i + 8) for i in range(COUNT - 8)]


def along_x(d):
    return [(i, (i // 64) * 64 + (i // 16 + d) % 4 * 16 + i % 16) for i in range(COUNT)]


def params(**kw):
    return pltpu.CompilerParams(vmem_limit_bytes=56 * 2**20, **kw)


def pack(k_ref, v_ref, nk_ref, nv_ref, q_ref, out_ref):
    for j in range(KVH):
        cols = slice(j * HD, (j + 1) * HD)
        for core in range(2):
            half = slice(32 * core, 32 * core + 32)
            new = nv_ref if core else nk_ref
            for y in range(2):
                d = y * 16 + j * 2 + core
                out_ref[d, 0:32, :] = k_ref[half, cols]
                out_ref[d, 32:64, :] = v_ref[half, cols]
                out_ref[d, 64:80, :] = new[:, cols]
                for h in range(HEADS):
                    g = head_of(d, h)
                    row = KVR + h * NT
                    out_ref[d, row : row + NT, :] = q_ref[:, g * HD : (g + 1) * HD]


def head_of(d, h):
    y, j, core = d // 16, d % 16 // 2, d % 2
    return j * GROUP + (y * 2 + core) * HEADS + h


def unpack_out(blk_ref, out_ref):
    for d in range(PEERS):
        for h in range(HEADS):
            g = head_of(d, h)
            out_ref[:, g * HD : (g + 1) * HD] = blk_ref[d, h * NT : (h + 1) * NT, :]


RB, KT = 512, 512
BLOCKS = ROWS // RB
STATE = 2 * HD


def pipelined(stages, blocks, tiles, state):
    def step(t, option, fill=True, first=False):
        for r in range(blocks):
            for lag in range(stages):
                at = r - lag
                if at >= 0:
                    if fill:
                        state(lag, t, at, option)
                elif not first:
                    state(lag, t - 1, at + blocks, option)

    for n, (start, end, option) in enumerate(tiles):
        if n == 0:
            step(start, option, first=True)
            start += 1
        if end - start == 1:
            step(start, option)
        elif end > start:
            lax.fori_loop(start, end, lambda t, c, o=option: (step(t, o), c)[1], 0)
    step(tiles[-1][1], tiles[-1][2], fill=False)


def question(pieces, first, last, s_ref, *refs):
    q_ref, refs = refs[0], refs[1:]
    kv, refs = refs[: 2 * len(pieces)], refs[2 * len(pieces) :]
    if not first:
        carry, refs = refs[0], refs[1:]
    out_ref, k_s, v_s, tok_s, s_s, p_s, a_s, m_s = refs[:8]
    total = refs[8] if last else out_ref
    core, x = s_ref[0], s_ref[1]

    def token(src, t, at_x):
        return ((src // 16) * 4 + at_x) * 256 + (src % 16) * 16 + t

    old = sum(2 * peers * 32 for _, peers in pieces)
    at, fresh = 0, old
    tok_s[0] = jnp.full((8, KT), -1, jnp.int32)
    for c, (src0, peers) in enumerate(pieces):
        mine, other = kv[2 * c], kv[2 * c + 1]
        for ref in (mine, other):
            rows = slice(at, at + peers * 32)
            k_s[rows, :] = ref[:, 0:32, :].reshape(peers * 32, HD)
            v_s[rows, :HD] = ref[:, 32:64, :].reshape(peers * 32, HD)
            at += peers * 32
        keys = peers * NT
        a = mine[:, 64:80, :].reshape(keys, HD)
        b = other[:, 64:80, :].reshape(keys, HD)
        rows = slice(fresh, fresh + keys)
        k_s[rows, :] = jnp.where(core == 0, a, b)
        v_s[rows, :HD] = jnp.where(core == 0, b, a)
        col = src0 * NT + lax.broadcasted_iota(jnp.int32, (8, keys), 1)
        start = (fresh - old) % KT
        tok_s[1 + (fresh - old) // KT, :, start : start + keys] = token(
            col // 16, col % 16, s_ref[2 + c]
        )
        fresh += keys
    v_s[:, HD:] = jnp.ones((fresh, HD), BF)
    if first:
        m_s[...] = jnp.full((ROWS, HD), NEG, F32)
        total[...] = jnp.zeros((ROWS, STATE), F32)
    else:
        m_s[...] = jnp.broadcast_to(carry[:, STATE - 1 :], (ROWS, HD))
        total[...] = carry[...]
    old_tiles = old // KT
    lanes = [slice(j * HD, (j + 1) * HD) for j in range(KT // HD)]

    def keys_of(t):
        return pl.ds(t * KT if isinstance(t, int) else pl.multiple_of(t * KT, KT), KT)

    def stage(which, t, r, masked):
        slot, rows = r % 2, slice(r * RB, (r + 1) * RB)
        if which == 0:
            per = RB // (HEADS * NT)
            q = q_ref[r * per : (r + 1) * per, KVR:, :].reshape(RB, HD)
            s_s[slot] = lax.dot_general(
                q, k_s[keys_of(t), :], (((1,), (1,)), ((), ())), preferred_element_type=F32
            )
        elif which == 1:
            s = [s_s[slot, :, j] for j in lanes]
            if masked:
                row = r * RB + lax.broadcasted_iota(jnp.int32, (RB, HD), 0)
                q_tok = token(row // 64, row % 16, x)
                seen = [tok_s[t - old_tiles + 1, 0:1, j] <= q_tok for j in lanes]
                s = [jnp.where(v, a, NEG) for v, a in zip(seen, s)]
            top = jnp.max(functools.reduce(jnp.maximum, s), axis=1, keepdims=True)
            before = m_s[rows, :]
            m = jnp.maximum(before, top)
            m_s[rows, :] = m
            a_s[slot] = jnp.exp2((before - m) * SCALE)
            for j, a in zip(lanes, s):
                p_s[slot, :, j] = jnp.exp2((a - m) * SCALE).astype(BF)
        else:
            pv = jnp.dot(p_s[slot], v_s[keys_of(t), :], preferred_element_type=F32)
            a = a_s[slot]
            total[rows, :HD] = total[rows, :HD] * a + pv[:, :HD]
            total[rows, HD:] = total[rows, HD:] * a + pv[:, HD:]

    pipelined(3, BLOCKS, [(0, old_tiles, False), (old_tiles, fresh // KT, True)], stage)
    if last:
        out_ref[...] = (total[:, :HD] / total[:, HD : HD + 1]).astype(BF)
    else:
        lane = lax.broadcasted_iota(jnp.int32, (ROWS, HD), 1)
        total[:, HD:] = jnp.where(lane == HD - 1, m_s[...], total[:, HD:])


def ask(q, pieces, places, state, last):
    kinds = tuple((p[2], p[1].shape[0]) for p in pieces)
    blocks = [b for p in pieces for b in p[:2]]
    keys = sum(80 * k[1] for k in kinds)
    tiles = sum(16 * k[1] for k in kinds) // KT
    scratch = [
        pltpu.VMEM((keys, HD), BF),
        pltpu.VMEM((keys, 2 * HD), BF),
        pltpu.VMEM((1 + tiles, 8, KT), jnp.int32),
        pltpu.VMEM((2, RB, KT), F32),
        pltpu.VMEM((2, RB, KT), BF),
        pltpu.VMEM((2, RB, HD), F32),
        pltpu.VMEM((ROWS, HD), F32),
    ]
    if last:
        scratch.append(pltpu.VMEM((ROWS, STATE), F32))
    carry = [] if state is None else [state]
    return pl.pallas_call(
        functools.partial(question, kinds, state is None, last),
        out_shape=jax.ShapeDtypeStruct((ROWS, HD), BF)
        if last
        else jax.ShapeDtypeStruct((ROWS, STATE), F32),
        in_specs=[pl.BlockSpec(memory_space=pltpu.SMEM)] + [VM] * (1 + len(blocks) + len(carry)),
        out_specs=VM,
        scratch_shapes=scratch,
        compiler_params=params(),
        cost_estimate=pl.CostEstimate(
            flops=6 * ROWS * keys * HD, bytes_accessed=4 * 2**20, transcendentals=ROWS * keys
        ),
        name="question",
    )(places, q, *blocks, *carry)


PARTS, KEYS = 2, 768
PART = GROUP // PARTS


def passage(s_ref, q_ref, start_ref, *refs):
    wins, o_ref, (bias_ref, s_s, p_s) = refs[:6], refs[6], refs[7:]
    yh, core = s_ref[0], s_ref[1]
    col = lax.broadcasted_iota(jnp.int32, (PT, KEYS), 1)
    blk, t = col // 64, col % 64
    side, level, flip = blk // 6, blk % 6 // 2, blk % 2
    pos = level * 256 + (yh ^ flip) * 128 + (core ^ side) * 64 + t
    q_pos = 512 + yh * 128 + core * 64 + lax.broadcasted_iota(jnp.int32, (PT, KEYS), 0)
    bias_ref[...] = jnp.where((pos <= q_pos) & (pos >= start_ref[...]), 0.0, NEG)
    lanes = [slice(j * HD, (j + 1) * HD) for j in range(KEYS // HD)]

    def columns(j):
        return pl.ds(j * HD if isinstance(j, int) else pl.multiple_of(j * HD, HD), HD)

    def stage(which, j, part, _):
        slot = part % 2
        if which == 0:
            k = jnp.concatenate([w[:, columns(j)] for w in wins], axis=0)
            q = [q_ref[:, columns(j * GROUP + part * PART + h)] for h in range(PART)]
            s_s[slot] = lax.dot_general(
                jnp.concatenate(q, axis=0), k, (((1,), (1,)), ((), ())), preferred_element_type=F32
            )
        elif which == 1:
            for h in range(PART):
                rows = slice(h * PT, (h + 1) * PT)
                s = [s_s[slot, rows, l] + bias_ref[:, l] for l in lanes]
                m = jnp.max(functools.reduce(jnp.maximum, s), axis=1, keepdims=True)
                for l, a in zip(lanes, s):
                    p_s[slot, rows, l] = jnp.exp2((a - m) * SCALE).astype(BF)
        else:
            v = jnp.concatenate([w[:, columns(j + KVH)] for w in wins], axis=0)
            v = jnp.concatenate([v, jnp.ones_like(v)], axis=1)
            o = jnp.dot(p_s[slot], v, preferred_element_type=F32)
            o = (o[:, :HD] / o[:, HD:]).astype(BF)
            for h in range(PART):
                o_ref[:, columns(j * GROUP + part * PART + h)] = o[h * PT : (h + 1) * PT]

    pipelined(3, PARTS, [(0, KVH, None)], stage)


def passages(passage_q, start, y_hi, core, wins):
    place = jnp.stack([y_hi, core]).astype(jnp.int32)
    return pl.pallas_call(
        passage,
        out_shape=jax.ShapeDtypeStruct((PT, QH * HD), BF),
        in_specs=[pl.BlockSpec(memory_space=pltpu.SMEM)] + [VM] * 8,
        out_specs=VM,
        scratch_shapes=[
            pltpu.VMEM((PT, KEYS), F32),
            pltpu.VMEM((2, PART * PT, KEYS), F32),
            pltpu.VMEM((2, PART * PT, KEYS), BF),
        ],
        compiler_params=params(),
        cost_estimate=pl.CostEstimate(
            flops=6 * PT * QH * KEYS * HD, bytes_accessed=7 * 2**20, transcendentals=PT * QH * KEYS
        ),
        name="passage",
    )(place, passage_q, start, *wins)


def permute(block, route):
    return lax.ppermute(block, BOTH, route)


def together(*values):
    return lax.optimization_barrier(values)


def exchange(blocks):
    return lax.all_to_all(
        blocks, BOTH, split_axis=0, concat_axis=0, tiled=True, axis_index_groups=GROUPS
    )


def on_device(passage_q, passage_k, passage_v, new_q, new_k, new_v, segments):
    ctx, head = lax.axis_index("ctx"), lax.axis_index("head")
    x, core, y_hi = ctx % 4, head % 2, head // 2 % 2
    shape = jax.ShapeDtypeStruct

    blocks = pl.pallas_call(
        pack,
        out_shape=shape((PEERS, KVR + HEADS * NT, HD), BF),
        in_specs=[VM] * 5,
        out_specs=VM,
        compiler_params=params(),
        name="pack",
    )(passage_k, passage_v, new_k, new_v, new_q)
    own = jnp.concatenate([passage_k, passage_v], axis=1)
    got, other_y = together(exchange(blocks), permute(own, OTHER_Y))
    kv0 = got[:, :KVR]
    kv0_other = permute(kv0, SIBLING)
    left = permute(kv0, along_x(1))
    right = permute(kv0, along_x(3))
    level0 = jnp.concatenate([own, other_y], axis=0)
    level1 = permute(level0, BACK1)
    level2 = permute(level0, BACK2)

    places = lambda *d: jnp.stack([core, x] + [(x + i) % 4 for i in d]).astype(jnp.int32)
    state = ask(got, [(got, kv0_other, 0)], places(0), None, False)
    left, right, state = together(left, right, state)
    far = [permute(left[:16], along_x(1)), permute(right[16:], along_x(3))]
    sides = [(b, permute(b, SIBLING), 0) for b in (left, right)]
    state = ask(got, sides, places(3, 1), state, False)
    *far, level1, level2 = together(*far, level1, level2, state)[:4]
    far = [(b, permute(b, SIBLING), 16 * i) for i, b in enumerate(far)]
    wins = [level2, level1, level0]
    wins += [permute(w, SIBLING) for w in wins]
    out_rows = ask(got, far, places(2, 2), state, True)
    new_blocks = exchange(out_rows.reshape(PEERS, HEADS * NT, HD))
    new_out = pl.pallas_call(
        unpack_out,
        out_shape=shape((NT, QH * HD), BF),
        in_specs=[VM],
        out_specs=VM,
        compiler_params=params(),
        name="unpack_out",
    )(new_blocks)

    flat = ctx * 16 + head
    padded = jnp.concatenate([jnp.full((512,), -1, jnp.int32), segments])
    near = lax.dynamic_slice_in_dim(padded, flat // 4 * 256, 768, 0)
    seg_q = lax.dynamic_slice_in_dim(segments, flat * PT, PT, 0)
    start = jnp.sum((near[None, :] < seg_q[:, None]).astype(jnp.int32), axis=1, keepdims=True)
    pass_out = passages(passage_q, start, y_hi, core, wins)
    return pass_out, new_out


def solution(mesh):
    row = P(BOTH, None)
    return jax.shard_map(
        on_device,
        mesh=mesh,
        in_specs=(row,) * 6 + (P(),),
        out_specs=(row, row),
        check_vma=False,
    )
```

time: 175 us -> 140 us (0.80)
  waiting for transfers between devices: 52.4 us -> 21.4 us
  Pallas kernels: 70.2 us -> 64.4 us
  starting transfers between devices: 46.1 us -> 44 us
  local copies, waits for them, and re-layouts: 4.05 us -> 6 us
  other arithmetic: 0.83 us -> 2.74 us
    all_to_all x3 -> x2, waiting for transfers between devices: 27.9 us -> 0.01 us  [exchange(): lax.all_to_all(blocks, BOTH, split_axis=0, concat_axis=0, tiled=True, axi...]
    all_to_all x3 -> x2, starting transfers between devices: 30.5 us -> 22.7 us  [exchange(): lax.all_to_all(blocks, BOTH, split_axis=0, concat_axis=0, tiled=True, axi...]
    ppermute x13 -> x15, starting transfers between devices: 15.6 us -> 21.3 us  [permute(): return lax.ppermute(block, BOTH, route)]
    pallas_call x4 -> x5, Pallas kernels: 68.2 us -> 62.5 us  [the longest x3 44.8 us: ask(): pl.pallas_call(functools.partial(question, kinds, state is None, last), o...]
    ppermute x13 -> x15, waiting for transfers between devices: 24.6 us -> 21.4 us  [permute(): return lax.ppermute(block, BOTH, route)]
    another operation x1 -> x4, other arithmetic: 0.65 us -> 2.51 us  [the longest x3 1.92 us: on_device(): jnp.stack([core, x] + [(x + i) % 4 for i in d]).astype(jnp.int32)]
    unnamed x17 -> x29, local copies, waits for them, and re-layouts: 2.59 us -> 4.07 us
  transfers between devices with their start and end apart: 16 -> 17, of which waited for: 4 -> 2; matrix products, arithmetic and copies ran while one was open for 2% -> 3% of each run, Pallas kernels for 38% -> 43%
where the time goes in v2:
time: 140 us; the launch traced here: 139 us
  Pallas kernels  64.4 us (46%)
  starting transfers between devices  44 us (31%)
  waiting for transfers between devices  21.4 us (15%)
  local copies, waits for them, and re-layouts  6 us (4%)
  other arithmetic  2.74 us (2%)
    pallas_call x3, Pallas kernels, ask(): pl.pallas_call(functools.partial(question, kinds, state is None, last), o...  44.8 us
    all_to_all x2, starting transfers between devices, exchange(): lax.all_to_all(blocks, BOTH, split_axis=0, concat_axis=0, tiled=True, axi...  22.7 us
    ppermute x15, waiting for transfers between devices, permute(): return lax.ppermute(block, BOTH, route)  21.4 us
    ppermute x15, starting transfers between devices, permute(): return lax.ppermute(block, BOTH, route)  21.3 us
    pallas_call x1, Pallas kernels, passages(): pl.pallas_call(passage, out_shape=jax.ShapeDtypeStruct((PT, QH * HD), BF)...  15.3 us
    unnamed x29, local copies, waits for them, and re-layouts  4.07 us
  transfers between devices with their start and end apart: 17, of which 2 were waited for; matrix products, arithmetic and copies ran while one was open for 3% of the time, Pallas kernels for 43%

profile of v2, /device:TPU:1, one launch (start us, length us, event | category | flops | bytes accessed | tf_op | source)
XLA Modules:
  0.0 139.4 jit_solution(2666000166838308300)
XLA Ops:
  0.7 2.4 %pack.1 = bf16[32,144,128]{2,1,0:T(8,128)(2,1)} custom-call(bf16[64,1024]{1,0:T(8,128)(2,1)} %k_ref.1, bf16[64,1024]{1,0:T(8,128)(2,1)} %v_ref.1, bf16[16,1024]{1,0:T(8,128)(2,1)} %nk_ref.1, bf16[16,1024]{1,0:T(8,128)(2,1)} %nv_ref.1, bf16[16,16384]{1,0:T(8,128)(2,1)} %q_ref.2), custom_call_target="tpu_custom_call" | custom-call | tf_op jit(solution)/shard_map/pack/pallas_call | solution.py:294
  3.1 9.6 %all-to-all-start = ((bf16[32,144,128]{2,1,0:T(8,128)(2,1)}), bf16[32,144,128]{2,1,0:T(8,128)(2,1)S(1)}, u32[]{:S(2)}, u32[]{:S(2)}) async-start(bf16[32,144,128]{2,1,0:T(8,128)(2,1)} %pack.1), calls=%async_computation | async-start | bytes 2359296 | tf_op jit(solution)/shard_map/all_to_all | solution.py:284
  12.8 3.0 %collective-permute-start = (bf16[64,2048]{1,0:T(8,128)(2,1)S(1)}, bf16[64,2048]{1,0:T(8,128)(2,1)S(1)}, u32[]{:S(2)}, u32[]{:S(2)}) collective-permute-start(bf16[64,2048]{1,0:T(8,128)(2,1)S(1)} %constant_dynamic-update-slice_fusion), channel_id=1, source_target_pairs={{0,2},{1,3},{2,0},{3,1},{4,6},{5,7},{6,4},{7,5},{8,10},{9,11},{10,... | collective-permute-start | bytes 786440 | tf_op jit(solution)/shard_map/ppermute | solution.py:276
  15.7 19.0 %collective-permute-done = bf16[64,2048]{1,0:T(8,128)(2,1)S(1)} collective-permute-done((bf16[64,2048]{1,0:T(8,128)(2,1)S(1)}, bf16[64,2048]{1,0:T(8,128)(2,1)S(1)}, u32[]{:S(2)}, u32[]{:S(2)}) %collective-permute-start) | collective-permute-done | bytes 262176 | tf_op jit(solution)/shard_map/ppermute | solution.py:276
  34.7 0.0 all-to-all-done.refs_0_.refs_1_
  34.8 1.0 collective-permute-start.3
  35.7 1.2 collective-permute-start.1
  36.9 1.5 %collective-permute-start.2 = (bf16[32,80,128]{2,1,0:T(8,128)(2,1)S(1)}, bf16[32,80,128]{2,1,0:T(8,128)(2,1)}, u32[]{:S(2)}, u32[]{:S(2)}) collective-permute-start(bf16[32,80,128]{2,1,0:T(8,128)(2,1)S(1)} %slice.9), channel_id=1, source_target_pairs={{0,48},{1,49},{2,50},{3,51},{4,52},{5,53},{6,54},{7,55},{8,56},{9,... | collective-permute-start | bytes 1966088 | tf_op jit(solution)/shard_map/ppermute | solution.py:276
  38.4 0.6 pad_add_fusion.1.s_ref
  39.0 0.0 collective-permute-done.3.refs_2_
  39.0 11.9 %question.3.refs_5_ = f32[2048,256]{1,0:T(8,128)} custom-call(s32[3]{0:T(128)} %pad_add_fusion.1.s_ref, bf16[32,144,128]{2,1,0:T(8,128)(2,1)} %copy-done, bf16[32,144,128]{2,1,0:T(8,128)(2,1)} %copy-done, bf16[32,80,128]{2,1,0:T(8,128)(2,1)} %collective-permute-done.3.refs_2_), custom_call_target="tpu_custom_call" | custom-call | flops 4026531840 | bytes 4194304 | tf_op jit(solution)/shard_map/question/pallas_call | solution.py:195
  50.9 2.3 %collective-permute-done.1.refs_1_ = bf16[32,80,128]{2,1,0:T(8,128)(2,1)S(1)} collective-permute-done((bf16[32,80,128]{2,1,0:T(8,128)(2,1)S(1)}, bf16[32,80,128]{2,1,0:T(8,128)(2,1)S(1)}, u32[]{:S(2)}, u32[]{:S(2)}) %collective-permute-start.1) | collective-permute-done | bytes 655392 | tf_op jit(solution)/shard_map/ppermute | solution.py:276
  53.2 1.0 collective-permute-start.8
  54.2 0.0 collective-permute-start.9
  54.2 0.1 dynamic_slice.7
  54.3 0.7 pad_add_fusion.2.s_ref
  55.0 3.1 %collective-permute-start.6 = (bf16[128,2048]{1,0:T(8,128)(2,1)S(1)}, bf16[128,2048]{1,0:T(8,128)(2,1)S(1)}, u32[]{:S(2)}, u32[]{:S(2)}) collective-permute-start(bf16[128,2048]{1,0:T(8,128)(2,1)S(1)} %pad_maximum_fusion.refs_2_), channel_id=1, source_target_pairs={{0,4},{1,5},{2,6},{3,7},{4,8},{5,9},{6,10},{7,11},{8,12},{9,13},{1... | collective-permute-start | bytes 1572872 | tf_op jit(solution)/shard_map/ppermute | solution.py:276
  58.1 5.1 %collective-permute-start.7 = (bf16[128,2048]{1,0:T(8,128)(2,1)S(1)}, bf16[128,2048]{1,0:T(8,128)(2,1)}, u32[]{:S(2)}, u32[]{:S(2)}) collective-permute-start(bf16[128,2048]{1,0:T(8,128)(2,1)S(1)} %pad_maximum_fusion.refs_2_), channel_id=1, source_target_pairs={{0,8},{1,9},{2,10},{3,11},{4,12},{5,13},{6,14},{7,15},{8,16},{9,17... | collective-permute-start | bytes 1572872 | tf_op jit(solution)/shard_map/ppermute | solution.py:276
  63.2 1.0 slice.11
  64.2 0.5 collective-permute-start.4
  64.7 2.3 %collective-permute-start.5 = (bf16[16,80,128]{2,1,0:T(8,128)(2,1)S(1)}, bf16[16,80,128]{2,1,0:T(8,128)(2,1)}, u32[]{:S(2)}, u32[]{:S(2)}) collective-permute-start(bf16[16,80,128]{2,1,0:T(8,128)(2,1)S(1)} %slice.11), channel_id=1, source_target_pairs={{0,48},{1,49},{2,50},{3,51},{4,52},{5,53},{6,54},{7,55},{8,56},{9,... | collective-permute-start | bytes 983048 | tf_op jit(solution)/shard_map/ppermute | solution.py:276
  67.0 0.0 collective-permute-done.9.refs_4_
  67.0 21.0 %question.4.refs_5_ = f32[2048,256]{1,0:T(8,128)} custom-call(s32[4]{0:T(128)} %pad_add_fusion.2.s_ref, bf16[32,144,128]{2,1,0:T(8,128)(2,1)} %copy-done, bf16[32,80,128]{2,1,0:T(8,128)(2,1)} %copy-done.5, bf16[32,80,128]{2,1,0:T(8,128)(2,1)} %copy-done.7, bf16[32,80,128]{2,1,0:T(8,128)(2,1)} %collective-permute-done.2.refs_3_, ...), custom_call_target="tpu_custom_call" | custom-call | flops 8053063680 | bytes 4194304 | tf_op jit(solution)/shard_map/question/pallas_call | solution.py:195
  88.0 0.0 collective-permute-done.6.refs_1_
  88.0 0.0 collective-permute-done.4.refs_1_
  88.0 0.0 collective-permute-done.5.refs_3_
  88.0 1.7 %collective-permute-start.13 = (bf16[16,80,128]{2,1,0:T(8,128)(2,1)}, bf16[16,80,128]{2,1,0:T(8,128)(2,1)S(1)}, u32[]{:S(2)}, u32[]{:S(2)}) collective-permute-start(bf16[16,80,128]{2,1,0:T(8,128)(2,1)} %collective-permute-done.4.refs_1_), channel_id=1, source_target_pairs={{0,1},{1,0},{2,3},{3,2},{4,5},{5,4},{6,7},{7,6},{8,9},{9,8},{10,11... | collective-permute-start | bytes 983048 | tf_op jit(solution)/shard_map/ppermute | solution.py:276
  89.7 0.1 collective-permute-start.14
  89.8 0.1 pad_dynamic-slice_fusion
  89.9 0.2 convert_reduce_fusion
  90.1 0.5 collective-permute-start.12
  90.6 0.1 collective-permute-start.10
  90.7 0.4 collective-permute-start.11
  91.1 0.7 pad_add_fusion.4.s_ref
  91.8 0.0 collective-permute-done.13.refs_2_
  91.8 0.7 copy-done.12
  92.5 0.7 copy-done.13
  93.2 11.9 %question.5 = bf16[2048,128]{1,0:T(8,128)(2,1)} custom-call(s32[4]{0:T(128)} %pad_add_fusion.4.s_ref, bf16[32,144,128]{2,1,0:T(8,128)(2,1)} %copy-done, bf16[16,80,128]{2,1,0:T(8,128)(2,1)} %collective-permute-done.4.refs_1_, bf16[16,80,128]{2,1,0:T(8,128)(2,1)} %copy-done.12, bf16[16,80,128]{2,1,0:T(8,128)(2,1)} %collective-permute-done.5.refs_3_, ...), custom_call_target="tpu_custom_call" | custom-call | flops 4026531840 | bytes 4194304 | tf_op jit(solution)/shard_map/question/pallas_call | solution.py:195
  105.1 13.1 %all-to-all-start.1 = ((bf16[32,64,128]{2,1,0:T(8,128)(2,1)}), bf16[32,64,128]{2,1,0:T(8,128)(2,1)S(1)}, u32[]{:S(2)}, u32[]{:S(2)}) async-start(bf16[32,64,128]{2,1,0:T(8,128)(2,1)} %bitcast.9), calls=%async_computation.1 | async-start | bytes 1048576 | tf_op jit(solution)/shard_map/all_to_all | solution.py:284
  118.2 0.6 pad_add_fusion.s_ref
  118.8 0.7 copy.10.start_ref
  119.5 0.0 collective-permute-done.12.refs_5_
  119.6 0.8 copy-done.9
  120.4 0.2 copy-done.10
  120.5 0.8 copy-done.11
  121.3 15.3 %passage.1 = bf16[64,16384]{1,0:T(8,128)(2,1)} custom-call(s32[2]{0:T(128)} %pad_add_fusion.s_ref, bf16[64,16384]{1,0:T(8,128)(2,1)} %q_ref.3, s32[64,1]{1,0:T(8,128)} %copy.10.start_ref, bf16[128,2048]{1,0:T(8,128)(2,1)} %collective-permute-done.7.refs_0_, bf16[128,2048]{1,0:T(8,128)(2,1)} %copy-done.8, bf16[128,2048]{1,0:T(8,128)(2,1)} %copy-done.4, ...), custom_call_target="tpu_custom_call" | custom-call | flops 4831838208 | bytes 7340032 | tf_op jit(solution)/shard_map/passage/pallas_call | solution.py:257
  136.6 0.8 copy-done.1
  137.4 1.9 %unpack_out.1 = bf16[16,16384]{1,0:T(8,128)(2,1)} custom-call(bf16[32,64,128]{2,1,0:T(8,128)(2,1)} %copy-done.1), custom_call_target="tpu_custom_call" | custom-call | tf_op jit(solution)/shard_map/unpack_out/pallas_call | solution.py:324
  (34 shorter events, 0.2 us)
Async XLA Ops:
  0.6 12.1 %copy-start.2 = (bf16[64,1024]{1,0:T(8,128)(2,1)S(1)}, bf16[64,1024]{1,0:T(8,128)(2,1)}, u32[]{:S(2)}) copy-start(bf16[64,1024]{1,0:T(8,128)(2,1)} %k_ref.1) | copy-start | bytes 393220
  0.6 12.1 %copy-start.3 = (bf16[64,1024]{1,0:T(8,128)(2,1)S(1)}, bf16[64,1024]{1,0:T(8,128)(2,1)}, u32[]{:S(2)}) copy-start(bf16[64,1024]{1,0:T(8,128)(2,1)} %v_ref.1) | copy-start | bytes 393220
  3.1 31.6 %all-to-all-start = ((bf16[32,144,128]{2,1,0:T(8,128)(2,1)}), bf16[32,144,128]{2,1,0:T(8,128)(2,1)S(1)}, u32[]{:S(2)}, u32[]{:S(2)}) async-start(bf16[32,144,128]{2,1,0:T(8,128)(2,1)} %pack.1), calls=%async_computation | async-start | bytes 2359296 | tf_op jit(solution)/shard_map/all_to_all | solution.py:284
  12.8 22.0 %collective-permute-start = (bf16[64,2048]{1,0:T(8,128)(2,1)S(1)}, bf16[64,2048]{1,0:T(8,128)(2,1)S(1)}, u32[]{:S(2)}, u32[]{:S(2)}) collective-permute-start(bf16[64,2048]{1,0:T(8,128)(2,1)S(1)} %constant_dynamic-update-slice_fusion), channel_id=1, source_target_pairs={{0,2},{1,3},{2,0},{3,1},{4,6},{5,7},{6,4},{7,5},{8,10},{9,11},{10,... | collective-permute-start | bytes 786440 | tf_op jit(solution)/shard_map/ppermute | solution.py:276
  34.7 4.3 %copy-start = (bf16[32,144,128]{2,1,0:T(8,128)(2,1)}, bf16[32,144,128]{2,1,0:T(8,128)(2,1)S(1)}, u32[]{:S(2)}) copy-start(bf16[32,144,128]{2,1,0:T(8,128)(2,1)S(1)} %all-to-all-done.refs_0_.refs_1_) | copy-start | bytes 3538948
  34.8 4.3 %collective-permute-start.3 = (bf16[32,80,128]{2,1,0:T(8,128)(2,1)S(1)}, bf16[32,80,128]{2,1,0:T(8,128)(2,1)}, u32[]{:S(2)}, u32[]{:S(2)}) collective-permute-start(bf16[32,80,128]{2,1,0:T(8,128)(2,1)S(1)} %slice.9), channel_id=1, source_target_pairs={{0,1},{1,0},{2,3},{3,2},{4,5},{5,4},{6,7},{7,6},{8,9},{9,8},{10,11... | collective-permute-start | bytes 1966088 | tf_op jit(solution)/shard_map/ppermute | solution.py:276
  35.7 17.5 %collective-permute-start.1 = (bf16[32,80,128]{2,1,0:T(8,128)(2,1)S(1)}, bf16[32,80,128]{2,1,0:T(8,128)(2,1)S(1)}, u32[]{:S(2)}, u32[]{:S(2)}) collective-permute-start(bf16[32,80,128]{2,1,0:T(8,128)(2,1)S(1)} %slice.9), channel_id=1, source_target_pairs={{0,16},{1,17},{2,18},{3,19},{4,20},{5,21},{6,22},{7,23},{8,24},{9,... | collective-permute-start | bytes 1966088 | tf_op jit(solution)/shard_map/ppermute | solution.py:276
  36.9 16.3 %collective-permute-start.2 = (bf16[32,80,128]{2,1,0:T(8,128)(2,1)S(1)}, bf16[32,80,128]{2,1,0:T(8,128)(2,1)}, u32[]{:S(2)}, u32[]{:S(2)}) collective-permute-start(bf16[32,80,128]{2,1,0:T(8,128)(2,1)S(1)} %slice.9), channel_id=1, source_target_pairs={{0,48},{1,49},{2,50},{3,51},{4,52},{5,53},{6,54},{7,55},{8,56},{9,... | collective-permute-start | bytes 1966088 | tf_op jit(solution)/shard_map/ppermute | solution.py:276
  39.0 15.2 %copy-start.6 = (s32[8192]{0:T(1024)S(1)}, s32[8192]{0:T(1024)}, u32[]{:S(2)}) copy-start(s32[8192]{0:T(1024)} %param.13) | copy-start | bytes 98308
  53.2 13.8 %copy-start.5 = (bf16[32,80,128]{2,1,0:T(8,128)(2,1)}, bf16[32,80,128]{2,1,0:T(8,128)(2,1)S(1)}, u32[]{:S(2)}) copy-start(bf16[32,80,128]{2,1,0:T(8,128)(2,1)S(1)} %collective-permute-done.1.refs_1_) | copy-start | bytes 1966084
  53.2 11.5 %collective-permute-start.8 = (bf16[32,80,128]{2,1,0:T(8,128)(2,1)S(1)}, bf16[32,80,128]{2,1,0:T(8,128)(2,1)S(1)}, u32[]{:S(2)}, u32[]{:S(2)}) collective-permute-start(bf16[32,80,128]{2,1,0:T(8,128)(2,1)S(1)} %collective-permute-done.1.refs_1_), channel_id=1, source_target_pairs={{0,1},{1,0},{2,3},{3,2},{4,5},{5,4},{6,7},{7,6},{8,9},{9,8},{10,11... | collective-permute-start | bytes 1966088 | tf_op jit(solution)/shard_map/ppermute | solution.py:276
  54.2 12.8 %collective-permute-start.9 = (bf16[32,80,128]{2,1,0:T(8,128)(2,1)}, bf16[32,80,128]{2,1,0:T(8,128)(2,1)}, u32[]{:S(2)}, u32[]{:S(2)}) collective-permute-start(bf16[32,80,128]{2,1,0:T(8,128)(2,1)} %collective-permute-done.2.refs_3_), channel_id=1, source_target_pairs={{0,1},{1,0},{2,3},{3,2},{4,5},{5,4},{6,7},{7,6},{8,9},{9,8},{10,11... | collective-permute-start | bytes 1966088 | tf_op jit(solution)/shard_map/ppermute | solution.py:276
  55.0 35.1 %copy-start.4 = (bf16[128,2048]{1,0:T(8,128)(2,1)}, bf16[128,2048]{1,0:T(8,128)(2,1)S(1)}, u32[]{:S(2)}) copy-start(bf16[128,2048]{1,0:T(8,128)(2,1)S(1)} %pad_maximum_fusion.refs_2_) | copy-start | bytes 1572868
  55.0 33.0 %collective-permute-start.6 = (bf16[128,2048]{1,0:T(8,128)(2,1)S(1)}, bf16[128,2048]{1,0:T(8,128)(2,1)S(1)}, u32[]{:S(2)}, u32[]{:S(2)}) collective-permute-start(bf16[128,2048]{1,0:T(8,128)(2,1)S(1)} %pad_maximum_fusion.refs_2_), channel_id=1, source_target_pairs={{0,4},{1,5},{2,6},{3,7},{4,8},{5,9},{6,10},{7,11},{8,12},{9,13},{1... | collective-permute-start | bytes 1572872 | tf_op jit(solution)/shard_map/ppermute | solution.py:276
  58.1 29.9 %collective-permute-start.7 = (bf16[128,2048]{1,0:T(8,128)(2,1)S(1)}, bf16[128,2048]{1,0:T(8,128)(2,1)}, u32[]{:S(2)}, u32[]{:S(2)}) collective-permute-start(bf16[128,2048]{1,0:T(8,128)(2,1)S(1)} %pad_maximum_fusion.refs_2_), channel_id=1, source_target_pairs={{0,8},{1,9},{2,10},{3,11},{4,12},{5,13},{6,14},{7,15},{8,16},{9,17... | collective-permute-start | bytes 1572872 | tf_op jit(solution)/shard_map/ppermute | solution.py:276
  64.2 23.8 %collective-permute-start.4 = (bf16[16,80,128]{2,1,0:T(8,128)(2,1)S(1)}, bf16[16,80,128]{2,1,0:T(8,128)(2,1)}, u32[]{:S(2)}, u32[]{:S(2)}) collective-permute-start(bf16[16,80,128]{2,1,0:T(8,128)(2,1)S(1)} %slice.10), channel_id=1, source_target_pairs={{0,16},{1,17},{2,18},{3,19},{4,20},{5,21},{6,22},{7,23},{8,24},{9,... | collective-permute-start | bytes 983048 | tf_op jit(solution)/shard_map/ppermute | solution.py:276
  64.7 2.3 %copy-start.7 = (bf16[32,80,128]{2,1,0:T(8,128)(2,1)}, bf16[32,80,128]{2,1,0:T(8,128)(2,1)S(1)}, u32[]{:S(2)}) copy-start(bf16[32,80,128]{2,1,0:T(8,128)(2,1)S(1)} %collective-permute-done.8.refs_2_) | copy-start | bytes 1966084
  64.7 23.3 %collective-permute-start.5 = (bf16[16,80,128]{2,1,0:T(8,128)(2,1)S(1)}, bf16[16,80,128]{2,1,0:T(8,128)(2,1)}, u32[]{:S(2)}, u32[]{:S(2)}) collective-permute-start(bf16[16,80,128]{2,1,0:T(8,128)(2,1)S(1)} %slice.11), channel_id=1, source_target_pairs={{0,48},{1,49},{2,50},{3,51},{4,52},{5,53},{6,54},{7,55},{8,56},{9,... | collective-permute-start | bytes 983048 | tf_op jit(solution)/shard_map/ppermute | solution.py:276
  88.0 17.1 %copy-start.8 = (bf16[128,2048]{1,0:T(8,128)(2,1)}, bf16[128,2048]{1,0:T(8,128)(2,1)S(1)}, u32[]{:S(2)}) copy-start(bf16[128,2048]{1,0:T(8,128)(2,1)S(1)} %collective-permute-done.6.refs_1_) | copy-start | bytes 1572868
  88.0 3.7 %collective-permute-start.13 = (bf16[16,80,128]{2,1,0:T(8,128)(2,1)}, bf16[16,80,128]{2,1,0:T(8,128)(2,1)S(1)}, u32[]{:S(2)}, u32[]{:S(2)}) collective-permute-start(bf16[16,80,128]{2,1,0:T(8,128)(2,1)} %collective-permute-done.4.refs_1_), channel_id=1, source_target_pairs={{0,1},{1,0},{2,3},{3,2},{4,5},{5,4},{6,7},{7,6},{8,9},{9,8},{10,11... | collective-permute-start | bytes 983048 | tf_op jit(solution)/shard_map/ppermute | solution.py:276
  89.7 2.0 %collective-permute-start.14 = (bf16[16,80,128]{2,1,0:T(8,128)(2,1)}, bf16[16,80,128]{2,1,0:T(8,128)(2,1)S(1)}, u32[]{:S(2)}, u32[]{:S(2)}) collective-permute-start(bf16[16,80,128]{2,1,0:T(8,128)(2,1)} %collective-permute-done.5.refs_3_), channel_id=1, source_target_pairs={{0,1},{1,0},{2,3},{3,2},{4,5},{5,4},{6,7},{7,6},{8,9},{9,8},{10,11... | collective-permute-start | bytes 983048 | tf_op jit(solution)/shard_map/ppermute | solution.py:276
  90.1 29.5 %collective-permute-start.12 = (bf16[128,2048]{1,0:T(8,128)(2,1)S(1)}, bf16[128,2048]{1,0:T(8,128)(2,1)S(1)}, u32[]{:S(2)}, u32[]{:S(2)}) collective-permute-start(bf16[128,2048]{1,0:T(8,128)(2,1)S(1)} %pad_maximum_fusion.refs_2_), channel_id=1, source_target_pairs={{0,1},{1,0},{2,3},{3,2},{4,5},{5,4},{6,7},{7,6},{8,9},{9,8},{10,11... | collective-permute-start | bytes 1572872 | tf_op jit(solution)/shard_map/ppermute | solution.py:276
  90.6 29.0 %collective-permute-start.10 = (bf16[128,2048]{1,0:T(8,128)(2,1)}, bf16[128,2048]{1,0:T(8,128)(2,1)S(1)}, u32[]{:S(2)}, u32[]{:S(2)}) collective-permute-start(bf16[128,2048]{1,0:T(8,128)(2,1)} %collective-permute-done.7.refs_0_), channel_id=1, source_target_pairs={{0,1},{1,0},{2,3},{3,2},{4,5},{5,4},{6,7},{7,6},{8,9},{9,8},{10,11... | collective-permute-start | bytes 1572872 | tf_op jit(solution)/shard_map/ppermute | solution.py:276
  90.7 28.9 %collective-permute-start.11 = (bf16[128,2048]{1,0:T(8,128)(2,1)S(1)}, bf16[128,2048]{1,0:T(8,128)(2,1)S(1)}, u32[]{:S(2)}, u32[]{:S(2)}) collective-permute-start(bf16[128,2048]{1,0:T(8,128)(2,1)S(1)} %collective-permute-done.6.refs_1_), channel_id=1, source_target_pairs={{0,1},{1,0},{2,3},{3,2},{4,5},{5,4},{6,7},{7,6},{8,9},{9,8},{10,11... | collective-permute-start | bytes 1572872 | tf_op jit(solution)/shard_map/ppermute | solution.py:276
  91.8 0.7 copy-start.12
  92.5 0.7 copy-start.13
  105.1 31.5 %all-to-all-start.1 = ((bf16[32,64,128]{2,1,0:T(8,128)(2,1)}), bf16[32,64,128]{2,1,0:T(8,128)(2,1)S(1)}, u32[]{:S(2)}, u32[]{:S(2)}) async-start(bf16[32,64,128]{2,1,0:T(8,128)(2,1)} %bitcast.9), calls=%async_computation.1 | async-start | bytes 1048576 | tf_op jit(solution)/shard_map/all_to_all | solution.py:284
  119.5 0.8 copy-start.9
  119.6 1.0 copy-start.10
  120.5 0.8 copy-start.11
  136.6 0.8 copy-start.1

commit v3 on v2

--- a/solution.py
+++ b/solution.py
@@ -36,7 +36,7 @@
     return pltpu.CompilerParams(vmem_limit_bytes=56 * 2**20, **kw)
 
 
-def pack(k_ref, v_ref, nk_ref, nv_ref, q_ref, out_ref):
+def pack_kv(k_ref, v_ref, nk_ref, nv_ref, out_ref):
     for j in range(KVH):
         cols = slice(j * HD, (j + 1) * HD)
         for core in range(2):
@@ -47,15 +47,18 @@
                 out_ref[d, 0:32, :] = k_ref[half, cols]
                 out_ref[d, 32:64, :] = v_ref[half, cols]
                 out_ref[d, 64:80, :] = new[:, cols]
-                for h in range(HEADS):
-                    g = head_of(d, h)
-                    row = KVR + h * NT
-                    out_ref[d, row : row + NT, :] = q_ref[:, g * HD : (g + 1) * HD]
 
 
 def head_of(d, h):
     y, j, core = d // 16, d % 16 // 2, d % 2
     return j * GROUP + (y * 2 + core) * HEADS + h
+
+
+def pack_q(q_ref, out_ref):
+    for d in range(PEERS):
+        for h in range(HEADS):
+            g = head_of(d, h)
+            out_ref[d, h * NT : (h + 1) * NT, :] = q_ref[:, g * HD : (g + 1) * HD]
 
 
 def unpack_out(blk_ref, out_ref):
@@ -92,22 +95,22 @@
     step(tiles[-1][1], tiles[-1][2], fill=False)
 
 
-def question(pieces, first, last, s_ref, *refs):
+def question(pieces, first, last, *refs):
     q_ref, refs = refs[0], refs[1:]
     kv, refs = refs[: 2 * len(pieces)], refs[2 * len(pieces) :]
     if not first:
         carry, refs = refs[0], refs[1:]
     out_ref, k_s, v_s, tok_s, s_s, p_s, a_s, m_s = refs[:8]
     total = refs[8] if last else out_ref
-    core, x = s_ref[0], s_ref[1]
+    core, x = lax.axis_index("head") % 2, lax.axis_index("ctx") % 4
 
     def token(src, t, at_x):
         return ((src // 16) * 4 + at_x) * 256 + (src % 16) * 16 + t
 
-    old = sum(2 * peers * 32 for _, peers in pieces)
+    old = sum(2 * peers * 32 for _, peers, _ in pieces)
     at, fresh = 0, old
     tok_s[0] = jnp.full((8, KT), -1, jnp.int32)
-    for c, (src0, peers) in enumerate(pieces):
+    for c, (src0, peers, away) in enumerate(pieces):
         mine, other = kv[2 * c], kv[2 * c + 1]
         for ref in (mine, other):
             rows = slice(at, at + peers * 32)
@@ -123,7 +126,7 @@
         col = src0 * NT + lax.broadcasted_iota(jnp.int32, (8, keys), 1)
         start = (fresh - old) % KT
         tok_s[1 + (fresh - old) // KT, :, start : start + keys] = token(
-            col // 16, col % 16, s_ref[2 + c]
+            col // 16, col % 16, (x + away) % 4
         )
         fresh += keys
     v_s[:, HD:] = jnp.ones((fresh, HD), BF)
@@ -143,7 +146,7 @@
         slot, rows = r % 2, slice(r * RB, (r + 1) * RB)
         if which == 0:
             per = RB // (HEADS * NT)
-            q = q_ref[r * per : (r + 1) * per, KVR:, :].reshape(RB, HD)
+            q = q_ref[r * per : (r + 1) * per].reshape(RB, HD)
             s_s[slot] = lax.dot_general(
                 q, k_s[keys_of(t), :], (((1,), (1,)), ((), ())), preferred_element_type=F32
             )
@@ -175,8 +178,8 @@
         total[:, HD:] = jnp.where(lane == HD - 1, m_s[...], total[:, HD:])
 
 
-def ask(q, pieces, places, state, last):
-    kinds = tuple((p[2], p[1].shape[0]) for p in pieces)
+def ask(q, pieces, state, last):
+    kinds = tuple((p[2], p[1].shape[0], p[3]) for p in pieces)
     blocks = [b for p in pieces for b in p[:2]]
     keys = sum(80 * k[1] for k in kinds)
     tiles = sum(16 * k[1] for k in kinds) // KT
@@ -197,7 +200,7 @@
         out_shape=jax.ShapeDtypeStruct((ROWS, HD), BF)
         if last
         else jax.ShapeDtypeStruct((ROWS, STATE), F32),
-        in_specs=[pl.BlockSpec(memory_space=pltpu.SMEM)] + [VM] * (1 + len(blocks) + len(carry)),
+        in_specs=[VM] * (1 + len(blocks) + len(carry)),
         out_specs=VM,
         scratch_shapes=scratch,
         compiler_params=params(),
@@ -205,20 +208,20 @@
             flops=6 * ROWS * keys * HD, bytes_accessed=4 * 2**20, transcendentals=ROWS * keys
         ),
         name="question",
-    )(places, q, *blocks, *carry)
-
-
-PARTS, KEYS = 2, 768
+    )(q, *blocks, *carry)
+
+
+PARTS, KEYS = 2, 640
 PART = GROUP // PARTS
 
 
-def passage(s_ref, q_ref, start_ref, *refs):
-    wins, o_ref, (bias_ref, s_s, p_s) = refs[:6], refs[6], refs[7:]
-    yh, core = s_ref[0], s_ref[1]
+def passage(q_ref, start_ref, *refs):
+    wins, o_ref, (bias_ref, s_s, p_s) = refs[:4], refs[4], refs[5:]
+    yh, core = lax.axis_index("head") // 2 % 2, lax.axis_index("head") % 2
     col = lax.broadcasted_iota(jnp.int32, (PT, KEYS), 1)
-    blk, t = col // 64, col % 64
-    side, level, flip = blk // 6, blk % 6 // 2, blk % 2
-    pos = level * 256 + (yh ^ flip) * 128 + (core ^ side) * 64 + t
+    side, blk, t = col // 320, col // 64 % 5, col % 64
+    level = jnp.where(blk < 3, 2 - blk, jnp.where(blk == 3, 1, 2 * yh))
+    pos = level * 256 + (yh ^ (blk // 3)) * 128 + (core ^ side) * 64 + t
     q_pos = 512 + yh * 128 + core * 64 + lax.broadcasted_iota(jnp.int32, (PT, KEYS), 0)
     bias_ref[...] = jnp.where((pos <= q_pos) & (pos >= start_ref[...]), 0.0, NEG)
     lanes = [slice(j * HD, (j + 1) * HD) for j in range(KEYS // HD)]
@@ -252,12 +255,11 @@
     pipelined(3, PARTS, [(0, KVH, None)], stage)
 
 
-def passages(passage_q, start, y_hi, core, wins):
-    place = jnp.stack([y_hi, core]).astype(jnp.int32)
+def passages(passage_q, start, wins):
     return pl.pallas_call(
         passage,
         out_shape=jax.ShapeDtypeStruct((PT, QH * HD), BF),
-        in_specs=[pl.BlockSpec(memory_space=pltpu.SMEM)] + [VM] * 8,
+        in_specs=[VM] * 6,
         out_specs=VM,
         scratch_shapes=[
             pltpu.VMEM((PT, KEYS), F32),
@@ -269,7 +271,7 @@
             flops=6 * PT * QH * KEYS * HD, bytes_accessed=7 * 2**20, transcendentals=PT * QH * KEYS
         ),
         name="passage",
-    )(place, passage_q, start, *wins)
+    )(passage_q, start, *wins)
 
 
 def permute(block, route):
@@ -288,39 +290,51 @@
 
 def on_device(passage_q, passage_k, passage_v, new_q, new_k, new_v, segments):
     ctx, head = lax.axis_index("ctx"), lax.axis_index("head")
-    x, core, y_hi = ctx % 4, head % 2, head // 2 % 2
+    y_hi = head // 2 % 2
     shape = jax.ShapeDtypeStruct
 
-    blocks = pl.pallas_call(
-        pack,
-        out_shape=shape((PEERS, KVR + HEADS * NT, HD), BF),
-        in_specs=[VM] * 5,
-        out_specs=VM,
-        compiler_params=params(),
-        name="pack",
-    )(passage_k, passage_v, new_k, new_v, new_q)
+    def packed(kernel, rows, *arrays):
+        return pl.pallas_call(
+            kernel,
+            out_shape=shape((PEERS, rows, HD), BF),
+            in_specs=[VM] * len(arrays),
+            out_specs=VM,
+            compiler_params=params(),
+            name=kernel.__name__,
+        )(*arrays)
+
+    kv_blocks = packed(pack_kv, KVR, passage_k, passage_v, new_k, new_v)
+    q_blocks = packed(pack_q, HEADS * NT, new_q)
+
+    flat = ctx * 16 + head
+    padded = jnp.concatenate([jnp.full((512,), -1, jnp.int32), segments])
+    around = lax.dynamic_slice_in_dim(padded, flat // 4 * 256, 768, 0)
+    seg_q = lax.dynamic_slice_in_dim(segments, flat * PT, PT, 0)
+    start = jnp.sum((around[None, :] < seg_q[:, None]).astype(jnp.int32), axis=1, keepdims=True)
+
     own = jnp.concatenate([passage_k, passage_v], axis=1)
-    got, other_y = together(exchange(blocks), permute(own, OTHER_Y))
-    kv0 = got[:, :KVR]
+    kv0, q_blocks, own, start = together(exchange(kv_blocks), q_blocks, own, start)
     kv0_other = permute(kv0, SIBLING)
     left = permute(kv0, along_x(1))
     right = permute(kv0, along_x(3))
-    level0 = jnp.concatenate([own, other_y], axis=0)
-    level1 = permute(level0, BACK1)
-    level2 = permute(level0, BACK2)
-
-    places = lambda *d: jnp.stack([core, x] + [(x + i) % 4 for i in d]).astype(jnp.int32)
-    state = ask(got, [(got, kv0_other, 0)], places(0), None, False)
-    left, right, state = together(left, right, state)
+    q, left, right = together(exchange(q_blocks), left, right)
+    back1, back2 = permute(own, BACK1), permute(own, BACK2)
+
     far = [permute(left[:16], along_x(1)), permute(right[16:], along_x(3))]
-    sides = [(b, permute(b, SIBLING), 0) for b in (left, right)]
-    state = ask(got, sides, places(3, 1), state, False)
-    *far, level1, level2 = together(*far, level1, level2, state)[:4]
-    far = [(b, permute(b, SIBLING), 16 * i) for i, b in enumerate(far)]
-    wins = [level2, level1, level0]
-    wins += [permute(w, SIBLING) for w in wins]
-    out_rows = ask(got, far, places(2, 2), state, True)
+    near = [(kv0, kv0_other, 0, 0)]
+    near += [(b, permute(b, SIBLING), 0, d) for b, d in ((left, 3), (right, 1))]
+    state = ask(q, near, None, False)
+    *far, back1, back2, state = together(*far, back1, back2, state)
+    across = permute(jnp.concatenate([back1, jnp.where(y_hi == 0, own, back2)]), OTHER_Y)
+    column = jnp.concatenate([own, back1, back2])
+    column_other = permute(column, SIBLING)
+    far = [(b, permute(b, SIBLING), 16 * i, 2) for i, b in enumerate(far)]
+    out_rows = ask(q, far, state, True)
+    across, column_other, out_rows = together(across, column_other, out_rows)
+    wins = [column, across, column_other, permute(across, SIBLING)]
     new_blocks = exchange(out_rows.reshape(PEERS, HEADS * NT, HD))
+    pass_out = passages(passage_q, start, wins)
+    pass_out, new_blocks = together(pass_out, new_blocks)
     new_out = pl.pallas_call(
         unpack_out,
         out_shape=shape((NT, QH * HD), BF),
@@ -330,12 +344,6 @@
         name="unpack_out",
     )(new_blocks)
 
-    flat = ctx * 16 + head
-    padded = jnp.concatenate([jnp.full((512,), -1, jnp.int32), segments])
-    near = lax.dynamic_slice_in_dim(padded, flat // 4 * 256, 768, 0)
-    seg_q = lax.dynamic_slice_in_dim(segments, flat * PT, PT, 0)
-    start = jnp.sum((near[None, :] < seg_q[:, None]).astype(jnp.int32), axis=1, keepdims=True)
-    pass_out = passages(passage_q, start, y_hi, core, wins)
     return pass_out, new_out
 
 

time: 140 us -> 123 us (0.88)
  starting transfers between devices: 44 us -> 35 us
  Pallas kernels: 64.4 us -> 59.7 us
  local copies, waits for them, and re-layouts: 6 us -> 3.56 us
  other arithmetic: 2.74 us -> 0.31 us
  waiting for transfers between devices: 21.4 us -> 22.9 us
    all_to_all x2 -> x3, waiting for transfers between devices: 0.01 us -> 21.7 us  [exchange(): lax.all_to_all(blocks, BOTH, split_axis=0, concat_axis=0, tiled=True, axi...]
    ppermute x15 -> x14, waiting for transfers between devices: 21.4 us -> 1.26 us  [permute(): return lax.ppermute(block, BOTH, route)]
    ppermute x15 -> x14, starting transfers between devices: 21.3 us -> 16.6 us  [permute(): return lax.ppermute(block, BOTH, route)]
    pallas_call x3 -> x2, Pallas kernels: 44.8 us -> 40.2 us  [ask(): pl.pallas_call(functools.partial(question, kinds, state is None, last), o...]
    all_to_all x2 -> x3, starting transfers between devices: 22.7 us -> 18.4 us  [exchange(): lax.all_to_all(blocks, BOTH, split_axis=0, concat_axis=0, tiled=True, axi...]
    another operation x4 -> x0, other arithmetic: 2.51 us -> none  [the longest x3 1.92 us: on_device(): jnp.stack([core, x] + [(x + i) % 4 for i in d]).astype(jnp.int32)]
    pallas_call x1, Pallas kernels: 15.3 us -> 13.7 us  [passages(): pl.pallas_call(passage, out_shape=jax.ShapeDtypeStruct((PT, QH * HD), BF)...]
    pallas_call x1 -> x2, Pallas kernels: 2.43 us -> 3.87 us  [packed(): pl.pallas_call(kernel, out_shape=shape((PEERS, rows, HD), BF), in_specs=[...]
  transfers between devices with their start and end apart: 17 -> 17, of which waited for: 2 -> 5; matrix products, arithmetic and copies ran while one was open for 3% -> 1% of each run, Pallas kernels for 43% -> 46%
where the time goes in v3:
time: 123 us; the launch traced here: 122 us
  Pallas kernels  59.7 us (49%)
  starting transfers between devices  35 us (28%)
  waiting for transfers between devices  22.9 us (19%)
  local copies, waits for them, and re-layouts  3.56 us (3%)
    pallas_call x2, Pallas kernels, ask(): pl.pallas_call(functools.partial(question, kinds, state is None, last), o...  40.2 us
    all_to_all x3, waiting for transfers between devices, exchange(): lax.all_to_all(blocks, BOTH, split_axis=0, concat_axis=0, tiled=True, axi...  21.7 us
    all_to_all x3, starting transfers between devices, exchange(): lax.all_to_all(blocks, BOTH, split_axis=0, concat_axis=0, tiled=True, axi...  18.4 us
    ppermute x14, starting transfers between devices, permute(): return lax.ppermute(block, BOTH, route)  16.6 us
    pallas_call x1, Pallas kernels, passages(): pl.pallas_call(passage, out_shape=jax.ShapeDtypeStruct((PT, QH * HD), BF)...  13.7 us
    pallas_call x2, Pallas kernels, packed(): pl.pallas_call(kernel, out_shape=shape((PEERS, rows, HD), BF), in_specs=[...  3.87 us
    unnamed x34, local copies, waits for them, and re-layouts  2.66 us
  transfers between devices with their start and end apart: 17, of which 5 were waited for; matrix products, arithmetic and copies ran while one was open for 1% of the time, Pallas kernels for 46%

profile of v3, /device:TPU:1, one launch (start us, length us, event | category | flops | bytes accessed | tf_op | source)
XLA Modules:
  0.0 122.4 jit_solution(16100450195503461138)
XLA Ops:
  0.7 1.9 %pack_kv.1 = bf16[32,80,128]{2,1,0:T(8,128)(2,1)} custom-call(bf16[64,1024]{1,0:T(8,128)(2,1)} %k_ref.1, bf16[64,1024]{1,0:T(8,128)(2,1)} %v_ref.1, bf16[16,1024]{1,0:T(8,128)(2,1)} %nk_ref.1, bf16[16,1024]{1,0:T(8,128)(2,1)} %nv_ref.1), custom_call_target="tpu_custom_call" | custom-call | tf_op jit(solution)/shard_map/pack_kv/pallas_call | solution.py:297
  2.6 9.6 %all-to-all-start = ((bf16[32,80,128]{2,1,0:T(8,128)(2,1)}), bf16[32,80,128]{2,1,0:T(8,128)(2,1)S(1)}, u32[]{:S(2)}, u32[]{:S(2)}) async-start(bf16[32,80,128]{2,1,0:T(8,128)(2,1)} %pack_kv.1), calls=%async_computation | async-start | bytes 1310720 | tf_op jit(solution)/shard_map/all_to_all | solution.py:286
  12.2 1.9 %pack_q.1 = bf16[32,64,128]{2,1,0:T(8,128)(2,1)} custom-call(bf16[16,16384]{1,0:T(8,128)(2,1)} %q_ref.2), custom_call_target="tpu_custom_call" | custom-call | tf_op jit(solution)/shard_map/pack_q/pallas_call | solution.py:297
  14.2 0.1 dynamic_slice.7
  14.2 0.1 pad_dynamic-slice_fusion
  14.3 0.2 convert_reduce_fusion
  14.5 10.5 %all-to-all-done.refs_1_ = bf16[32,80,128]{2,1,0:T(8,128)(2,1)S(1)} async-done(((bf16[32,80,128]{2,1,0:T(8,128)(2,1)}), bf16[32,80,128]{2,1,0:T(8,128)(2,1)S(1)}, u32[]{:S(2)}, u32[]{:S(2)}) %all-to-all-start) | async-done | bytes 655392 | tf_op jit(solution)/shard_map/all_to_all | solution.py:286
  25.1 1.2 collective-permute-start
  26.3 1.5 %collective-permute-start.1 = (bf16[32,80,128]{2,1,0:T(8,128)(2,1)S(1)}, bf16[32,80,128]{2,1,0:T(8,128)(2,1)S(1)}, u32[]{:S(2)}, u32[]{:S(2)}) collective-permute-start(bf16[32,80,128]{2,1,0:T(8,128)(2,1)S(1)} %all-to-all-done.refs_1_), channel_id=1, source_target_pairs={{0,48},{1,49},{2,50},{3,51},{4,52},{5,53},{6,54},{7,55},{8,56},{9,... | collective-permute-start | bytes 1966088 | tf_op jit(solution)/shard_map/ppermute | solution.py:278
  27.7 4.4 %all-to-all-start.1 = ((bf16[32,64,128]{2,1,0:T(8,128)(2,1)}), bf16[32,64,128]{2,1,0:T(8,128)(2,1)S(1)}, u32[]{:S(2)}, u32[]{:S(2)}) async-start(bf16[32,64,128]{2,1,0:T(8,128)(2,1)} %pack_q.1), calls=%async_computation.1 | async-start | bytes 1048576 | tf_op jit(solution)/shard_map/all_to_all | solution.py:286
  32.2 0.4 collective-permute-start.6
  32.6 11.1 %all-to-all-done.1.refs_0_ = bf16[32,64,128]{2,1,0:T(8,128)(2,1)S(1)} async-done(((bf16[32,64,128]{2,1,0:T(8,128)(2,1)}), bf16[32,64,128]{2,1,0:T(8,128)(2,1)S(1)}, u32[]{:S(2)}, u32[]{:S(2)}) %all-to-all-start.1) | async-done | bytes 524320 | tf_op jit(solution)/shard_map/all_to_all | solution.py:286
  43.7 0.0 collective-permute-done.refs_3_
  43.7 0.0 collective-permute-done.1.refs_5_
  43.7 0.4 collective-permute-start.7
  44.1 0.2 collective-permute-start.8
  44.3 1.9 %collective-permute-start.4 = (bf16[64,2048]{1,0:T(8,128)(2,1)S(1)}, bf16[64,2048]{1,0:T(8,128)(2,1)S(1)}, u32[]{:S(2)}, u32[]{:S(2)}) collective-permute-start(bf16[64,2048]{1,0:T(8,128)(2,1)S(1)} %pad_maximum_fusion.1), channel_id=1, source_target_pairs={{0,4},{1,5},{2,6},{3,7},{4,8},{5,9},{6,10},{7,11},{8,12},{9,13},{1... | collective-permute-start | bytes 786440 | tf_op jit(solution)/shard_map/ppermute | solution.py:278
  46.2 4.0 %collective-permute-start.5 = (bf16[64,2048]{1,0:T(8,128)(2,1)S(1)}, bf16[64,2048]{1,0:T(8,128)(2,1)S(1)}, u32[]{:S(2)}, u32[]{:S(2)}) collective-permute-start(bf16[64,2048]{1,0:T(8,128)(2,1)S(1)} %pad_maximum_fusion.1), channel_id=1, source_target_pairs={{0,8},{1,9},{2,10},{3,11},{4,12},{5,13},{6,14},{7,15},{8,16},{9,17... | collective-permute-start | bytes 786440 | tf_op jit(solution)/shard_map/ppermute | solution.py:278
  50.3 0.0 collective-permute-done.6.refs_2_
  50.3 0.4 collective-permute-start.2
  50.7 0.0 collective-permute-done.7.refs_4_
  50.7 2.3 %collective-permute-start.3 = (bf16[16,80,128]{2,1,0:T(8,128)(2,1)S(1)}, bf16[16,80,128]{2,1,0:T(8,128)(2,1)S(1)}, u32[]{:S(2)}, u32[]{:S(2)}) collective-permute-start(bf16[16,80,128]{2,1,0:T(8,128)(2,1)S(1)} %slice.7), channel_id=1, source_target_pairs={{0,48},{1,49},{2,50},{3,51},{4,52},{5,53},{6,54},{7,55},{8,56},{9,... | collective-permute-start | bytes 983048 | tf_op jit(solution)/shard_map/ppermute | solution.py:278
  53.0 0.0 collective-permute-done.8.refs_6_
  53.1 28.5 %question.2.refs_5_ = f32[2048,256]{1,0:T(8,128)} custom-call(bf16[32,64,128]{2,1,0:T(8,128)(2,1)} %copy-done.2, bf16[32,80,128]{2,1,0:T(8,128)(2,1)} %copy-done.1, bf16[32,80,128]{2,1,0:T(8,128)(2,1)} %collective-permute-done.6.refs_2_, bf16[32,80,128]{2,1,0:T(8,128)(2,1)} %copy-done.5, bf16[32,80,128]{2,1,0:T(8,128)(2,1)} %collective-permute-done.7.refs_4_, ...), custom_call_target="tpu_custom_call" | custom-call | flops 12079595520 | bytes 4194304 | tf_op jit(solution)/shard_map/question/pallas_call | solution.py:198
  81.5 0.0 collective-permute-done.4
  81.5 0.0 collective-permute-done.5
  81.5 0.0 collective-permute-done.2.refs_1_
  81.6 0.0 collective-permute-done.3.refs_3_
  81.6 0.1 broadcast_select_fusion
  81.7 1.6 %collective-permute-start.10 = (bf16[192,2048]{1,0:T(8,128)(2,1)S(1)}, bf16[192,2048]{1,0:T(8,128)(2,1)S(1)}, u32[]{:S(2)}, u32[]{:S(2)}) collective-permute-start(bf16[192,2048]{1,0:T(8,128)(2,1)S(1)} %get-tuple-element.37.refs_0_), channel_id=1, source_target_pairs={{0,1},{1,0},{2,3},{3,2},{4,5},{5,4},{6,7},{7,6},{8,9},{9,8},{10,11... | collective-permute-start | bytes 2359304 | tf_op jit(solution)/shard_map/ppermute | solution.py:278
  83.3 0.1 collective-permute-start.11
  83.4 0.4 collective-permute-start.12
  83.8 1.3 %collective-permute-start.9 = (bf16[128,2048]{1,0:T(8,128)(2,1)S(1)}, bf16[128,2048]{1,0:T(8,128)(2,1)S(1)}, u32[]{:S(2)}, u32[]{:S(2)}) collective-permute-start(bf16[128,2048]{1,0:T(8,128)(2,1)S(1)} %pad_maximum_fusion), channel_id=1, source_target_pairs={{0,2},{1,3},{2,0},{3,1},{4,6},{5,7},{6,4},{7,5},{8,10},{9,11},{10,... | collective-permute-start | bytes 1572872 | tf_op jit(solution)/shard_map/ppermute | solution.py:278
  85.1 0.5 collective-permute-done.11.refs_2_
  85.7 0.5 collective-permute-done.12.refs_4_
  86.1 0.3 copy-done.14
  86.4 0.7 copy-done.15
  87.1 11.7 %question.3 = bf16[2048,128]{1,0:T(8,128)(2,1)} custom-call(bf16[32,64,128]{2,1,0:T(8,128)(2,1)} %copy-done.2, bf16[16,80,128]{2,1,0:T(8,128)(2,1)} %copy-done.12, bf16[16,80,128]{2,1,0:T(8,128)(2,1)} %copy-done.14, bf16[16,80,128]{2,1,0:T(8,128)(2,1)} %copy-done.13, bf16[16,80,128]{2,1,0:T(8,128)(2,1)} %copy-done.15, f32[2048,256]{1,0:T(8,128)} %question.2.refs_5_), custom_call_target="tpu_custom_call" | custom-call | flops 4026531840 | bytes 4194304 | tf_op jit(solution)/shard_map/question/pallas_call | solution.py:198
  98.8 0.2 collective-permute-done.9.refs_1_
  99.1 0.0 collective-permute-done.10.refs_2_
  99.1 0.9 collective-permute-start.13
  100.0 4.4 %all-to-all-start.2 = ((bf16[32,64,128]{2,1,0:T(8,128)(2,1)}), bf16[32,64,128]{2,1,0:T(8,128)(2,1)S(1)}, u32[]{:S(2)}, u32[]{:S(2)}) async-start(bf16[32,64,128]{2,1,0:T(8,128)(2,1)} %bitcast.2), calls=%async_computation.2 | async-start | bytes 1048576 | tf_op jit(solution)/shard_map/all_to_all | solution.py:286
  104.4 0.7 copy.10.start_ref
  105.1 0.8 copy-done.11
  105.9 13.7 %passage.1 = bf16[64,16384]{1,0:T(8,128)(2,1)} custom-call(bf16[64,16384]{1,0:T(8,128)(2,1)} %q_ref.3, s32[64,1]{1,0:T(8,128)} %copy.10.start_ref, bf16[192,2048]{1,0:T(8,128)(2,1)} %copy-done.7, bf16[128,2048]{1,0:T(8,128)(2,1)} %copy-done.10, bf16[192,2048]{1,0:T(8,128)(2,1)} %copy-done.9, bf16[128,2048]{1,0:T(8,128)(2,1)} %copy-done.11), custom_call_target="tpu_custom_call" | custom-call | flops 4026531840 | bytes 7340032 | tf_op jit(solution)/shard_map/passage/pallas_call | solution.py:259
  119.7 0.0 all-to-all-done.2.blk_ref
  119.7 0.8 copy-done
  120.5 1.9 %unpack_out.1 = bf16[16,16384]{1,0:T(8,128)(2,1)} custom-call(bf16[32,64,128]{2,1,0:T(8,128)(2,1)} %copy-done), custom_call_target="tpu_custom_call" | custom-call | tf_op jit(solution)/shard_map/unpack_out/pallas_call | solution.py:338
  (35 shorter events, 0.2 us)
Async XLA Ops:
  0.6 13.9 %copy-start.4 = (bf16[64,1024]{1,0:T(8,128)(2,1)S(1)}, bf16[64,1024]{1,0:T(8,128)(2,1)}, u32[]{:S(2)}) copy-start(bf16[64,1024]{1,0:T(8,128)(2,1)} %k_ref.1) | copy-start | bytes 393220
  0.6 13.9 %copy-start.3 = (bf16[64,1024]{1,0:T(8,128)(2,1)S(1)}, bf16[64,1024]{1,0:T(8,128)(2,1)}, u32[]{:S(2)}) copy-start(bf16[64,1024]{1,0:T(8,128)(2,1)} %v_ref.1) | copy-start | bytes 393220
  0.7 13.5 %copy-start.8 = (s32[8192]{0:T(1024)S(1)}, s32[8192]{0:T(1024)}, u32[]{:S(2)}) copy-start(s32[8192]{0:T(1024)} %param.13) | copy-start | bytes 98308
  2.6 22.5 %all-to-all-start = ((bf16[32,80,128]{2,1,0:T(8,128)(2,1)}), bf16[32,80,128]{2,1,0:T(8,128)(2,1)S(1)}, u32[]{:S(2)}, u32[]{:S(2)}) async-start(bf16[32,80,128]{2,1,0:T(8,128)(2,1)} %pack_kv.1), calls=%async_computation | async-start | bytes 1310720 | tf_op jit(solution)/shard_map/all_to_all | solution.py:286
  25.1 28.0 %copy-start.1 = (bf16[32,80,128]{2,1,0:T(8,128)(2,1)}, bf16[32,80,128]{2,1,0:T(8,128)(2,1)S(1)}, u32[]{:S(2)}) copy-start(bf16[32,80,128]{2,1,0:T(8,128)(2,1)S(1)} %all-to-all-done.refs_1_) | copy-start | bytes 1966084
  25.1 18.6 %collective-permute-start = (bf16[32,80,128]{2,1,0:T(8,128)(2,1)S(1)}, bf16[32,80,128]{2,1,0:T(8,128)(2,1)S(1)}, u32[]{:S(2)}, u32[]{:S(2)}) collective-permute-start(bf16[32,80,128]{2,1,0:T(8,128)(2,1)S(1)} %all-to-all-done.refs_1_), channel_id=1, source_target_pairs={{0,16},{1,17},{2,18},{3,19},{4,20},{5,21},{6,22},{7,23},{8,24},{9,... | collective-permute-start | bytes 1966088 | tf_op jit(solution)/shard_map/ppermute | solution.py:278
  26.3 17.4 %collective-permute-start.1 = (bf16[32,80,128]{2,1,0:T(8,128)(2,1)S(1)}, bf16[32,80,128]{2,1,0:T(8,128)(2,1)S(1)}, u32[]{:S(2)}, u32[]{:S(2)}) collective-permute-start(bf16[32,80,128]{2,1,0:T(8,128)(2,1)S(1)} %all-to-all-done.refs_1_), channel_id=1, source_target_pairs={{0,48},{1,49},{2,50},{3,51},{4,52},{5,53},{6,54},{7,55},{8,56},{9,... | collective-permute-start | bytes 1966088 | tf_op jit(solution)/shard_map/ppermute | solution.py:278
  27.7 15.9 %all-to-all-start.1 = ((bf16[32,64,128]{2,1,0:T(8,128)(2,1)}), bf16[32,64,128]{2,1,0:T(8,128)(2,1)S(1)}, u32[]{:S(2)}, u32[]{:S(2)}) async-start(bf16[32,64,128]{2,1,0:T(8,128)(2,1)} %pack_q.1), calls=%async_computation.1 | async-start | bytes 1048576 | tf_op jit(solution)/shard_map/all_to_all | solution.py:286
  32.2 18.1 %collective-permute-start.6 = (bf16[32,80,128]{2,1,0:T(8,128)(2,1)S(1)}, bf16[32,80,128]{2,1,0:T(8,128)(2,1)}, u32[]{:S(2)}, u32[]{:S(2)}) collective-permute-start(bf16[32,80,128]{2,1,0:T(8,128)(2,1)S(1)} %all-to-all-done.refs_1_), channel_id=1, source_target_pairs={{0,1},{1,0},{2,3},{3,2},{4,5},{5,4},{6,7},{7,6},{8,9},{9,8},{10,11... | collective-permute-start | bytes 1966088 | tf_op jit(solution)/shard_map/ppermute | solution.py:278
  43.7 9.3 %copy-start.2 = (bf16[32,64,128]{2,1,0:T(8,128)(2,1)}, bf16[32,64,128]{2,1,0:T(8,128)(2,1)S(1)}, u32[]{:S(2)}) copy-start(bf16[32,64,128]{2,1,0:T(8,128)(2,1)S(1)} %all-to-all-done.1.refs_0_) | copy-start | bytes 1572868
  43.7 9.3 %copy-start.5 = (bf16[32,80,128]{2,1,0:T(8,128)(2,1)}, bf16[32,80,128]{2,1,0:T(8,128)(2,1)S(1)}, u32[]{:S(2)}) copy-start(bf16[32,80,128]{2,1,0:T(8,128)(2,1)S(1)} %collective-permute-done.refs_3_) | copy-start | bytes 1966084
  43.7 9.3 %copy-start.6 = (bf16[32,80,128]{2,1,0:T(8,128)(2,1)}, bf16[32,80,128]{2,1,0:T(8,128)(2,1)S(1)}, u32[]{:S(2)}) copy-start(bf16[32,80,128]{2,1,0:T(8,128)(2,1)S(1)} %collective-permute-done.1.refs_5_) | copy-start | bytes 1966084
  43.7 7.0 %collective-permute-start.7 = (bf16[32,80,128]{2,1,0:T(8,128)(2,1)S(1)}, bf16[32,80,128]{2,1,0:T(8,128)(2,1)}, u32[]{:S(2)}, u32[]{:S(2)}) collective-permute-start(bf16[32,80,128]{2,1,0:T(8,128)(2,1)S(1)} %collective-permute-done.refs_3_), channel_id=1, source_target_pairs={{0,1},{1,0},{2,3},{3,2},{4,5},{5,4},{6,7},{7,6},{8,9},{9,8},{10,11... | collective-permute-start | bytes 1966088 | tf_op jit(solution)/shard_map/ppermute | solution.py:278
  44.1 8.9 %collective-permute-start.8 = (bf16[32,80,128]{2,1,0:T(8,128)(2,1)S(1)}, bf16[32,80,128]{2,1,0:T(8,128)(2,1)}, u32[]{:S(2)}, u32[]{:S(2)}) collective-permute-start(bf16[32,80,128]{2,1,0:T(8,128)(2,1)S(1)} %collective-permute-done.1.refs_5_), channel_id=1, source_target_pairs={{0,1},{1,0},{2,3},{3,2},{4,5},{5,4},{6,7},{7,6},{8,9},{9,8},{10,11... | collective-permute-start | bytes 1966088 | tf_op jit(solution)/shard_map/ppermute | solution.py:278
  44.3 37.2 %collective-permute-start.4 = (bf16[64,2048]{1,0:T(8,128)(2,1)S(1)}, bf16[64,2048]{1,0:T(8,128)(2,1)S(1)}, u32[]{:S(2)}, u32[]{:S(2)}) collective-permute-start(bf16[64,2048]{1,0:T(8,128)(2,1)S(1)} %pad_maximum_fusion.1), channel_id=1, source_target_pairs={{0,4},{1,5},{2,6},{3,7},{4,8},{5,9},{6,10},{7,11},{8,12},{9,13},{1... | collective-permute-start | bytes 786440 | tf_op jit(solution)/shard_map/ppermute | solution.py:278
  46.2 35.3 %collective-permute-start.5 = (bf16[64,2048]{1,0:T(8,128)(2,1)S(1)}, bf16[64,2048]{1,0:T(8,128)(2,1)S(1)}, u32[]{:S(2)}, u32[]{:S(2)}) collective-permute-start(bf16[64,2048]{1,0:T(8,128)(2,1)S(1)} %pad_maximum_fusion.1), channel_id=1, source_target_pairs={{0,8},{1,9},{2,10},{3,11},{4,12},{5,13},{6,14},{7,15},{8,16},{9,17... | collective-permute-start | bytes 786440 | tf_op jit(solution)/shard_map/ppermute | solution.py:278
  50.3 31.3 %collective-permute-start.2 = (bf16[16,80,128]{2,1,0:T(8,128)(2,1)S(1)}, bf16[16,80,128]{2,1,0:T(8,128)(2,1)S(1)}, u32[]{:S(2)}, u32[]{:S(2)}) collective-permute-start(bf16[16,80,128]{2,1,0:T(8,128)(2,1)S(1)} %slice.6), channel_id=1, source_target_pairs={{0,16},{1,17},{2,18},{3,19},{4,20},{5,21},{6,22},{7,23},{8,24},{9,... | collective-permute-start | bytes 983048 | tf_op jit(solution)/shard_map/ppermute | solution.py:278
  50.7 30.8 %collective-permute-start.3 = (bf16[16,80,128]{2,1,0:T(8,128)(2,1)S(1)}, bf16[16,80,128]{2,1,0:T(8,128)(2,1)S(1)}, u32[]{:S(2)}, u32[]{:S(2)}) collective-permute-start(bf16[16,80,128]{2,1,0:T(8,128)(2,1)S(1)} %slice.7), channel_id=1, source_target_pairs={{0,48},{1,49},{2,50},{3,51},{4,52},{5,53},{6,54},{7,55},{8,56},{9,... | collective-permute-start | bytes 983048 | tf_op jit(solution)/shard_map/ppermute | solution.py:278
  81.5 4.6 %copy-start.12 = (bf16[16,80,128]{2,1,0:T(8,128)(2,1)}, bf16[16,80,128]{2,1,0:T(8,128)(2,1)S(1)}, u32[]{:S(2)}) copy-start(bf16[16,80,128]{2,1,0:T(8,128)(2,1)S(1)} %collective-permute-done.2.refs_1_) | copy-start | bytes 983044
  81.6 4.6 %copy-start.13 = (bf16[16,80,128]{2,1,0:T(8,128)(2,1)}, bf16[16,80,128]{2,1,0:T(8,128)(2,1)S(1)}, u32[]{:S(2)}) copy-start(bf16[16,80,128]{2,1,0:T(8,128)(2,1)S(1)} %collective-permute-done.3.refs_3_) | copy-start | bytes 983044
  81.7 17.2 %copy-start.7 = (bf16[192,2048]{1,0:T(8,128)(2,1)}, bf16[192,2048]{1,0:T(8,128)(2,1)S(1)}, u32[]{:S(2)}) copy-start(bf16[192,2048]{1,0:T(8,128)(2,1)S(1)} %get-tuple-element.37.refs_0_) | copy-start | bytes 2359300
  81.7 17.4 %collective-permute-start.10 = (bf16[192,2048]{1,0:T(8,128)(2,1)S(1)}, bf16[192,2048]{1,0:T(8,128)(2,1)S(1)}, u32[]{:S(2)}, u32[]{:S(2)}) collective-permute-start(bf16[192,2048]{1,0:T(8,128)(2,1)S(1)} %get-tuple-element.37.refs_0_), channel_id=1, source_target_pairs={{0,1},{1,0},{2,3},{3,2},{4,5},{5,4},{6,7},{7,6},{8,9},{9,8},{10,11... | collective-permute-start | bytes 2359304 | tf_op jit(solution)/shard_map/ppermute | solution.py:278
  83.3 2.4 %collective-permute-start.11 = (bf16[16,80,128]{2,1,0:T(8,128)(2,1)S(1)}, bf16[16,80,128]{2,1,0:T(8,128)(2,1)S(1)}, u32[]{:S(2)}, u32[]{:S(2)}) collective-permute-start(bf16[16,80,128]{2,1,0:T(8,128)(2,1)S(1)} %collective-permute-done.2.refs_1_), channel_id=1, source_target_pairs={{0,1},{1,0},{2,3},{3,2},{4,5},{5,4},{6,7},{7,6},{8,9},{9,8},{10,11... | collective-permute-start | bytes 983048 | tf_op jit(solution)/shard_map/ppermute | solution.py:278
  83.4 2.8 %collective-permute-start.12 = (bf16[16,80,128]{2,1,0:T(8,128)(2,1)S(1)}, bf16[16,80,128]{2,1,0:T(8,128)(2,1)S(1)}, u32[]{:S(2)}, u32[]{:S(2)}) collective-permute-start(bf16[16,80,128]{2,1,0:T(8,128)(2,1)S(1)} %collective-permute-done.3.refs_3_), channel_id=1, source_target_pairs={{0,1},{1,0},{2,3},{3,2},{4,5},{5,4},{6,7},{7,6},{8,9},{9,8},{10,11... | collective-permute-start | bytes 983048 | tf_op jit(solution)/shard_map/ppermute | solution.py:278
  83.8 15.2 %collective-permute-start.9 = (bf16[128,2048]{1,0:T(8,128)(2,1)S(1)}, bf16[128,2048]{1,0:T(8,128)(2,1)S(1)}, u32[]{:S(2)}, u32[]{:S(2)}) collective-permute-start(bf16[128,2048]{1,0:T(8,128)(2,1)S(1)} %pad_maximum_fusion), channel_id=1, source_target_pairs={{0,2},{1,3},{2,0},{3,1},{4,6},{5,7},{6,4},{7,5},{8,10},{9,11},{10,... | collective-permute-start | bytes 1572872 | tf_op jit(solution)/shard_map/ppermute | solution.py:278
  85.7 0.7 copy-start.14
  86.4 0.7 copy-start.15
  99.1 6.0 %copy-start.10 = (bf16[128,2048]{1,0:T(8,128)(2,1)}, bf16[128,2048]{1,0:T(8,128)(2,1)S(1)}, u32[]{:S(2)}) copy-start(bf16[128,2048]{1,0:T(8,128)(2,1)S(1)} %collective-permute-done.9.refs_1_) | copy-start | bytes 1572868
  99.1 6.0 %copy-start.9 = (bf16[192,2048]{1,0:T(8,128)(2,1)}, bf16[192,2048]{1,0:T(8,128)(2,1)S(1)}, u32[]{:S(2)}) copy-start(bf16[192,2048]{1,0:T(8,128)(2,1)S(1)} %collective-permute-done.10.refs_2_) | copy-start | bytes 2359300
  99.1 6.0 %collective-permute-start.13 = (bf16[128,2048]{1,0:T(8,128)(2,1)S(1)}, bf16[128,2048]{1,0:T(8,128)(2,1)S(1)}, u32[]{:S(2)}, u32[]{:S(2)}) collective-permute-start(bf16[128,2048]{1,0:T(8,128)(2,1)S(1)} %collective-permute-done.9.refs_1_), channel_id=1, source_target_pairs={{0,1},{1,0},{2,3},{3,2},{4,5},{5,4},{6,7},{7,6},{8,9},{9,8},{10,11... | collective-permute-start | bytes 1572872 | tf_op jit(solution)/shard_map/ppermute | solution.py:278
  100.0 19.6 %all-to-all-start.2 = ((bf16[32,64,128]{2,1,0:T(8,128)(2,1)}), bf16[32,64,128]{2,1,0:T(8,128)(2,1)S(1)}, u32[]{:S(2)}, u32[]{:S(2)}) async-start(bf16[32,64,128]{2,1,0:T(8,128)(2,1)} %bitcast.2), calls=%async_computation.2 | async-start | bytes 1048576 | tf_op jit(solution)/shard_map/all_to_all | solution.py:286
  105.1 0.8 copy-start.11
  119.7 0.8 copy-start

commit v4 on v3

--- a/solution.py
+++ b/solution.py
@@ -73,7 +73,7 @@
 STATE = 2 * HD
 
 
-def pipelined(stages, blocks, tiles, state):
+def pipelined(stages, blocks, tiles, state, unroll=1):
     def step(t, option, fill=True, first=False):
         for r in range(blocks):
             for lag in range(stages):
@@ -91,7 +91,7 @@
         if end - start == 1:
             step(start, option)
         elif end > start:
-            lax.fori_loop(start, end, lambda t, c, o=option: (step(t, o), c)[1], 0)
+            lax.fori_loop(start, end, lambda t, c, o=option: (step(t, o), c)[1], 0, unroll=unroll)
     step(tiles[-1][1], tiles[-1][2], fill=False)
 
 
@@ -139,24 +139,29 @@
     old_tiles = old // KT
     lanes = [slice(j * HD, (j + 1) * HD) for j in range(KT // HD)]
 
-    def keys_of(t):
-        return pl.ds(t * KT if isinstance(t, int) else pl.multiple_of(t * KT, KT), KT)
+    def keys_of(t, width):
+        return pl.ds(t * KT if isinstance(t, int) else pl.multiple_of(t * KT, KT), width)
 
     def stage(which, t, r, masked):
         slot, rows = r % 2, slice(r * RB, (r + 1) * RB)
+        early = masked and r < BLOCKS // 2
+        width = KT // 2 if early else KT
+        half = KT // HD // 2
         if which == 0:
             per = RB // (HEADS * NT)
             q = q_ref[r * per : (r + 1) * per].reshape(RB, HD)
-            s_s[slot] = lax.dot_general(
-                q, k_s[keys_of(t), :], (((1,), (1,)), ((), ())), preferred_element_type=F32
+            k = k_s[keys_of(t, width), :]
+            s_s[slot, :, :width] = lax.dot_general(
+                q, k, (((1,), (1,)), ((), ())), preferred_element_type=F32
             )
         elif which == 1:
-            s = [s_s[slot, :, j] for j in lanes]
+            s = [s_s[slot, :, j] for j in lanes[: width // HD]]
             if masked:
                 row = r * RB + lax.broadcasted_iota(jnp.int32, (RB, HD), 0)
                 q_tok = token(row // 64, row % 16, x)
-                seen = [tok_s[t - old_tiles + 1, 0:1, j] <= q_tok for j in lanes]
-                s = [jnp.where(v, a, NEG) for v, a in zip(seen, s)]
+                for j in range(half) if early else range(half, 2 * half):
+                    seen = tok_s[t - old_tiles + 1, 0:1, lanes[j]] <= q_tok
+                    s[j] = jnp.where(seen, s[j], NEG)
             top = jnp.max(functools.reduce(jnp.maximum, s), axis=1, keepdims=True)
             before = m_s[rows, :]
             m = jnp.maximum(before, top)
@@ -165,12 +170,13 @@
             for j, a in zip(lanes, s):
                 p_s[slot, :, j] = jnp.exp2((a - m) * SCALE).astype(BF)
         else:
-            pv = jnp.dot(p_s[slot], v_s[keys_of(t), :], preferred_element_type=F32)
+            v = v_s[keys_of(t, width), :]
+            pv = jnp.dot(p_s[slot, :, :width], v, preferred_element_type=F32)
             a = a_s[slot]
             total[rows, :HD] = total[rows, :HD] * a + pv[:, :HD]
             total[rows, HD:] = total[rows, HD:] * a + pv[:, HD:]
 
-    pipelined(3, BLOCKS, [(0, old_tiles, False), (old_tiles, fresh // KT, True)], stage)
+    pipelined(3, BLOCKS, [(0, old_tiles, False), (old_tiles, fresh // KT, True)], stage, 2)
     if last:
         out_ref[...] = (total[:, :HD] / total[:, HD : HD + 1]).astype(BF)
     else:
@@ -218,11 +224,11 @@
 def passage(q_ref, start_ref, *refs):
     wins, o_ref, (bias_ref, s_s, p_s) = refs[:4], refs[4], refs[5:]
     yh, core = lax.axis_index("head") // 2 % 2, lax.axis_index("head") % 2
-    col = lax.broadcasted_iota(jnp.int32, (PT, KEYS), 1)
+    col = lax.broadcasted_iota(jnp.int32, (1, KEYS), 1)
     side, blk, t = col // 320, col // 64 % 5, col % 64
     level = jnp.where(blk < 3, 2 - blk, jnp.where(blk == 3, 1, 2 * yh))
     pos = level * 256 + (yh ^ (blk // 3)) * 128 + (core ^ side) * 64 + t
-    q_pos = 512 + yh * 128 + core * 64 + lax.broadcasted_iota(jnp.int32, (PT, KEYS), 0)
+    q_pos = 512 + yh * 128 + core * 64 + lax.broadcasted_iota(jnp.int32, (PT, 1), 0)
     bias_ref[...] = jnp.where((pos <= q_pos) & (pos >= start_ref[...]), 0.0, NEG)
     lanes = [slice(j * HD, (j + 1) * HD) for j in range(KEYS // HD)]
 

time: 123 us -> 120 us (0.976)
  Pallas kernels: 59.7 us -> 56 us
    pallas_call x2, Pallas kernels: 40.2 us -> 36.5 us  [ask(): pl.pallas_call(functools.partial(question, kinds, state is None, last), o...]
  transfers between devices with their start and end apart: 17 -> 17, of which waited for: 5 -> 5; matrix products, arithmetic and copies ran while one was open for 1% -> 1% of each run, Pallas kernels for 46% -> 44%
where the time goes in v4:
time: 120 us; the launch traced here: 119 us
  Pallas kernels  56 us (47%)
  starting transfers between devices  35 us (29%)
  waiting for transfers between devices  23.4 us (20%)
  local copies, waits for them, and re-layouts  3.56 us (3%)
    pallas_call x2, Pallas kernels, ask(): pl.pallas_call(functools.partial(question, kinds, state is None, last), o...  36.5 us
    all_to_all x3, waiting for transfers between devices, exchange(): lax.all_to_all(blocks, BOTH, split_axis=0, concat_axis=0, tiled=True, axi...  21.7 us
    all_to_all x3, starting transfers between devices, exchange(): lax.all_to_all(blocks, BOTH, split_axis=0, concat_axis=0, tiled=True, axi...  18.5 us
    ppermute x14, starting transfers between devices, permute(): return lax.ppermute(block, BOTH, route)  16.5 us
    pallas_call x1, Pallas kernels, passages(): pl.pallas_call(passage, out_shape=jax.ShapeDtypeStruct((PT, QH * HD), BF)...  13.7 us
    pallas_call x2, Pallas kernels, packed(): pl.pallas_call(kernel, out_shape=shape((PEERS, rows, HD), BF), in_specs=[...  3.87 us
    unnamed x34, local copies, waits for them, and re-layouts  2.66 us
  transfers between devices with their start and end apart: 17, of which 5 were waited for; matrix products, arithmetic and copies ran while one was open for 1% of the time, Pallas kernels for 44%

profile of v4, /device:TPU:1, one launch (start us, length us, event | category | flops | bytes accessed | tf_op | source)
XLA Modules:
  0.0 119.1 jit_solution(4061354361800194539)
XLA Ops:
  0.7 1.9 %pack_kv.1 = bf16[32,80,128]{2,1,0:T(8,128)(2,1)} custom-call(bf16[64,1024]{1,0:T(8,128)(2,1)} %k_ref.1, bf16[64,1024]{1,0:T(8,128)(2,1)} %v_ref.1, bf16[16,1024]{1,0:T(8,128)(2,1)} %nk_ref.1, bf16[16,1024]{1,0:T(8,128)(2,1)} %nv_ref.1), custom_call_target="tpu_custom_call" | custom-call | tf_op jit(solution)/shard_map/pack_kv/pallas_call | solution.py:303
  2.6 9.6 %all-to-all-start = ((bf16[32,80,128]{2,1,0:T(8,128)(2,1)}), bf16[32,80,128]{2,1,0:T(8,128)(2,1)S(1)}, u32[]{:S(2)}, u32[]{:S(2)}) async-start(bf16[32,80,128]{2,1,0:T(8,128)(2,1)} %pack_kv.1), calls=%async_computation | async-start | bytes 1310720 | tf_op jit(solution)/shard_map/all_to_all | solution.py:292
  12.2 1.9 %pack_q.1 = bf16[32,64,128]{2,1,0:T(8,128)(2,1)} custom-call(bf16[16,16384]{1,0:T(8,128)(2,1)} %q_ref.2), custom_call_target="tpu_custom_call" | custom-call | tf_op jit(solution)/shard_map/pack_q/pallas_call | solution.py:303
  14.2 0.1 dynamic_slice.7
  14.2 0.1 pad_dynamic-slice_fusion
  14.3 0.2 convert_reduce_fusion
  14.5 10.5 %all-to-all-done.refs_1_ = bf16[32,80,128]{2,1,0:T(8,128)(2,1)S(1)} async-done(((bf16[32,80,128]{2,1,0:T(8,128)(2,1)}), bf16[32,80,128]{2,1,0:T(8,128)(2,1)S(1)}, u32[]{:S(2)}, u32[]{:S(2)}) %all-to-all-start) | async-done | bytes 655392 | tf_op jit(solution)/shard_map/all_to_all | solution.py:292
  25.1 1.2 %collective-permute-start = (bf16[32,80,128]{2,1,0:T(8,128)(2,1)S(1)}, bf16[32,80,128]{2,1,0:T(8,128)(2,1)S(1)}, u32[]{:S(2)}, u32[]{:S(2)}) collective-permute-start(bf16[32,80,128]{2,1,0:T(8,128)(2,1)S(1)} %all-to-all-done.refs_1_), channel_id=1, source_target_pairs={{0,16},{1,17},{2,18},{3,19},{4,20},{5,21},{6,22},{7,23},{8,24},{9,... | collective-permute-start | bytes 1966088 | tf_op jit(solution)/shard_map/ppermute | solution.py:284
  26.3 1.5 %collective-permute-start.1 = (bf16[32,80,128]{2,1,0:T(8,128)(2,1)S(1)}, bf16[32,80,128]{2,1,0:T(8,128)(2,1)S(1)}, u32[]{:S(2)}, u32[]{:S(2)}) collective-permute-start(bf16[32,80,128]{2,1,0:T(8,128)(2,1)S(1)} %all-to-all-done.refs_1_), channel_id=1, source_target_pairs={{0,48},{1,49},{2,50},{3,51},{4,52},{5,53},{6,54},{7,55},{8,56},{9,... | collective-permute-start | bytes 1966088 | tf_op jit(solution)/shard_map/ppermute | solution.py:284
  27.7 4.4 %all-to-all-start.1 = ((bf16[32,64,128]{2,1,0:T(8,128)(2,1)}), bf16[32,64,128]{2,1,0:T(8,128)(2,1)S(1)}, u32[]{:S(2)}, u32[]{:S(2)}) async-start(bf16[32,64,128]{2,1,0:T(8,128)(2,1)} %pack_q.1), calls=%async_computation.1 | async-start | bytes 1048576 | tf_op jit(solution)/shard_map/all_to_all | solution.py:292
  32.2 0.4 collective-permute-start.6
  32.6 11.1 %all-to-all-done.1.refs_0_ = bf16[32,64,128]{2,1,0:T(8,128)(2,1)S(1)} async-done(((bf16[32,64,128]{2,1,0:T(8,128)(2,1)}), bf16[32,64,128]{2,1,0:T(8,128)(2,1)S(1)}, u32[]{:S(2)}, u32[]{:S(2)}) %all-to-all-start.1) | async-done | bytes 524320 | tf_op jit(solution)/shard_map/all_to_all | solution.py:292
  43.7 0.0 collective-permute-done.refs_3_
  43.7 0.0 collective-permute-done.1.refs_5_
  43.7 0.4 collective-permute-start.7
  44.1 0.2 collective-permute-start.8
  44.3 1.9 %collective-permute-start.4 = (bf16[64,2048]{1,0:T(8,128)(2,1)S(1)}, bf16[64,2048]{1,0:T(8,128)(2,1)S(1)}, u32[]{:S(2)}, u32[]{:S(2)}) collective-permute-start(bf16[64,2048]{1,0:T(8,128)(2,1)S(1)} %pad_maximum_fusion.1), channel_id=1, source_target_pairs={{0,4},{1,5},{2,6},{3,7},{4,8},{5,9},{6,10},{7,11},{8,12},{9,13},{1... | collective-permute-start | bytes 786440 | tf_op jit(solution)/shard_map/ppermute | solution.py:284
  46.2 4.0 %collective-permute-start.5 = (bf16[64,2048]{1,0:T(8,128)(2,1)S(1)}, bf16[64,2048]{1,0:T(8,128)(2,1)S(1)}, u32[]{:S(2)}, u32[]{:S(2)}) collective-permute-start(bf16[64,2048]{1,0:T(8,128)(2,1)S(1)} %pad_maximum_fusion.1), channel_id=1, source_target_pairs={{0,8},{1,9},{2,10},{3,11},{4,12},{5,13},{6,14},{7,15},{8,16},{9,17... | collective-permute-start | bytes 786440 | tf_op jit(solution)/shard_map/ppermute | solution.py:284
  50.3 0.0 collective-permute-done.6.refs_2_
  50.3 0.4 collective-permute-start.2
  50.7 0.0 collective-permute-done.7.refs_4_
  50.7 2.3 %collective-permute-start.3 = (bf16[16,80,128]{2,1,0:T(8,128)(2,1)S(1)}, bf16[16,80,128]{2,1,0:T(8,128)(2,1)S(1)}, u32[]{:S(2)}, u32[]{:S(2)}) collective-permute-start(bf16[16,80,128]{2,1,0:T(8,128)(2,1)S(1)} %slice.7), channel_id=1, source_target_pairs={{0,48},{1,49},{2,50},{3,51},{4,52},{5,53},{6,54},{7,55},{8,56},{9,... | collective-permute-start | bytes 983048 | tf_op jit(solution)/shard_map/ppermute | solution.py:284
  53.0 0.0 collective-permute-done.8.refs_6_
  53.1 25.2 %question.2.refs_5_ = f32[2048,256]{1,0:T(8,128)} custom-call(bf16[32,64,128]{2,1,0:T(8,128)(2,1)} %copy-done.2, bf16[32,80,128]{2,1,0:T(8,128)(2,1)} %copy-done.1, bf16[32,80,128]{2,1,0:T(8,128)(2,1)} %collective-permute-done.6.refs_2_, bf16[32,80,128]{2,1,0:T(8,128)(2,1)} %copy-done.5, bf16[32,80,128]{2,1,0:T(8,128)(2,1)} %collective-permute-done.7.refs_4_, ...), custom_call_target="tpu_custom_call" | custom-call | flops 12079595520 | bytes 4194304 | tf_op jit(solution)/shard_map/question/pallas_call | solution.py:204
  78.3 0.0 collective-permute-done.4
  78.3 0.0 collective-permute-done.5
  78.3 0.0 collective-permute-done.3.refs_3_
  78.3 0.1 broadcast_select_fusion
  78.4 1.6 %collective-permute-start.10 = (bf16[192,2048]{1,0:T(8,128)(2,1)S(1)}, bf16[192,2048]{1,0:T(8,128)(2,1)S(1)}, u32[]{:S(2)}, u32[]{:S(2)}) collective-permute-start(bf16[192,2048]{1,0:T(8,128)(2,1)S(1)} %get-tuple-element.37.refs_0_), channel_id=1, source_target_pairs={{0,1},{1,0},{2,3},{3,2},{4,5},{5,4},{6,7},{7,6},{8,9},{9,8},{10,11... | collective-permute-start | bytes 2359304 | tf_op jit(solution)/shard_map/ppermute | solution.py:284
  80.0 0.1 collective-permute-start.11
  80.1 0.4 collective-permute-start.12
  80.6 1.1 collective-permute-start.9
  81.7 0.7 collective-permute-done.11.refs_2_
  82.4 0.5 collective-permute-done.12.refs_4_
  82.9 0.3 copy-done.14
  83.1 0.7 copy-done.15
  83.9 11.3 %question.3 = bf16[2048,128]{1,0:T(8,128)(2,1)} custom-call(bf16[32,64,128]{2,1,0:T(8,128)(2,1)} %copy-done.2, bf16[16,80,128]{2,1,0:T(8,128)(2,1)} %copy-done.12, bf16[16,80,128]{2,1,0:T(8,128)(2,1)} %copy-done.14, bf16[16,80,128]{2,1,0:T(8,128)(2,1)} %copy-done.13, bf16[16,80,128]{2,1,0:T(8,128)(2,1)} %copy-done.15, f32[2048,256]{1,0:T(8,128)} %question.2.refs_5_), custom_call_target="tpu_custom_call" | custom-call | flops 4026531840 | bytes 4194304 | tf_op jit(solution)/shard_map/question/pallas_call | solution.py:204
  95.1 0.5 collective-permute-done.9.refs_1_
  95.6 0.0 collective-permute-done.10.refs_2_
  95.6 0.9 collective-permute-start.13
  96.6 4.5 %all-to-all-start.2 = ((bf16[32,64,128]{2,1,0:T(8,128)(2,1)}), bf16[32,64,128]{2,1,0:T(8,128)(2,1)S(1)}, u32[]{:S(2)}, u32[]{:S(2)}) async-start(bf16[32,64,128]{2,1,0:T(8,128)(2,1)} %bitcast.2), calls=%async_computation.2 | async-start | bytes 1048576 | tf_op jit(solution)/shard_map/all_to_all | solution.py:292
  101.1 0.7 copy.10.start_ref
  101.8 0.0 collective-permute-done.13.refs_3_
  101.9 0.8 copy-done.11
  102.7 13.7 %passage.1 = bf16[64,16384]{1,0:T(8,128)(2,1)} custom-call(bf16[64,16384]{1,0:T(8,128)(2,1)} %q_ref.3, s32[64,1]{1,0:T(8,128)} %copy.10.start_ref, bf16[192,2048]{1,0:T(8,128)(2,1)} %copy-done.7, bf16[128,2048]{1,0:T(8,128)(2,1)} %copy-done.10, bf16[192,2048]{1,0:T(8,128)(2,1)} %copy-done.9, bf16[128,2048]{1,0:T(8,128)(2,1)} %copy-done.11), custom_call_target="tpu_custom_call" | custom-call | flops 4026531840 | bytes 7340032 | tf_op jit(solution)/shard_map/passage/pallas_call | solution.py:265
  116.4 0.0 all-to-all-done.2.blk_ref
  116.4 0.8 copy-done
  117.2 1.9 %unpack_out.1 = bf16[16,16384]{1,0:T(8,128)(2,1)} custom-call(bf16[32,64,128]{2,1,0:T(8,128)(2,1)} %copy-done), custom_call_target="tpu_custom_call" | custom-call | tf_op jit(solution)/shard_map/unpack_out/pallas_call | solution.py:344
  (35 shorter events, 0.2 us)
Async XLA Ops:
  0.6 13.9 %copy-start.4 = (bf16[64,1024]{1,0:T(8,128)(2,1)S(1)}, bf16[64,1024]{1,0:T(8,128)(2,1)}, u32[]{:S(2)}) copy-start(bf16[64,1024]{1,0:T(8,128)(2,1)} %k_ref.1) | copy-start | bytes 393220
  0.6 13.9 %copy-start.3 = (bf16[64,1024]{1,0:T(8,128)(2,1)S(1)}, bf16[64,1024]{1,0:T(8,128)(2,1)}, u32[]{:S(2)}) copy-start(bf16[64,1024]{1,0:T(8,128)(2,1)} %v_ref.1) | copy-start | bytes 393220
  0.7 13.5 %copy-start.8 = (s32[8192]{0:T(1024)S(1)}, s32[8192]{0:T(1024)}, u32[]{:S(2)}) copy-start(s32[8192]{0:T(1024)} %param.13) | copy-start | bytes 98308
  2.6 22.5 %all-to-all-start = ((bf16[32,80,128]{2,1,0:T(8,128)(2,1)}), bf16[32,80,128]{2,1,0:T(8,128)(2,1)S(1)}, u32[]{:S(2)}, u32[]{:S(2)}) async-start(bf16[32,80,128]{2,1,0:T(8,128)(2,1)} %pack_kv.1), calls=%async_computation | async-start | bytes 1310720 | tf_op jit(solution)/shard_map/all_to_all | solution.py:292
  25.1 28.0 %copy-start.1 = (bf16[32,80,128]{2,1,0:T(8,128)(2,1)}, bf16[32,80,128]{2,1,0:T(8,128)(2,1)S(1)}, u32[]{:S(2)}) copy-start(bf16[32,80,128]{2,1,0:T(8,128)(2,1)S(1)} %all-to-all-done.refs_1_) | copy-start | bytes 1966084
  25.1 18.6 %collective-permute-start = (bf16[32,80,128]{2,1,0:T(8,128)(2,1)S(1)}, bf16[32,80,128]{2,1,0:T(8,128)(2,1)S(1)}, u32[]{:S(2)}, u32[]{:S(2)}) collective-permute-start(bf16[32,80,128]{2,1,0:T(8,128)(2,1)S(1)} %all-to-all-done.refs_1_), channel_id=1, source_target_pairs={{0,16},{1,17},{2,18},{3,19},{4,20},{5,21},{6,22},{7,23},{8,24},{9,... | collective-permute-start | bytes 1966088 | tf_op jit(solution)/shard_map/ppermute | solution.py:284
  26.3 17.4 %collective-permute-start.1 = (bf16[32,80,128]{2,1,0:T(8,128)(2,1)S(1)}, bf16[32,80,128]{2,1,0:T(8,128)(2,1)S(1)}, u32[]{:S(2)}, u32[]{:S(2)}) collective-permute-start(bf16[32,80,128]{2,1,0:T(8,128)(2,1)S(1)} %all-to-all-done.refs_1_), channel_id=1, source_target_pairs={{0,48},{1,49},{2,50},{3,51},{4,52},{5,53},{6,54},{7,55},{8,56},{9,... | collective-permute-start | bytes 1966088 | tf_op jit(solution)/shard_map/ppermute | solution.py:284
  27.7 15.9 %all-to-all-start.1 = ((bf16[32,64,128]{2,1,0:T(8,128)(2,1)}), bf16[32,64,128]{2,1,0:T(8,128)(2,1)S(1)}, u32[]{:S(2)}, u32[]{:S(2)}) async-start(bf16[32,64,128]{2,1,0:T(8,128)(2,1)} %pack_q.1), calls=%async_computation.1 | async-start | bytes 1048576 | tf_op jit(solution)/shard_map/all_to_all | solution.py:292
  32.2 18.1 %collective-permute-start.6 = (bf16[32,80,128]{2,1,0:T(8,128)(2,1)S(1)}, bf16[32,80,128]{2,1,0:T(8,128)(2,1)}, u32[]{:S(2)}, u32[]{:S(2)}) collective-permute-start(bf16[32,80,128]{2,1,0:T(8,128)(2,1)S(1)} %all-to-all-done.refs_1_), channel_id=1, source_target_pairs={{0,1},{1,0},{2,3},{3,2},{4,5},{5,4},{6,7},{7,6},{8,9},{9,8},{10,11... | collective-permute-start | bytes 1966088 | tf_op jit(solution)/shard_map/ppermute | solution.py:284
  43.7 9.3 %copy-start.2 = (bf16[32,64,128]{2,1,0:T(8,128)(2,1)}, bf16[32,64,128]{2,1,0:T(8,128)(2,1)S(1)}, u32[]{:S(2)}) copy-start(bf16[32,64,128]{2,1,0:T(8,128)(2,1)S(1)} %all-to-all-done.1.refs_0_) | copy-start | bytes 1572868
  43.7 9.3 %copy-start.5 = (bf16[32,80,128]{2,1,0:T(8,128)(2,1)}, bf16[32,80,128]{2,1,0:T(8,128)(2,1)S(1)}, u32[]{:S(2)}) copy-start(bf16[32,80,128]{2,1,0:T(8,128)(2,1)S(1)} %collective-permute-done.refs_3_) | copy-start | bytes 1966084
  43.7 9.3 %copy-start.6 = (bf16[32,80,128]{2,1,0:T(8,128)(2,1)}, bf16[32,80,128]{2,1,0:T(8,128)(2,1)S(1)}, u32[]{:S(2)}) copy-start(bf16[32,80,128]{2,1,0:T(8,128)(2,1)S(1)} %collective-permute-done.1.refs_5_) | copy-start | bytes 1966084
  43.7 7.0 %collective-permute-start.7 = (bf16[32,80,128]{2,1,0:T(8,128)(2,1)S(1)}, bf16[32,80,128]{2,1,0:T(8,128)(2,1)}, u32[]{:S(2)}, u32[]{:S(2)}) collective-permute-start(bf16[32,80,128]{2,1,0:T(8,128)(2,1)S(1)} %collective-permute-done.refs_3_), channel_id=1, source_target_pairs={{0,1},{1,0},{2,3},{3,2},{4,5},{5,4},{6,7},{7,6},{8,9},{9,8},{10,11... | collective-permute-start | bytes 1966088 | tf_op jit(solution)/shard_map/ppermute | solution.py:284
  44.1 8.9 %collective-permute-start.8 = (bf16[32,80,128]{2,1,0:T(8,128)(2,1)S(1)}, bf16[32,80,128]{2,1,0:T(8,128)(2,1)}, u32[]{:S(2)}, u32[]{:S(2)}) collective-permute-start(bf16[32,80,128]{2,1,0:T(8,128)(2,1)S(1)} %collective-permute-done.1.refs_5_), channel_id=1, source_target_pairs={{0,1},{1,0},{2,3},{3,2},{4,5},{5,4},{6,7},{7,6},{8,9},{9,8},{10,11... | collective-permute-start | bytes 1966088 | tf_op jit(solution)/shard_map/ppermute | solution.py:284
  44.3 33.9 %collective-permute-start.4 = (bf16[64,2048]{1,0:T(8,128)(2,1)S(1)}, bf16[64,2048]{1,0:T(8,128)(2,1)S(1)}, u32[]{:S(2)}, u32[]{:S(2)}) collective-permute-start(bf16[64,2048]{1,0:T(8,128)(2,1)S(1)} %pad_maximum_fusion.1), channel_id=1, source_target_pairs={{0,4},{1,5},{2,6},{3,7},{4,8},{5,9},{6,10},{7,11},{8,12},{9,13},{1... | collective-permute-start | bytes 786440 | tf_op jit(solution)/shard_map/ppermute | solution.py:284
  46.2 32.1 %collective-permute-start.5 = (bf16[64,2048]{1,0:T(8,128)(2,1)S(1)}, bf16[64,2048]{1,0:T(8,128)(2,1)S(1)}, u32[]{:S(2)}, u32[]{:S(2)}) collective-permute-start(bf16[64,2048]{1,0:T(8,128)(2,1)S(1)} %pad_maximum_fusion.1), channel_id=1, source_target_pairs={{0,8},{1,9},{2,10},{3,11},{4,12},{5,13},{6,14},{7,15},{8,16},{9,17... | collective-permute-start | bytes 786440 | tf_op jit(solution)/shard_map/ppermute | solution.py:284
  50.3 28.0 %collective-permute-start.2 = (bf16[16,80,128]{2,1,0:T(8,128)(2,1)S(1)}, bf16[16,80,128]{2,1,0:T(8,128)(2,1)S(1)}, u32[]{:S(2)}, u32[]{:S(2)}) collective-permute-start(bf16[16,80,128]{2,1,0:T(8,128)(2,1)S(1)} %slice.6), channel_id=1, source_target_pairs={{0,16},{1,17},{2,18},{3,19},{4,20},{5,21},{6,22},{7,23},{8,24},{9,... | collective-permute-start | bytes 983048 | tf_op jit(solution)/shard_map/ppermute | solution.py:284
  50.7 27.6 %collective-permute-start.3 = (bf16[16,80,128]{2,1,0:T(8,128)(2,1)S(1)}, bf16[16,80,128]{2,1,0:T(8,128)(2,1)S(1)}, u32[]{:S(2)}, u32[]{:S(2)}) collective-permute-start(bf16[16,80,128]{2,1,0:T(8,128)(2,1)S(1)} %slice.7), channel_id=1, source_target_pairs={{0,48},{1,49},{2,50},{3,51},{4,52},{5,53},{6,54},{7,55},{8,56},{9,... | collective-permute-start | bytes 983048 | tf_op jit(solution)/shard_map/ppermute | solution.py:284
  78.3 4.6 %copy-start.12 = (bf16[16,80,128]{2,1,0:T(8,128)(2,1)}, bf16[16,80,128]{2,1,0:T(8,128)(2,1)S(1)}, u32[]{:S(2)}) copy-start(bf16[16,80,128]{2,1,0:T(8,128)(2,1)S(1)} %collective-permute-done.2.refs_1_) | copy-start | bytes 983044
  78.3 4.6 %copy-start.13 = (bf16[16,80,128]{2,1,0:T(8,128)(2,1)}, bf16[16,80,128]{2,1,0:T(8,128)(2,1)S(1)}, u32[]{:S(2)}) copy-start(bf16[16,80,128]{2,1,0:T(8,128)(2,1)S(1)} %collective-permute-done.3.refs_3_) | copy-start | bytes 983044
  78.4 16.7 %copy-start.7 = (bf16[192,2048]{1,0:T(8,128)(2,1)}, bf16[192,2048]{1,0:T(8,128)(2,1)S(1)}, u32[]{:S(2)}) copy-start(bf16[192,2048]{1,0:T(8,128)(2,1)S(1)} %get-tuple-element.37.refs_0_) | copy-start | bytes 2359300
  78.4 17.2 %collective-permute-start.10 = (bf16[192,2048]{1,0:T(8,128)(2,1)S(1)}, bf16[192,2048]{1,0:T(8,128)(2,1)S(1)}, u32[]{:S(2)}, u32[]{:S(2)}) collective-permute-start(bf16[192,2048]{1,0:T(8,128)(2,1)S(1)} %get-tuple-element.37.refs_0_), channel_id=1, source_target_pairs={{0,1},{1,0},{2,3},{3,2},{4,5},{5,4},{6,7},{7,6},{8,9},{9,8},{10,11... | collective-permute-start | bytes 2359304 | tf_op jit(solution)/shard_map/ppermute | solution.py:284
  80.0 2.4 %collective-permute-start.11 = (bf16[16,80,128]{2,1,0:T(8,128)(2,1)S(1)}, bf16[16,80,128]{2,1,0:T(8,128)(2,1)S(1)}, u32[]{:S(2)}, u32[]{:S(2)}) collective-permute-start(bf16[16,80,128]{2,1,0:T(8,128)(2,1)S(1)} %collective-permute-done.2.refs_1_), channel_id=1, source_target_pairs={{0,1},{1,0},{2,3},{3,2},{4,5},{5,4},{6,7},{7,6},{8,9},{9,8},{10,11... | collective-permute-start | bytes 983048 | tf_op jit(solution)/shard_map/ppermute | solution.py:284
  80.1 2.8 %collective-permute-start.12 = (bf16[16,80,128]{2,1,0:T(8,128)(2,1)S(1)}, bf16[16,80,128]{2,1,0:T(8,128)(2,1)S(1)}, u32[]{:S(2)}, u32[]{:S(2)}) collective-permute-start(bf16[16,80,128]{2,1,0:T(8,128)(2,1)S(1)} %collective-permute-done.3.refs_3_), channel_id=1, source_target_pairs={{0,1},{1,0},{2,3},{3,2},{4,5},{5,4},{6,7},{7,6},{8,9},{9,8},{10,11... | collective-permute-start | bytes 983048 | tf_op jit(solution)/shard_map/ppermute | solution.py:284
  80.6 15.1 %collective-permute-start.9 = (bf16[128,2048]{1,0:T(8,128)(2,1)S(1)}, bf16[128,2048]{1,0:T(8,128)(2,1)S(1)}, u32[]{:S(2)}, u32[]{:S(2)}) collective-permute-start(bf16[128,2048]{1,0:T(8,128)(2,1)S(1)} %pad_maximum_fusion), channel_id=1, source_target_pairs={{0,2},{1,3},{2,0},{3,1},{4,6},{5,7},{6,4},{7,5},{8,10},{9,11},{10,... | collective-permute-start | bytes 1572872 | tf_op jit(solution)/shard_map/ppermute | solution.py:284
  82.4 0.7 copy-start.14
  83.1 0.7 copy-start.15
  95.6 6.2 %copy-start.10 = (bf16[128,2048]{1,0:T(8,128)(2,1)}, bf16[128,2048]{1,0:T(8,128)(2,1)S(1)}, u32[]{:S(2)}) copy-start(bf16[128,2048]{1,0:T(8,128)(2,1)S(1)} %collective-permute-done.9.refs_1_) | copy-start | bytes 1572868
  95.6 6.2 %copy-start.9 = (bf16[192,2048]{1,0:T(8,128)(2,1)}, bf16[192,2048]{1,0:T(8,128)(2,1)S(1)}, u32[]{:S(2)}) copy-start(bf16[192,2048]{1,0:T(8,128)(2,1)S(1)} %collective-permute-done.10.refs_2_) | copy-start | bytes 2359300
  95.6 6.2 %collective-permute-start.13 = (bf16[128,2048]{1,0:T(8,128)(2,1)S(1)}, bf16[128,2048]{1,0:T(8,128)(2,1)S(1)}, u32[]{:S(2)}, u32[]{:S(2)}) collective-permute-start(bf16[128,2048]{1,0:T(8,128)(2,1)S(1)} %collective-permute-done.9.refs_1_), channel_id=1, source_target_pairs={{0,1},{1,0},{2,3},{3,2},{4,5},{5,4},{6,7},{7,6},{8,9},{9,8},{10,11... | collective-permute-start | bytes 1572872 | tf_op jit(solution)/shard_map/ppermute | solution.py:284
  96.6 19.8 %all-to-all-start.2 = ((bf16[32,64,128]{2,1,0:T(8,128)(2,1)}), bf16[32,64,128]{2,1,0:T(8,128)(2,1)S(1)}, u32[]{:S(2)}, u32[]{:S(2)}) async-start(bf16[32,64,128]{2,1,0:T(8,128)(2,1)} %bitcast.2), calls=%async_computation.2 | async-start | bytes 1048576 | tf_op jit(solution)/shard_map/all_to_all | solution.py:292
  101.8 0.8 copy-start.11
  116.4 0.8 copy-start

commit v5 on v4

--- a/solution.py
+++ b/solution.py
@@ -59,13 +59,6 @@
         for h in range(HEADS):
             g = head_of(d, h)
             out_ref[d, h * NT : (h + 1) * NT, :] = q_ref[:, g * HD : (g + 1) * HD]
-
-
-def unpack_out(blk_ref, out_ref):
-    for d in range(PEERS):
-        for h in range(HEADS):
-            g = head_of(d, h)
-            out_ref[:, g * HD : (g + 1) * HD] = blk_ref[d, h * NT : (h + 1) * NT, :]
 
 
 RB, KT = 512, 512
@@ -341,15 +334,8 @@
     new_blocks = exchange(out_rows.reshape(PEERS, HEADS * NT, HD))
     pass_out = passages(passage_q, start, wins)
     pass_out, new_blocks = together(pass_out, new_blocks)
-    new_out = pl.pallas_call(
-        unpack_out,
-        out_shape=shape((NT, QH * HD), BF),
-        in_specs=[VM],
-        out_specs=VM,
-        compiler_params=params(),
-        name="unpack_out",
-    )(new_blocks)
-
+    new_out = new_blocks.reshape(2, KVH, 2, HEADS, NT, HD).transpose(4, 1, 0, 2, 3, 5)
+    new_out = new_out.reshape(NT, QH * HD)
     return pass_out, new_out
 
 

time: 120 us -> 118 us (0.983)
  Pallas kernels: 56 us -> 54.1 us
    pallas_call x1 -> x0, Pallas kernels: 1.92 us -> none  [on_device(): pl.pallas_call(unpack_out, out_shape=shape((NT, QH * HD), BF), in_specs=[...]
    reshape x0 -> x2, local copies, waits for them, and re-layouts: none -> 1.44 us  [the longest x1 1.19 us: on_device(): new_out = new_out.reshape(NT, QH * HD)]
    unnamed x34 -> x32, local copies, waits for them, and re-layouts: 2.66 us -> 1.88 us
where the time goes in v5:
time: 118 us
  Pallas kernels  54.1 us (46%)
  starting transfers between devices  35 us (30%)
  waiting for transfers between devices  23.3 us (20%)
  local copies, waits for them, and re-layouts  4.21 us (4%)
    pallas_call x2, Pallas kernels, ask(): pl.pallas_call(functools.partial(question, kinds, state is None, last), o...  36.5 us
    all_to_all x3, waiting for transfers between devices, exchange(): lax.all_to_all(blocks, BOTH, split_axis=0, concat_axis=0, tiled=True, axi...  21.7 us
    all_to_all x3, starting transfers between devices, exchange(): lax.all_to_all(blocks, BOTH, split_axis=0, concat_axis=0, tiled=True, axi...  18.5 us
    ppermute x14, starting transfers between devices, permute(): return lax.ppermute(block, BOTH, route)  16.5 us
    pallas_call x1, Pallas kernels, passages(): pl.pallas_call(passage, out_shape=jax.ShapeDtypeStruct((PT, QH * HD), BF)...  13.7 us
    pallas_call x2, Pallas kernels, packed(): pl.pallas_call(kernel, out_shape=shape((PEERS, rows, HD), BF), in_specs=[...  3.87 us
  transfers between devices with their start and end apart: 17, of which 5 were waited for; matrix products, arithmetic and copies ran while one was open for 1% of the time, Pallas kernels for 44%

profile of v5, /device:TPU:1, one launch (start us, length us, event | category | flops | bytes accessed | tf_op | source)
XLA Modules:
  0.0 117.8 jit_solution(16049835083362660417)
XLA Ops:
  0.7 1.9 %pack_kv.1 = bf16[32,80,128]{2,1,0:T(8,128)(2,1)} custom-call(bf16[64,1024]{1,0:T(8,128)(2,1)} %k_ref.1, bf16[64,1024]{1,0:T(8,128)(2,1)} %v_ref.1, bf16[16,1024]{1,0:T(8,128)(2,1)} %nk_ref.1, bf16[16,1024]{1,0:T(8,128)(2,1)} %nv_ref.1), custom_call_target="tpu_custom_call" | custom-call | tf_op jit(solution)/shard_map/pack_kv/pallas_call | solution.py:296
  2.6 9.6 %all-to-all-start = ((bf16[32,80,128]{2,1,0:T(8,128)(2,1)}), bf16[32,80,128]{2,1,0:T(8,128)(2,1)S(1)}, u32[]{:S(2)}, u32[]{:S(2)}) async-start(bf16[32,80,128]{2,1,0:T(8,128)(2,1)} %pack_kv.1), calls=%async_computation | async-start | bytes 1310720 | tf_op jit(solution)/shard_map/all_to_all | solution.py:285
  12.2 1.9 %pack_q.1 = bf16[32,64,128]{2,1,0:T(8,128)(2,1)} custom-call(bf16[16,16384]{1,0:T(8,128)(2,1)} %q_ref.2), custom_call_target="tpu_custom_call" | custom-call | tf_op jit(solution)/shard_map/pack_q/pallas_call | solution.py:296
  14.2 0.1 dynamic_slice.7
  14.2 0.1 pad_dynamic-slice_fusion
  14.3 0.2 convert_reduce_fusion
  14.5 10.5 %all-to-all-done.refs_1_ = bf16[32,80,128]{2,1,0:T(8,128)(2,1)S(1)} async-done(((bf16[32,80,128]{2,1,0:T(8,128)(2,1)}), bf16[32,80,128]{2,1,0:T(8,128)(2,1)S(1)}, u32[]{:S(2)}, u32[]{:S(2)}) %all-to-all-start) | async-done | bytes 655392 | tf_op jit(solution)/shard_map/all_to_all | solution.py:285
  25.1 1.2 %collective-permute-start = (bf16[32,80,128]{2,1,0:T(8,128)(2,1)S(1)}, bf16[32,80,128]{2,1,0:T(8,128)(2,1)S(1)}, u32[]{:S(2)}, u32[]{:S(2)}) collective-permute-start(bf16[32,80,128]{2,1,0:T(8,128)(2,1)S(1)} %all-to-all-done.refs_1_), channel_id=1, source_target_pairs={{0,16},{1,17},{2,18},{3,19},{4,20},{5,21},{6,22},{7,23},{8,24},{9,... | collective-permute-start | bytes 1966088 | tf_op jit(solution)/shard_map/ppermute | solution.py:277
  26.3 1.5 %collective-permute-start.1 = (bf16[32,80,128]{2,1,0:T(8,128)(2,1)S(1)}, bf16[32,80,128]{2,1,0:T(8,128)(2,1)S(1)}, u32[]{:S(2)}, u32[]{:S(2)}) collective-permute-start(bf16[32,80,128]{2,1,0:T(8,128)(2,1)S(1)} %all-to-all-done.refs_1_), channel_id=1, source_target_pairs={{0,48},{1,49},{2,50},{3,51},{4,52},{5,53},{6,54},{7,55},{8,56},{9,... | collective-permute-start | bytes 1966088 | tf_op jit(solution)/shard_map/ppermute | solution.py:277
  27.7 4.4 %all-to-all-start.1 = ((bf16[32,64,128]{2,1,0:T(8,128)(2,1)}), bf16[32,64,128]{2,1,0:T(8,128)(2,1)S(1)}, u32[]{:S(2)}, u32[]{:S(2)}) async-start(bf16[32,64,128]{2,1,0:T(8,128)(2,1)} %pack_q.1), calls=%async_computation.1 | async-start | bytes 1048576 | tf_op jit(solution)/shard_map/all_to_all | solution.py:285
  32.2 0.4 collective-permute-start.6
  32.6 11.1 %all-to-all-done.1.refs_0_ = bf16[32,64,128]{2,1,0:T(8,128)(2,1)S(1)} async-done(((bf16[32,64,128]{2,1,0:T(8,128)(2,1)}), bf16[32,64,128]{2,1,0:T(8,128)(2,1)S(1)}, u32[]{:S(2)}, u32[]{:S(2)}) %all-to-all-start.1) | async-done | bytes 524320 | tf_op jit(solution)/shard_map/all_to_all | solution.py:285
  43.7 0.0 collective-permute-done.refs_3_
  43.7 0.0 collective-permute-done.1.refs_5_
  43.7 0.4 collective-permute-start.7
  44.1 0.2 collective-permute-start.8
  44.3 1.9 %collective-permute-start.4 = (bf16[64,2048]{1,0:T(8,128)(2,1)S(1)}, bf16[64,2048]{1,0:T(8,128)(2,1)S(1)}, u32[]{:S(2)}, u32[]{:S(2)}) collective-permute-start(bf16[64,2048]{1,0:T(8,128)(2,1)S(1)} %pad_maximum_fusion.1), channel_id=1, source_target_pairs={{0,4},{1,5},{2,6},{3,7},{4,8},{5,9},{6,10},{7,11},{8,12},{9,13},{1... | collective-permute-start | bytes 786440 | tf_op jit(solution)/shard_map/ppermute | solution.py:277
  46.2 4.0 %collective-permute-start.5 = (bf16[64,2048]{1,0:T(8,128)(2,1)S(1)}, bf16[64,2048]{1,0:T(8,128)(2,1)S(1)}, u32[]{:S(2)}, u32[]{:S(2)}) collective-permute-start(bf16[64,2048]{1,0:T(8,128)(2,1)S(1)} %pad_maximum_fusion.1), channel_id=1, source_target_pairs={{0,8},{1,9},{2,10},{3,11},{4,12},{5,13},{6,14},{7,15},{8,16},{9,17... | collective-permute-start | bytes 786440 | tf_op jit(solution)/shard_map/ppermute | solution.py:277
  50.3 0.0 collective-permute-done.6.refs_2_
  50.3 0.4 collective-permute-start.2
  50.7 0.0 collective-permute-done.7.refs_4_
  50.7 2.3 %collective-permute-start.3 = (bf16[16,80,128]{2,1,0:T(8,128)(2,1)S(1)}, bf16[16,80,128]{2,1,0:T(8,128)(2,1)S(1)}, u32[]{:S(2)}, u32[]{:S(2)}) collective-permute-start(bf16[16,80,128]{2,1,0:T(8,128)(2,1)S(1)} %slice.7), channel_id=1, source_target_pairs={{0,48},{1,49},{2,50},{3,51},{4,52},{5,53},{6,54},{7,55},{8,56},{9,... | collective-permute-start | bytes 983048 | tf_op jit(solution)/shard_map/ppermute | solution.py:277
  53.0 0.0 collective-permute-done.8.refs_6_
  53.1 25.2 %question.2.refs_5_ = f32[2048,256]{1,0:T(8,128)} custom-call(bf16[32,64,128]{2,1,0:T(8,128)(2,1)} %copy-done.1, bf16[32,80,128]{2,1,0:T(8,128)(2,1)} %copy-done, bf16[32,80,128]{2,1,0:T(8,128)(2,1)} %collective-permute-done.6.refs_2_, bf16[32,80,128]{2,1,0:T(8,128)(2,1)} %copy-done.4, bf16[32,80,128]{2,1,0:T(8,128)(2,1)} %collective-permute-done.7.refs_4_, ...), custom_call_target="tpu_custom_call" | custom-call | flops 12079595520 | bytes 4194304 | tf_op jit(solution)/shard_map/question/pallas_call | solution.py:197
  78.3 0.0 collective-permute-done.4
  78.3 0.0 collective-permute-done.5
  78.3 0.0 collective-permute-done.2.refs_1_
  78.3 0.0 collective-permute-done.3.refs_3_
  78.3 0.1 broadcast_select_fusion
  78.4 1.6 %collective-permute-start.10 = (bf16[192,2048]{1,0:T(8,128)(2,1)S(1)}, bf16[192,2048]{1,0:T(8,128)(2,1)S(1)}, u32[]{:S(2)}, u32[]{:S(2)}) collective-permute-start(bf16[192,2048]{1,0:T(8,128)(2,1)S(1)} %get-tuple-element.37.refs_0_), channel_id=1, source_target_pairs={{0,1},{1,0},{2,3},{3,2},{4,5},{5,4},{6,7},{7,6},{8,9},{9,8},{10,11... | collective-permute-start | bytes 2359304 | tf_op jit(solution)/shard_map/ppermute | solution.py:277
  80.0 0.1 collective-permute-start.11
  80.1 0.4 collective-permute-start.12
  80.6 1.1 collective-permute-start.9
  81.7 0.7 collective-permute-done.11.refs_2_
  82.4 0.5 collective-permute-done.12.refs_4_
  82.9 0.3 copy-done.13
  83.1 0.7 copy-done.14
  83.9 11.3 %question.3 = bf16[2048,128]{1,0:T(8,128)(2,1)} custom-call(bf16[32,64,128]{2,1,0:T(8,128)(2,1)} %copy-done.1, bf16[16,80,128]{2,1,0:T(8,128)(2,1)} %copy-done.11, bf16[16,80,128]{2,1,0:T(8,128)(2,1)} %copy-done.13, bf16[16,80,128]{2,1,0:T(8,128)(2,1)} %copy-done.12, bf16[16,80,128]{2,1,0:T(8,128)(2,1)} %copy-done.14, f32[2048,256]{1,0:T(8,128)} %question.2.refs_5_), custom_call_target="tpu_custom_call" | custom-call | flops 4026531840 | bytes 4194304 | tf_op jit(solution)/shard_map/question/pallas_call | solution.py:197
  95.1 0.5 collective-permute-done.9.refs_1_
  95.6 0.0 collective-permute-done.10.refs_2_
  95.6 0.9 collective-permute-start.13
  96.6 4.5 %all-to-all-start.2 = ((bf16[32,64,128]{2,1,0:T(8,128)(2,1)}), bf16[32,64,128]{2,1,0:T(8,128)(2,1)S(1)}, u32[]{:S(2)}, u32[]{:S(2)}) async-start(bf16[32,64,128]{2,1,0:T(8,128)(2,1)} %bitcast.8), calls=%async_computation.2 | async-start | bytes 1048576 | tf_op jit(solution)/shard_map/all_to_all | solution.py:285
  101.1 0.7 copy.11.start_ref
  101.8 0.0 collective-permute-done.13.refs_3_
  101.9 0.8 copy-done.10
  102.7 13.7 %passage.1 = bf16[64,16384]{1,0:T(8,128)(2,1)} custom-call(bf16[64,16384]{1,0:T(8,128)(2,1)} %q_ref.3, s32[64,1]{1,0:T(8,128)} %copy.11.start_ref, bf16[192,2048]{1,0:T(8,128)(2,1)} %copy-done.6, bf16[128,2048]{1,0:T(8,128)(2,1)} %copy-done.9, bf16[192,2048]{1,0:T(8,128)(2,1)} %copy-done.8, bf16[128,2048]{1,0:T(8,128)(2,1)} %copy-done.10), custom_call_target="tpu_custom_call" | custom-call | flops 4026531840 | bytes 7340032 | tf_op jit(solution)/shard_map/passage/pallas_call | solution.py:258
  116.4 0.2 copy.14
  116.7 1.2 %reshape.17 = bf16[16,16384]{1,0:T(8,128)(2,1)} reshape(bf16[16,8,2,2,4,128]{5,4,3,2,1,0:T(4,128)(2,1)S(1)} %bitcast.7) | data formatting | bytes 1048576 | tf_op jit(solution)/shard_map/reshape | solution.py:338
  (34 shorter events, 0.2 us)
Async XLA Ops:
  0.6 13.9 %copy-start.3 = (bf16[64,1024]{1,0:T(8,128)(2,1)S(1)}, bf16[64,1024]{1,0:T(8,128)(2,1)}, u32[]{:S(2)}) copy-start(bf16[64,1024]{1,0:T(8,128)(2,1)} %k_ref.1) | copy-start | bytes 393220
  0.6 13.9 %copy-start.2 = (bf16[64,1024]{1,0:T(8,128)(2,1)S(1)}, bf16[64,1024]{1,0:T(8,128)(2,1)}, u32[]{:S(2)}) copy-start(bf16[64,1024]{1,0:T(8,128)(2,1)} %v_ref.1) | copy-start | bytes 393220
  0.7 13.5 %copy-start.7 = (s32[8192]{0:T(1024)S(1)}, s32[8192]{0:T(1024)}, u32[]{:S(2)}) copy-start(s32[8192]{0:T(1024)} %param.13) | copy-start | bytes 98308
  2.6 22.5 %all-to-all-start = ((bf16[32,80,128]{2,1,0:T(8,128)(2,1)}), bf16[32,80,128]{2,1,0:T(8,128)(2,1)S(1)}, u32[]{:S(2)}, u32[]{:S(2)}) async-start(bf16[32,80,128]{2,1,0:T(8,128)(2,1)} %pack_kv.1), calls=%async_computation | async-start | bytes 1310720 | tf_op jit(solution)/shard_map/all_to_all | solution.py:285
  25.1 28.0 %copy-start = (bf16[32,80,128]{2,1,0:T(8,128)(2,1)}, bf16[32,80,128]{2,1,0:T(8,128)(2,1)S(1)}, u32[]{:S(2)}) copy-start(bf16[32,80,128]{2,1,0:T(8,128)(2,1)S(1)} %all-to-all-done.refs_1_) | copy-start | bytes 1966084
  25.1 18.6 %collective-permute-start = (bf16[32,80,128]{2,1,0:T(8,128)(2,1)S(1)}, bf16[32,80,128]{2,1,0:T(8,128)(2,1)S(1)}, u32[]{:S(2)}, u32[]{:S(2)}) collective-permute-start(bf16[32,80,128]{2,1,0:T(8,128)(2,1)S(1)} %all-to-all-done.refs_1_), channel_id=1, source_target_pairs={{0,16},{1,17},{2,18},{3,19},{4,20},{5,21},{6,22},{7,23},{8,24},{9,... | collective-permute-start | bytes 1966088 | tf_op jit(solution)/shard_map/ppermute | solution.py:277
  26.3 17.4 %collective-permute-start.1 = (bf16[32,80,128]{2,1,0:T(8,128)(2,1)S(1)}, bf16[32,80,128]{2,1,0:T(8,128)(2,1)S(1)}, u32[]{:S(2)}, u32[]{:S(2)}) collective-permute-start(bf16[32,80,128]{2,1,0:T(8,128)(2,1)S(1)} %all-to-all-done.refs_1_), channel_id=1, source_target_pairs={{0,48},{1,49},{2,50},{3,51},{4,52},{5,53},{6,54},{7,55},{8,56},{9,... | collective-permute-start | bytes 1966088 | tf_op jit(solution)/shard_map/ppermute | solution.py:277
  27.7 15.9 %all-to-all-start.1 = ((bf16[32,64,128]{2,1,0:T(8,128)(2,1)}), bf16[32,64,128]{2,1,0:T(8,128)(2,1)S(1)}, u32[]{:S(2)}, u32[]{:S(2)}) async-start(bf16[32,64,128]{2,1,0:T(8,128)(2,1)} %pack_q.1), calls=%async_computation.1 | async-start | bytes 1048576 | tf_op jit(solution)/shard_map/all_to_all | solution.py:285
  32.2 18.1 %collective-permute-start.6 = (bf16[32,80,128]{2,1,0:T(8,128)(2,1)S(1)}, bf16[32,80,128]{2,1,0:T(8,128)(2,1)}, u32[]{:S(2)}, u32[]{:S(2)}) collective-permute-start(bf16[32,80,128]{2,1,0:T(8,128)(2,1)S(1)} %all-to-all-done.refs_1_), channel_id=1, source_target_pairs={{0,1},{1,0},{2,3},{3,2},{4,5},{5,4},{6,7},{7,6},{8,9},{9,8},{10,11... | collective-permute-start | bytes 1966088 | tf_op jit(solution)/shard_map/ppermute | solution.py:277
  43.7 9.3 %copy-start.1 = (bf16[32,64,128]{2,1,0:T(8,128)(2,1)}, bf16[32,64,128]{2,1,0:T(8,128)(2,1)S(1)}, u32[]{:S(2)}) copy-start(bf16[32,64,128]{2,1,0:T(8,128)(2,1)S(1)} %all-to-all-done.1.refs_0_) | copy-start | bytes 1572868
  43.7 9.3 %copy-start.4 = (bf16[32,80,128]{2,1,0:T(8,128)(2,1)}, bf16[32,80,128]{2,1,0:T(8,128)(2,1)S(1)}, u32[]{:S(2)}) copy-start(bf16[32,80,128]{2,1,0:T(8,128)(2,1)S(1)} %collective-permute-done.refs_3_) | copy-start | bytes 1966084
  43.7 9.3 %copy-start.5 = (bf16[32,80,128]{2,1,0:T(8,128)(2,1)}, bf16[32,80,128]{2,1,0:T(8,128)(2,1)S(1)}, u32[]{:S(2)}) copy-start(bf16[32,80,128]{2,1,0:T(8,128)(2,1)S(1)} %collective-permute-done.1.refs_5_) | copy-start | bytes 1966084
  43.7 7.0 %collective-permute-start.7 = (bf16[32,80,128]{2,1,0:T(8,128)(2,1)S(1)}, bf16[32,80,128]{2,1,0:T(8,128)(2,1)}, u32[]{:S(2)}, u32[]{:S(2)}) collective-permute-start(bf16[32,80,128]{2,1,0:T(8,128)(2,1)S(1)} %collective-permute-done.refs_3_), channel_id=1, source_target_pairs={{0,1},{1,0},{2,3},{3,2},{4,5},{5,4},{6,7},{7,6},{8,9},{9,8},{10,11... | collective-permute-start | bytes 1966088 | tf_op jit(solution)/shard_map/ppermute | solution.py:277
  44.1 8.9 %collective-permute-start.8 = (bf16[32,80,128]{2,1,0:T(8,128)(2,1)S(1)}, bf16[32,80,128]{2,1,0:T(8,128)(2,1)}, u32[]{:S(2)}, u32[]{:S(2)}) collective-permute-start(bf16[32,80,128]{2,1,0:T(8,128)(2,1)S(1)} %collective-permute-done.1.refs_5_), channel_id=1, source_target_pairs={{0,1},{1,0},{2,3},{3,2},{4,5},{5,4},{6,7},{7,6},{8,9},{9,8},{10,11... | collective-permute-start | bytes 1966088 | tf_op jit(solution)/shard_map/ppermute | solution.py:277
  44.3 33.9 %collective-permute-start.4 = (bf16[64,2048]{1,0:T(8,128)(2,1)S(1)}, bf16[64,2048]{1,0:T(8,128)(2,1)S(1)}, u32[]{:S(2)}, u32[]{:S(2)}) collective-permute-start(bf16[64,2048]{1,0:T(8,128)(2,1)S(1)} %pad_maximum_fusion.1), channel_id=1, source_target_pairs={{0,4},{1,5},{2,6},{3,7},{4,8},{5,9},{6,10},{7,11},{8,12},{9,13},{1... | collective-permute-start | bytes 786440 | tf_op jit(solution)/shard_map/ppermute | solution.py:277
  46.2 32.1 %collective-permute-start.5 = (bf16[64,2048]{1,0:T(8,128)(2,1)S(1)}, bf16[64,2048]{1,0:T(8,128)(2,1)S(1)}, u32[]{:S(2)}, u32[]{:S(2)}) collective-permute-start(bf16[64,2048]{1,0:T(8,128)(2,1)S(1)} %pad_maximum_fusion.1), channel_id=1, source_target_pairs={{0,8},{1,9},{2,10},{3,11},{4,12},{5,13},{6,14},{7,15},{8,16},{9,17... | collective-permute-start | bytes 786440 | tf_op jit(solution)/shard_map/ppermute | solution.py:277
  50.3 28.0 %collective-permute-start.2 = (bf16[16,80,128]{2,1,0:T(8,128)(2,1)S(1)}, bf16[16,80,128]{2,1,0:T(8,128)(2,1)S(1)}, u32[]{:S(2)}, u32[]{:S(2)}) collective-permute-start(bf16[16,80,128]{2,1,0:T(8,128)(2,1)S(1)} %slice.6), channel_id=1, source_target_pairs={{0,16},{1,17},{2,18},{3,19},{4,20},{5,21},{6,22},{7,23},{8,24},{9,... | collective-permute-start | bytes 983048 | tf_op jit(solution)/shard_map/ppermute | solution.py:277
  50.7 27.6 %collective-permute-start.3 = (bf16[16,80,128]{2,1,0:T(8,128)(2,1)S(1)}, bf16[16,80,128]{2,1,0:T(8,128)(2,1)S(1)}, u32[]{:S(2)}, u32[]{:S(2)}) collective-permute-start(bf16[16,80,128]{2,1,0:T(8,128)(2,1)S(1)} %slice.7), channel_id=1, source_target_pairs={{0,48},{1,49},{2,50},{3,51},{4,52},{5,53},{6,54},{7,55},{8,56},{9,... | collective-permute-start | bytes 983048 | tf_op jit(solution)/shard_map/ppermute | solution.py:277
  78.3 4.6 %copy-start.11 = (bf16[16,80,128]{2,1,0:T(8,128)(2,1)}, bf16[16,80,128]{2,1,0:T(8,128)(2,1)S(1)}, u32[]{:S(2)}) copy-start(bf16[16,80,128]{2,1,0:T(8,128)(2,1)S(1)} %collective-permute-done.2.refs_1_) | copy-start | bytes 983044
  78.3 4.6 %copy-start.12 = (bf16[16,80,128]{2,1,0:T(8,128)(2,1)}, bf16[16,80,128]{2,1,0:T(8,128)(2,1)S(1)}, u32[]{:S(2)}) copy-start(bf16[16,80,128]{2,1,0:T(8,128)(2,1)S(1)} %collective-permute-done.3.refs_3_) | copy-start | bytes 983044
  78.4 16.7 %copy-start.6 = (bf16[192,2048]{1,0:T(8,128)(2,1)}, bf16[192,2048]{1,0:T(8,128)(2,1)S(1)}, u32[]{:S(2)}) copy-start(bf16[192,2048]{1,0:T(8,128)(2,1)S(1)} %get-tuple-element.37.refs_0_) | copy-start | bytes 2359300
  78.4 17.2 %collective-permute-start.10 = (bf16[192,2048]{1,0:T(8,128)(2,1)S(1)}, bf16[192,2048]{1,0:T(8,128)(2,1)S(1)}, u32[]{:S(2)}, u32[]{:S(2)}) collective-permute-start(bf16[192,2048]{1,0:T(8,128)(2,1)S(1)} %get-tuple-element.37.refs_0_), channel_id=1, source_target_pairs={{0,1},{1,0},{2,3},{3,2},{4,5},{5,4},{6,7},{7,6},{8,9},{9,8},{10,11... | collective-permute-start | bytes 2359304 | tf_op jit(solution)/shard_map/ppermute | solution.py:277
  80.0 2.4 %collective-permute-start.11 = (bf16[16,80,128]{2,1,0:T(8,128)(2,1)S(1)}, bf16[16,80,128]{2,1,0:T(8,128)(2,1)S(1)}, u32[]{:S(2)}, u32[]{:S(2)}) collective-permute-start(bf16[16,80,128]{2,1,0:T(8,128)(2,1)S(1)} %collective-permute-done.2.refs_1_), channel_id=1, source_target_pairs={{0,1},{1,0},{2,3},{3,2},{4,5},{5,4},{6,7},{7,6},{8,9},{9,8},{10,11... | collective-permute-start | bytes 983048 | tf_op jit(solution)/shard_map/ppermute | solution.py:277
  80.1 2.8 %collective-permute-start.12 = (bf16[16,80,128]{2,1,0:T(8,128)(2,1)S(1)}, bf16[16,80,128]{2,1,0:T(8,128)(2,1)S(1)}, u32[]{:S(2)}, u32[]{:S(2)}) collective-permute-start(bf16[16,80,128]{2,1,0:T(8,128)(2,1)S(1)} %collective-permute-done.3.refs_3_), channel_id=1, source_target_pairs={{0,1},{1,0},{2,3},{3,2},{4,5},{5,4},{6,7},{7,6},{8,9},{9,8},{10,11... | collective-permute-start | bytes 983048 | tf_op jit(solution)/shard_map/ppermute | solution.py:277
  80.6 15.1 %collective-permute-start.9 = (bf16[128,2048]{1,0:T(8,128)(2,1)S(1)}, bf16[128,2048]{1,0:T(8,128)(2,1)S(1)}, u32[]{:S(2)}, u32[]{:S(2)}) collective-permute-start(bf16[128,2048]{1,0:T(8,128)(2,1)S(1)} %pad_maximum_fusion), channel_id=1, source_target_pairs={{0,2},{1,3},{2,0},{3,1},{4,6},{5,7},{6,4},{7,5},{8,10},{9,11},{10,... | collective-permute-start | bytes 1572872 | tf_op jit(solution)/shard_map/ppermute | solution.py:277
  82.4 0.7 copy-start.13
  83.1 0.7 copy-start.14
  95.6 6.2 %copy-start.9 = (bf16[128,2048]{1,0:T(8,128)(2,1)}, bf16[128,2048]{1,0:T(8,128)(2,1)S(1)}, u32[]{:S(2)}) copy-start(bf16[128,2048]{1,0:T(8,128)(2,1)S(1)} %collective-permute-done.9.refs_1_) | copy-start | bytes 1572868
  95.6 6.2 %copy-start.8 = (bf16[192,2048]{1,0:T(8,128)(2,1)}, bf16[192,2048]{1,0:T(8,128)(2,1)S(1)}, u32[]{:S(2)}) copy-start(bf16[192,2048]{1,0:T(8,128)(2,1)S(1)} %collective-permute-done.10.refs_2_) | copy-start | bytes 2359300
  95.6 6.2 %collective-permute-start.13 = (bf16[128,2048]{1,0:T(8,128)(2,1)S(1)}, bf16[128,2048]{1,0:T(8,128)(2,1)S(1)}, u32[]{:S(2)}, u32[]{:S(2)}) collective-permute-start(bf16[128,2048]{1,0:T(8,128)(2,1)S(1)} %collective-permute-done.9.refs_1_), channel_id=1, source_target_pairs={{0,1},{1,0},{2,3},{3,2},{4,5},{5,4},{6,7},{7,6},{8,9},{9,8},{10,11... | collective-permute-start | bytes 1572872 | tf_op jit(solution)/shard_map/ppermute | solution.py:277
  96.6 19.8 %all-to-all-start.2 = ((bf16[32,64,128]{2,1,0:T(8,128)(2,1)}), bf16[32,64,128]{2,1,0:T(8,128)(2,1)S(1)}, u32[]{:S(2)}, u32[]{:S(2)}) async-start(bf16[32,64,128]{2,1,0:T(8,128)(2,1)} %bitcast.8), calls=%async_computation.2 | async-start | bytes 1048576 | tf_op jit(solution)/shard_map/all_to_all | solution.py:285
  101.8 0.8 copy-start.10

commit v6 on v5

--- a/solution.py
+++ b/solution.py
@@ -251,7 +251,7 @@
             for h in range(PART):
                 o_ref[:, columns(j * GROUP + part * PART + h)] = o[h * PT : (h + 1) * PT]
 
-    pipelined(3, PARTS, [(0, KVH, None)], stage)
+    pipelined(3, PARTS, [(0, KVH, None)], stage, 2)
 
 
 def passages(passage_q, start, wins):

time: 118 us -> 118 us (level)
  no operation moved by 1% of the time
where the time goes in v6:
time: 118 us
  Pallas kernels  53.9 us (46%)
  starting transfers between devices  35 us (30%)
  waiting for transfers between devices  23.3 us (20%)
  local copies, waits for them, and re-layouts  4.21 us (4%)
    pallas_call x2, Pallas kernels, ask(): pl.pallas_call(functools.partial(question, kinds, state is None, last), o...  36.5 us
    all_to_all x3, waiting for transfers between devices, exchange(): lax.all_to_all(blocks, BOTH, split_axis=0, concat_axis=0, tiled=True, axi...  21.7 us
    all_to_all x3, starting transfers between devices, exchange(): lax.all_to_all(blocks, BOTH, split_axis=0, concat_axis=0, tiled=True, axi...  18.5 us
    ppermute x14, starting transfers between devices, permute(): return lax.ppermute(block, BOTH, route)  16.5 us
    pallas_call x1, Pallas kernels, passages(): pl.pallas_call(passage, out_shape=jax.ShapeDtypeStruct((PT, QH * HD), BF)...  13.6 us
    pallas_call x2, Pallas kernels, packed(): pl.pallas_call(kernel, out_shape=shape((PEERS, rows, HD), BF), in_specs=[...  3.87 us
  transfers between devices with their start and end apart: 17, of which 5 were waited for; matrix products, arithmetic and copies ran while one was open for 1% of the time, Pallas kernels for 44%

profile of v6, /device:TPU:1, one launch (start us, length us, event | category | flops | bytes accessed | tf_op | source)
XLA Modules:
  0.0 117.7 jit_solution(4991415782271372529)
XLA Ops:
  0.7 1.9 %pack_kv.1 = bf16[32,80,128]{2,1,0:T(8,128)(2,1)} custom-call(bf16[64,1024]{1,0:T(8,128)(2,1)} %k_ref.1, bf16[64,1024]{1,0:T(8,128)(2,1)} %v_ref.1, bf16[16,1024]{1,0:T(8,128)(2,1)} %nk_ref.1, bf16[16,1024]{1,0:T(8,128)(2,1)} %nv_ref.1), custom_call_target="tpu_custom_call" | custom-call | tf_op jit(solution)/shard_map/pack_kv/pallas_call | solution.py:296
  2.6 9.6 %all-to-all-start = ((bf16[32,80,128]{2,1,0:T(8,128)(2,1)}), bf16[32,80,128]{2,1,0:T(8,128)(2,1)S(1)}, u32[]{:S(2)}, u32[]{:S(2)}) async-start(bf16[32,80,128]{2,1,0:T(8,128)(2,1)} %pack_kv.1), calls=%async_computation | async-start | bytes 1310720 | tf_op jit(solution)/shard_map/all_to_all | solution.py:285
  12.2 1.9 %pack_q.1 = bf16[32,64,128]{2,1,0:T(8,128)(2,1)} custom-call(bf16[16,16384]{1,0:T(8,128)(2,1)} %q_ref.2), custom_call_target="tpu_custom_call" | custom-call | tf_op jit(solution)/shard_map/pack_q/pallas_call | solution.py:296
  14.2 0.1 dynamic_slice.7
  14.2 0.1 pad_dynamic-slice_fusion
  14.3 0.2 convert_reduce_fusion
  14.5 10.5 %all-to-all-done.refs_1_ = bf16[32,80,128]{2,1,0:T(8,128)(2,1)S(1)} async-done(((bf16[32,80,128]{2,1,0:T(8,128)(2,1)}), bf16[32,80,128]{2,1,0:T(8,128)(2,1)S(1)}, u32[]{:S(2)}, u32[]{:S(2)}) %all-to-all-start) | async-done | bytes 655392 | tf_op jit(solution)/shard_map/all_to_all | solution.py:285
  25.1 1.2 %collective-permute-start = (bf16[32,80,128]{2,1,0:T(8,128)(2,1)S(1)}, bf16[32,80,128]{2,1,0:T(8,128)(2,1)S(1)}, u32[]{:S(2)}, u32[]{:S(2)}) collective-permute-start(bf16[32,80,128]{2,1,0:T(8,128)(2,1)S(1)} %all-to-all-done.refs_1_), channel_id=1, source_target_pairs={{0,16},{1,17},{2,18},{3,19},{4,20},{5,21},{6,22},{7,23},{8,24},{9,... | collective-permute-start | bytes 1966088 | tf_op jit(solution)/shard_map/ppermute | solution.py:277
  26.3 1.5 %collective-permute-start.1 = (bf16[32,80,128]{2,1,0:T(8,128)(2,1)S(1)}, bf16[32,80,128]{2,1,0:T(8,128)(2,1)S(1)}, u32[]{:S(2)}, u32[]{:S(2)}) collective-permute-start(bf16[32,80,128]{2,1,0:T(8,128)(2,1)S(1)} %all-to-all-done.refs_1_), channel_id=1, source_target_pairs={{0,48},{1,49},{2,50},{3,51},{4,52},{5,53},{6,54},{7,55},{8,56},{9,... | collective-permute-start | bytes 1966088 | tf_op jit(solution)/shard_map/ppermute | solution.py:277
  27.7 4.4 %all-to-all-start.1 = ((bf16[32,64,128]{2,1,0:T(8,128)(2,1)}), bf16[32,64,128]{2,1,0:T(8,128)(2,1)S(1)}, u32[]{:S(2)}, u32[]{:S(2)}) async-start(bf16[32,64,128]{2,1,0:T(8,128)(2,1)} %pack_q.1), calls=%async_computation.1 | async-start | bytes 1048576 | tf_op jit(solution)/shard_map/all_to_all | solution.py:285
  32.2 0.4 collective-permute-start.6
  32.6 11.1 %all-to-all-done.1.refs_0_ = bf16[32,64,128]{2,1,0:T(8,128)(2,1)S(1)} async-done(((bf16[32,64,128]{2,1,0:T(8,128)(2,1)}), bf16[32,64,128]{2,1,0:T(8,128)(2,1)S(1)}, u32[]{:S(2)}, u32[]{:S(2)}) %all-to-all-start.1) | async-done | bytes 524320 | tf_op jit(solution)/shard_map/all_to_all | solution.py:285
  43.7 0.0 collective-permute-done.refs_3_
  43.7 0.0 collective-permute-done.1.refs_5_
  43.7 0.4 collective-permute-start.7
  44.1 0.2 collective-permute-start.8
  44.3 1.9 %collective-permute-start.4 = (bf16[64,2048]{1,0:T(8,128)(2,1)S(1)}, bf16[64,2048]{1,0:T(8,128)(2,1)S(1)}, u32[]{:S(2)}, u32[]{:S(2)}) collective-permute-start(bf16[64,2048]{1,0:T(8,128)(2,1)S(1)} %pad_maximum_fusion.1), channel_id=1, source_target_pairs={{0,4},{1,5},{2,6},{3,7},{4,8},{5,9},{6,10},{7,11},{8,12},{9,13},{1... | collective-permute-start | bytes 786440 | tf_op jit(solution)/shard_map/ppermute | solution.py:277
  46.2 4.0 %collective-permute-start.5 = (bf16[64,2048]{1,0:T(8,128)(2,1)S(1)}, bf16[64,2048]{1,0:T(8,128)(2,1)S(1)}, u32[]{:S(2)}, u32[]{:S(2)}) collective-permute-start(bf16[64,2048]{1,0:T(8,128)(2,1)S(1)} %pad_maximum_fusion.1), channel_id=1, source_target_pairs={{0,8},{1,9},{2,10},{3,11},{4,12},{5,13},{6,14},{7,15},{8,16},{9,17... | collective-permute-start | bytes 786440 | tf_op jit(solution)/shard_map/ppermute | solution.py:277
  50.3 0.0 collective-permute-done.6.refs_2_
  50.3 0.4 collective-permute-start.2
  50.7 0.0 collective-permute-done.7.refs_4_
  50.7 2.3 %collective-permute-start.3 = (bf16[16,80,128]{2,1,0:T(8,128)(2,1)S(1)}, bf16[16,80,128]{2,1,0:T(8,128)(2,1)S(1)}, u32[]{:S(2)}, u32[]{:S(2)}) collective-permute-start(bf16[16,80,128]{2,1,0:T(8,128)(2,1)S(1)} %slice.7), channel_id=1, source_target_pairs={{0,48},{1,49},{2,50},{3,51},{4,52},{5,53},{6,54},{7,55},{8,56},{9,... | collective-permute-start | bytes 983048 | tf_op jit(solution)/shard_map/ppermute | solution.py:277
  53.0 0.0 collective-permute-done.8.refs_6_
  53.1 25.2 %question.2.refs_5_ = f32[2048,256]{1,0:T(8,128)} custom-call(bf16[32,64,128]{2,1,0:T(8,128)(2,1)} %copy-done.1, bf16[32,80,128]{2,1,0:T(8,128)(2,1)} %copy-done, bf16[32,80,128]{2,1,0:T(8,128)(2,1)} %collective-permute-done.6.refs_2_, bf16[32,80,128]{2,1,0:T(8,128)(2,1)} %copy-done.4, bf16[32,80,128]{2,1,0:T(8,128)(2,1)} %collective-permute-done.7.refs_4_, ...), custom_call_target="tpu_custom_call" | custom-call | flops 12079595520 | bytes 4194304 | tf_op jit(solution)/shard_map/question/pallas_call | solution.py:197
  78.3 0.0 collective-permute-done.4
  78.3 0.0 collective-permute-done.5
  78.3 0.0 collective-permute-done.2.refs_1_
  78.3 0.0 collective-permute-done.3.refs_3_
  78.3 0.1 broadcast_select_fusion
  78.4 1.6 %collective-permute-start.10 = (bf16[192,2048]{1,0:T(8,128)(2,1)S(1)}, bf16[192,2048]{1,0:T(8,128)(2,1)S(1)}, u32[]{:S(2)}, u32[]{:S(2)}) collective-permute-start(bf16[192,2048]{1,0:T(8,128)(2,1)S(1)} %get-tuple-element.37.refs_0_), channel_id=1, source_target_pairs={{0,1},{1,0},{2,3},{3,2},{4,5},{5,4},{6,7},{7,6},{8,9},{9,8},{10,11... | collective-permute-start | bytes 2359304 | tf_op jit(solution)/shard_map/ppermute | solution.py:277
  80.0 0.1 collective-permute-start.11
  80.1 0.4 collective-permute-start.12
  80.6 1.1 collective-permute-start.9
  81.7 0.7 collective-permute-done.11.refs_2_
  82.4 0.5 collective-permute-done.12.refs_4_
  82.9 0.3 copy-done.13
  83.1 0.7 copy-done.14
  83.9 11.3 %question.3 = bf16[2048,128]{1,0:T(8,128)(2,1)} custom-call(bf16[32,64,128]{2,1,0:T(8,128)(2,1)} %copy-done.1, bf16[16,80,128]{2,1,0:T(8,128)(2,1)} %copy-done.11, bf16[16,80,128]{2,1,0:T(8,128)(2,1)} %copy-done.13, bf16[16,80,128]{2,1,0:T(8,128)(2,1)} %copy-done.12, bf16[16,80,128]{2,1,0:T(8,128)(2,1)} %copy-done.14, f32[2048,256]{1,0:T(8,128)} %question.2.refs_5_), custom_call_target="tpu_custom_call" | custom-call | flops 4026531840 | bytes 4194304 | tf_op jit(solution)/shard_map/question/pallas_call | solution.py:197
  95.1 0.5 collective-permute-done.9.refs_1_
  95.6 0.0 collective-permute-done.10.refs_2_
  95.6 0.9 collective-permute-start.13
  96.6 4.5 %all-to-all-start.2 = ((bf16[32,64,128]{2,1,0:T(8,128)(2,1)}), bf16[32,64,128]{2,1,0:T(8,128)(2,1)S(1)}, u32[]{:S(2)}, u32[]{:S(2)}) async-start(bf16[32,64,128]{2,1,0:T(8,128)(2,1)} %bitcast.8), calls=%async_computation.2 | async-start | bytes 1048576 | tf_op jit(solution)/shard_map/all_to_all | solution.py:285
  101.1 0.7 copy.11.start_ref
  101.8 0.0 collective-permute-done.13.refs_3_
  101.9 0.8 copy-done.10
  102.7 13.6 %passage.1 = bf16[64,16384]{1,0:T(8,128)(2,1)} custom-call(bf16[64,16384]{1,0:T(8,128)(2,1)} %q_ref.3, s32[64,1]{1,0:T(8,128)} %copy.11.start_ref, bf16[192,2048]{1,0:T(8,128)(2,1)} %copy-done.6, bf16[128,2048]{1,0:T(8,128)(2,1)} %copy-done.9, bf16[192,2048]{1,0:T(8,128)(2,1)} %copy-done.8, bf16[128,2048]{1,0:T(8,128)(2,1)} %copy-done.10), custom_call_target="tpu_custom_call" | custom-call | flops 4026531840 | bytes 7340032 | tf_op jit(solution)/shard_map/passage/pallas_call | solution.py:258
  116.3 0.2 copy.14
  116.5 1.2 %reshape.17 = bf16[16,16384]{1,0:T(8,128)(2,1)} reshape(bf16[16,8,2,2,4,128]{5,4,3,2,1,0:T(4,128)(2,1)S(1)} %bitcast.7) | data formatting | bytes 1048576 | tf_op jit(solution)/shard_map/reshape | solution.py:338
  (34 shorter events, 0.2 us)
Async XLA Ops:
  0.6 13.9 %copy-start.3 = (bf16[64,1024]{1,0:T(8,128)(2,1)S(1)}, bf16[64,1024]{1,0:T(8,128)(2,1)}, u32[]{:S(2)}) copy-start(bf16[64,1024]{1,0:T(8,128)(2,1)} %k_ref.1) | copy-start | bytes 393220
  0.6 13.9 %copy-start.2 = (bf16[64,1024]{1,0:T(8,128)(2,1)S(1)}, bf16[64,1024]{1,0:T(8,128)(2,1)}, u32[]{:S(2)}) copy-start(bf16[64,1024]{1,0:T(8,128)(2,1)} %v_ref.1) | copy-start | bytes 393220
  0.7 13.5 %copy-start.7 = (s32[8192]{0:T(1024)S(1)}, s32[8192]{0:T(1024)}, u32[]{:S(2)}) copy-start(s32[8192]{0:T(1024)} %param.13) | copy-start | bytes 98308
  2.6 22.5 %all-to-all-start = ((bf16[32,80,128]{2,1,0:T(8,128)(2,1)}), bf16[32,80,128]{2,1,0:T(8,128)(2,1)S(1)}, u32[]{:S(2)}, u32[]{:S(2)}) async-start(bf16[32,80,128]{2,1,0:T(8,128)(2,1)} %pack_kv.1), calls=%async_computation | async-start | bytes 1310720 | tf_op jit(solution)/shard_map/all_to_all | solution.py:285
  25.1 28.0 %copy-start = (bf16[32,80,128]{2,1,0:T(8,128)(2,1)}, bf16[32,80,128]{2,1,0:T(8,128)(2,1)S(1)}, u32[]{:S(2)}) copy-start(bf16[32,80,128]{2,1,0:T(8,128)(2,1)S(1)} %all-to-all-done.refs_1_) | copy-start | bytes 1966084
  25.1 18.6 %collective-permute-start = (bf16[32,80,128]{2,1,0:T(8,128)(2,1)S(1)}, bf16[32,80,128]{2,1,0:T(8,128)(2,1)S(1)}, u32[]{:S(2)}, u32[]{:S(2)}) collective-permute-start(bf16[32,80,128]{2,1,0:T(8,128)(2,1)S(1)} %all-to-all-done.refs_1_), channel_id=1, source_target_pairs={{0,16},{1,17},{2,18},{3,19},{4,20},{5,21},{6,22},{7,23},{8,24},{9,... | collective-permute-start | bytes 1966088 | tf_op jit(solution)/shard_map/ppermute | solution.py:277
  26.3 17.4 %collective-permute-start.1 = (bf16[32,80,128]{2,1,0:T(8,128)(2,1)S(1)}, bf16[32,80,128]{2,1,0:T(8,128)(2,1)S(1)}, u32[]{:S(2)}, u32[]{:S(2)}) collective-permute-start(bf16[32,80,128]{2,1,0:T(8,128)(2,1)S(1)} %all-to-all-done.refs_1_), channel_id=1, source_target_pairs={{0,48},{1,49},{2,50},{3,51},{4,52},{5,53},{6,54},{7,55},{8,56},{9,... | collective-permute-start | bytes 1966088 | tf_op jit(solution)/shard_map/ppermute | solution.py:277
  27.7 15.9 %all-to-all-start.1 = ((bf16[32,64,128]{2,1,0:T(8,128)(2,1)}), bf16[32,64,128]{2,1,0:T(8,128)(2,1)S(1)}, u32[]{:S(2)}, u32[]{:S(2)}) async-start(bf16[32,64,128]{2,1,0:T(8,128)(2,1)} %pack_q.1), calls=%async_computation.1 | async-start | bytes 1048576 | tf_op jit(solution)/shard_map/all_to_all | solution.py:285
  32.2 18.1 %collective-permute-start.6 = (bf16[32,80,128]{2,1,0:T(8,128)(2,1)S(1)}, bf16[32,80,128]{2,1,0:T(8,128)(2,1)}, u32[]{:S(2)}, u32[]{:S(2)}) collective-permute-start(bf16[32,80,128]{2,1,0:T(8,128)(2,1)S(1)} %all-to-all-done.refs_1_), channel_id=1, source_target_pairs={{0,1},{1,0},{2,3},{3,2},{4,5},{5,4},{6,7},{7,6},{8,9},{9,8},{10,11... | collective-permute-start | bytes 1966088 | tf_op jit(solution)/shard_map/ppermute | solution.py:277
  43.7 9.3 %copy-start.1 = (bf16[32,64,128]{2,1,0:T(8,128)(2,1)}, bf16[32,64,128]{2,1,0:T(8,128)(2,1)S(1)}, u32[]{:S(2)}) copy-start(bf16[32,64,128]{2,1,0:T(8,128)(2,1)S(1)} %all-to-all-done.1.refs_0_) | copy-start | bytes 1572868
  43.7 9.3 %copy-start.4 = (bf16[32,80,128]{2,1,0:T(8,128)(2,1)}, bf16[32,80,128]{2,1,0:T(8,128)(2,1)S(1)}, u32[]{:S(2)}) copy-start(bf16[32,80,128]{2,1,0:T(8,128)(2,1)S(1)} %collective-permute-done.refs_3_) | copy-start | bytes 1966084
  43.7 9.3 %copy-start.5 = (bf16[32,80,128]{2,1,0:T(8,128)(2,1)}, bf16[32,80,128]{2,1,0:T(8,128)(2,1)S(1)}, u32[]{:S(2)}) copy-start(bf16[32,80,128]{2,1,0:T(8,128)(2,1)S(1)} %collective-permute-done.1.refs_5_) | copy-start | bytes 1966084
  43.7 7.0 %collective-permute-start.7 = (bf16[32,80,128]{2,1,0:T(8,128)(2,1)S(1)}, bf16[32,80,128]{2,1,0:T(8,128)(2,1)}, u32[]{:S(2)}, u32[]{:S(2)}) collective-permute-start(bf16[32,80,128]{2,1,0:T(8,128)(2,1)S(1)} %collective-permute-done.refs_3_), channel_id=1, source_target_pairs={{0,1},{1,0},{2,3},{3,2},{4,5},{5,4},{6,7},{7,6},{8,9},{9,8},{10,11... | collective-permute-start | bytes 1966088 | tf_op jit(solution)/shard_map/ppermute | solution.py:277
  44.1 8.9 %collective-permute-start.8 = (bf16[32,80,128]{2,1,0:T(8,128)(2,1)S(1)}, bf16[32,80,128]{2,1,0:T(8,128)(2,1)}, u32[]{:S(2)}, u32[]{:S(2)}) collective-permute-start(bf16[32,80,128]{2,1,0:T(8,128)(2,1)S(1)} %collective-permute-done.1.refs_5_), channel_id=1, source_target_pairs={{0,1},{1,0},{2,3},{3,2},{4,5},{5,4},{6,7},{7,6},{8,9},{9,8},{10,11... | collective-permute-start | bytes 1966088 | tf_op jit(solution)/shard_map/ppermute | solution.py:277
  44.3 33.9 %collective-permute-start.4 = (bf16[64,2048]{1,0:T(8,128)(2,1)S(1)}, bf16[64,2048]{1,0:T(8,128)(2,1)S(1)}, u32[]{:S(2)}, u32[]{:S(2)}) collective-permute-start(bf16[64,2048]{1,0:T(8,128)(2,1)S(1)} %pad_maximum_fusion.1), channel_id=1, source_target_pairs={{0,4},{1,5},{2,6},{3,7},{4,8},{5,9},{6,10},{7,11},{8,12},{9,13},{1... | collective-permute-start | bytes 786440 | tf_op jit(solution)/shard_map/ppermute | solution.py:277
  46.2 32.1 %collective-permute-start.5 = (bf16[64,2048]{1,0:T(8,128)(2,1)S(1)}, bf16[64,2048]{1,0:T(8,128)(2,1)S(1)}, u32[]{:S(2)}, u32[]{:S(2)}) collective-permute-start(bf16[64,2048]{1,0:T(8,128)(2,1)S(1)} %pad_maximum_fusion.1), channel_id=1, source_target_pairs={{0,8},{1,9},{2,10},{3,11},{4,12},{5,13},{6,14},{7,15},{8,16},{9,17... | collective-permute-start | bytes 786440 | tf_op jit(solution)/shard_map/ppermute | solution.py:277
  50.3 28.0 %collective-permute-start.2 = (bf16[16,80,128]{2,1,0:T(8,128)(2,1)S(1)}, bf16[16,80,128]{2,1,0:T(8,128)(2,1)S(1)}, u32[]{:S(2)}, u32[]{:S(2)}) collective-permute-start(bf16[16,80,128]{2,1,0:T(8,128)(2,1)S(1)} %slice.6), channel_id=1, source_target_pairs={{0,16},{1,17},{2,18},{3,19},{4,20},{5,21},{6,22},{7,23},{8,24},{9,... | collective-permute-start | bytes 983048 | tf_op jit(solution)/shard_map/ppermute | solution.py:277
  50.7 27.6 %collective-permute-start.3 = (bf16[16,80,128]{2,1,0:T(8,128)(2,1)S(1)}, bf16[16,80,128]{2,1,0:T(8,128)(2,1)S(1)}, u32[]{:S(2)}, u32[]{:S(2)}) collective-permute-start(bf16[16,80,128]{2,1,0:T(8,128)(2,1)S(1)} %slice.7), channel_id=1, source_target_pairs={{0,48},{1,49},{2,50},{3,51},{4,52},{5,53},{6,54},{7,55},{8,56},{9,... | collective-permute-start | bytes 983048 | tf_op jit(solution)/shard_map/ppermute | solution.py:277
  78.3 4.6 %copy-start.11 = (bf16[16,80,128]{2,1,0:T(8,128)(2,1)}, bf16[16,80,128]{2,1,0:T(8,128)(2,1)S(1)}, u32[]{:S(2)}) copy-start(bf16[16,80,128]{2,1,0:T(8,128)(2,1)S(1)} %collective-permute-done.2.refs_1_) | copy-start | bytes 983044
  78.3 4.6 %copy-start.12 = (bf16[16,80,128]{2,1,0:T(8,128)(2,1)}, bf16[16,80,128]{2,1,0:T(8,128)(2,1)S(1)}, u32[]{:S(2)}) copy-start(bf16[16,80,128]{2,1,0:T(8,128)(2,1)S(1)} %collective-permute-done.3.refs_3_) | copy-start | bytes 983044
  78.4 16.7 %copy-start.6 = (bf16[192,2048]{1,0:T(8,128)(2,1)}, bf16[192,2048]{1,0:T(8,128)(2,1)S(1)}, u32[]{:S(2)}) copy-start(bf16[192,2048]{1,0:T(8,128)(2,1)S(1)} %get-tuple-element.37.refs_0_) | copy-start | bytes 2359300
  78.4 17.2 %collective-permute-start.10 = (bf16[192,2048]{1,0:T(8,128)(2,1)S(1)}, bf16[192,2048]{1,0:T(8,128)(2,1)S(1)}, u32[]{:S(2)}, u32[]{:S(2)}) collective-permute-start(bf16[192,2048]{1,0:T(8,128)(2,1)S(1)} %get-tuple-element.37.refs_0_), channel_id=1, source_target_pairs={{0,1},{1,0},{2,3},{3,2},{4,5},{5,4},{6,7},{7,6},{8,9},{9,8},{10,11... | collective-permute-start | bytes 2359304 | tf_op jit(solution)/shard_map/ppermute | solution.py:277
  80.0 2.4 %collective-permute-start.11 = (bf16[16,80,128]{2,1,0:T(8,128)(2,1)S(1)}, bf16[16,80,128]{2,1,0:T(8,128)(2,1)S(1)}, u32[]{:S(2)}, u32[]{:S(2)}) collective-permute-start(bf16[16,80,128]{2,1,0:T(8,128)(2,1)S(1)} %collective-permute-done.2.refs_1_), channel_id=1, source_target_pairs={{0,1},{1,0},{2,3},{3,2},{4,5},{5,4},{6,7},{7,6},{8,9},{9,8},{10,11... | collective-permute-start | bytes 983048 | tf_op jit(solution)/shard_map/ppermute | solution.py:277
  80.1 2.8 %collective-permute-start.12 = (bf16[16,80,128]{2,1,0:T(8,128)(2,1)S(1)}, bf16[16,80,128]{2,1,0:T(8,128)(2,1)S(1)}, u32[]{:S(2)}, u32[]{:S(2)}) collective-permute-start(bf16[16,80,128]{2,1,0:T(8,128)(2,1)S(1)} %collective-permute-done.3.refs_3_), channel_id=1, source_target_pairs={{0,1},{1,0},{2,3},{3,2},{4,5},{5,4},{6,7},{7,6},{8,9},{9,8},{10,11... | collective-permute-start | bytes 983048 | tf_op jit(solution)/shard_map/ppermute | solution.py:277
  80.6 15.1 %collective-permute-start.9 = (bf16[128,2048]{1,0:T(8,128)(2,1)S(1)}, bf16[128,2048]{1,0:T(8,128)(2,1)S(1)}, u32[]{:S(2)}, u32[]{:S(2)}) collective-permute-start(bf16[128,2048]{1,0:T(8,128)(2,1)S(1)} %pad_maximum_fusion), channel_id=1, source_target_pairs={{0,2},{1,3},{2,0},{3,1},{4,6},{5,7},{6,4},{7,5},{8,10},{9,11},{10,... | collective-permute-start | bytes 1572872 | tf_op jit(solution)/shard_map/ppermute | solution.py:277
  82.4 0.7 copy-start.13
  83.1 0.7 copy-start.14
  95.6 6.2 %copy-start.9 = (bf16[128,2048]{1,0:T(8,128)(2,1)}, bf16[128,2048]{1,0:T(8,128)(2,1)S(1)}, u32[]{:S(2)}) copy-start(bf16[128,2048]{1,0:T(8,128)(2,1)S(1)} %collective-permute-done.9.refs_1_) | copy-start | bytes 1572868
  95.6 6.2 %copy-start.8 = (bf16[192,2048]{1,0:T(8,128)(2,1)}, bf16[192,2048]{1,0:T(8,128)(2,1)S(1)}, u32[]{:S(2)}) copy-start(bf16[192,2048]{1,0:T(8,128)(2,1)S(1)} %collective-permute-done.10.refs_2_) | copy-start | bytes 2359300
  95.6 6.2 %collective-permute-start.13 = (bf16[128,2048]{1,0:T(8,128)(2,1)S(1)}, bf16[128,2048]{1,0:T(8,128)(2,1)S(1)}, u32[]{:S(2)}, u32[]{:S(2)}) collective-permute-start(bf16[128,2048]{1,0:T(8,128)(2,1)S(1)} %collective-permute-done.9.refs_1_), channel_id=1, source_target_pairs={{0,1},{1,0},{2,3},{3,2},{4,5},{5,4},{6,7},{7,6},{8,9},{9,8},{10,11... | collective-permute-start | bytes 1572872 | tf_op jit(solution)/shard_map/ppermute | solution.py:277
  96.6 19.7 %all-to-all-start.2 = ((bf16[32,64,128]{2,1,0:T(8,128)(2,1)}), bf16[32,64,128]{2,1,0:T(8,128)(2,1)S(1)}, u32[]{:S(2)}, u32[]{:S(2)}) async-start(bf16[32,64,128]{2,1,0:T(8,128)(2,1)} %bitcast.8), calls=%async_computation.2 | async-start | bytes 1048576 | tf_op jit(solution)/shard_map/all_to_all | solution.py:285
  101.8 0.8 copy-start.10
